TPU v7x, 512 devices: a whole 4x4x16 slice. The times are simulated.
512 devices in a mesh: ctx: 32 (over z_lo, x), tp: 16 (over y, z_hi, core).
Axes of the slice: x: 4, y: 4, z: 16 (z_hi: 2, z_lo: 8; z = z_hi * 8 + z_lo), core: 2. Of those that a mesh axis runs over, the one named last changes fastest.
Arguments:
- query_plain: bfloat16 [4096, 8192], P('ctx', 'tp'), may hold values from -6 to 6
- query_rotary: bfloat16 [4096, 4096], P('ctx', 'tp'), may hold values from -6 to 6
- latent_keys: bfloat16 [4096, 576], P(('ctx', 'tp')), may hold values from -100 to 100
- span_order: int32 [64], replicated, may hold values from 0 to 63, each once
- key_up: bfloat16 [64, 128, 512], P('tp'), may hold values from -0.5 to 0.5
- value_up: bfloat16 [64, 512, 128], P('tp'), may hold values from -0.5 to 0.5
- output_weight: bfloat16 [8192, 3584], P('tp'), may hold values from -0.125 to 0.125
Outputs:
- mixed: bfloat16 [4096, 3584], P('ctx', 'tp')
Inputs may be any that keep to these rules, and one draw needn't show every extreme that they name: Stored rows s * 64 to (s + 1) * 64 - 1 are the tokens of span span_order[s] of the sequence, in order; each span appears once.
All inputs are finite; a program needn't handle non-finite values.
Results may differ from a plain program's by a relative error of at most 0.015.
Values may be sent and summed in bfloat16 or wider, within the bound.
No kernel may reach another device: no remote copies, remote signals or barrier semaphores. Data moves between devices by JAX's collectives and lax.ppermute only.
A program may use at most 64 MiB of HBM per device.

v0:
```python
import math

import jax
import jax.numpy as jnp
from jax import lax
from jax.sharding import Mesh
from jax.sharding import PartitionSpec as P

CTX = ("ctx_0", "ctx_1")
CTX_TP = ("ctx_0", "ctx_1", "tp")


rope_base = 10000.0
fill_score = -1e30
key_block_rows = 512


def laid_out(tiles, dim):
    lengths = list(tiles.shape[1:])
    lengths[dim] *= tiles.shape[0]
    return jnp.moveaxis(tiles, 0, dim).reshape(lengths)


def sent_to_all(value, axis):
    copies = jnp.broadcast_to(value, (lax.axis_size(axis), *value.shape))
    return lax.all_to_all(copies, axis, split_axis=0, concat_axis=0, tiled=True)


def gather_directly(value, axis, dim):
    return laid_out(sent_to_all(value, axis), dim)


def all_blocks(value, axes, turns):
    tiles = value[None]
    for k in turns:
        tiles = lax.all_gather(tiles, axes[k], axis=0, tiled=True)
    block = [lax.axis_size(axes[k]) for k in reversed(turns)]
    tiles = tiles.reshape(*block, *value.shape)
    turned = sorted(range(len(turns)), key=lambda place: turns[len(turns) - 1 - place])
    return tiles.transpose(*turned, *range(len(turns), tiles.ndim)).reshape(-1, *value.shape)


def gathered_by_axis(value, axes, turns, dim):
    return laid_out(all_blocks(value, axes, turns), dim)


def rotate_pairs(values, places):
    halfway = values.shape[-1] // 2
    frequency = rope_base ** (-jnp.arange(halfway, dtype=jnp.float32) * 2.0 / values.shape[-1])
    angles = places.astype(jnp.float32)[:, None] * frequency[None, :]
    cosine = jnp.cos(angles)
    sine_part = jnp.sin(angles)
    if values.ndim == 3:
        cosine = cosine[:, None, :]
        sine_part = sine_part[:, None, :]
    first_half = values[..., :halfway]
    second_half = values[..., halfway:]
    return jnp.concatenate(
        [
            first_half * cosine - second_half * sine_part,
            first_half * sine_part + second_half * cosine,
        ],
        axis=-1,
    )


def token_places(span_table, indices, span_len):
    slot_ids = indices // span_len
    slot_table = jnp.arange(span_table.shape[0], dtype=jnp.int32)
    picked = jnp.sum(
        jnp.where(slot_ids[:, None] == slot_table[None, :], span_table[None, :], 0), axis=1
    )
    return picked * span_len + indices % span_len


def attend_block(
    carry_state, keys_block, key_places, queries, query_places, latent_width, score_scale
):
    running_max, running_sum, summed = carry_state
    scores = jnp.dot(queries, keys_block.T, preferred_element_type=jnp.float32) * score_scale
    allowed = key_places[None, :] <= query_places[:, None]
    masked = jnp.where(allowed, scores, fill_score)
    new_max = jnp.maximum(running_max, jnp.max(masked, axis=1))
    weights = jnp.where(allowed, jnp.exp(scores - new_max[:, None]), 0.0)
    factor = jnp.exp(running_max - new_max)
    new_sum = running_sum * factor + jnp.sum(weights, axis=1)
    new_summed = summed * factor[:, None] + jnp.dot(
        weights.astype(jnp.bfloat16),
        keys_block[:, :latent_width],
        preferred_element_type=jnp.float32,
    )
    return (new_max, new_sum, new_summed)


def attend_guarded(
    carry_state, keys_block, key_places, queries, query_places, latest, latent_width, score_scale
):
    return lax.cond(
        jnp.min(key_places) > latest,
        lambda carried: carried,
        lambda carried: attend_block(
            carried, keys_block, key_places, queries, query_places, latent_width, score_scale
        ),
        carry_state,
    )


def make_folder(queries, row_places, latest, span_order, span_len, latent_width, score_scale):

    def fold_piece(carry_state, key_piece, offset):
        piece_rows = key_piece.shape[0]
        key_places = token_places(span_order, jnp.arange(piece_rows, dtype=jnp.int32), span_len)

        def step_block(carried, block_parts):
            return (
                attend_guarded(
                    carried,
                    block_parts[0],
                    block_parts[1],
                    queries,
                    row_places,
                    latest,
                    latent_width,
                    score_scale,
                ),
                None,
            )

        stacked = key_piece.reshape(
            piece_rows // key_block_rows, key_block_rows, key_piece.shape[1]
        )
        stacked_places = key_places.reshape(piece_rows // key_block_rows, key_block_rows)
        result_state, unused = lax.scan(step_block, carry_state, (stacked, stacked_places))
        return result_state

    return fold_piece


def start_state(row_count, latent_width):
    return (
        jnp.full((row_count,), fill_score, jnp.float32),
        jnp.zeros((row_count,), jnp.float32),
        jnp.zeros((row_count,), jnp.float32)[:, None] + jnp.zeros((1, latent_width), jnp.float32),
    )


def project_out(final_state, token_count, head_count, latent_width, value_up, output_weight):
    running_max, running_sum, summed = final_state
    mixed_latent = (
        (summed / running_sum[:, None])
        .astype(jnp.bfloat16)
        .reshape(token_count, head_count, latent_width)
    )
    head_out = jnp.einsum(
        "thl,hlv->thv", mixed_latent, value_up, preferred_element_type=jnp.float32
    ).astype(jnp.bfloat16)
    head_out = head_out.reshape(token_count, head_count * value_up.shape[2])
    return jnp.dot(head_out, output_weight, preferred_element_type=jnp.float32)


def on_device(query_plain, query_rotary, latent_keys, span_order, key_up, value_up, output_weight):
    local_tokens = query_plain.shape[0]
    head_count = key_up.shape[0]
    plain_width = key_up.shape[1]
    latent_width = key_up.shape[2]
    rotary_width = query_rotary.shape[1] // head_count
    span_len = local_tokens // 2
    score_scale = 1.0 / math.sqrt(plain_width + rotary_width)
    first_row = lax.axis_index(CTX) * local_tokens
    query_places = token_places(
        span_order, first_row + jnp.arange(local_tokens, dtype=jnp.int32), span_len
    )
    absorbed = jnp.einsum(
        "thn,hnl->thl",
        query_plain.reshape(local_tokens, head_count, plain_width),
        key_up,
        preferred_element_type=jnp.float32,
    ).astype(jnp.bfloat16)
    turned = rotate_pairs(
        query_rotary.reshape(local_tokens, head_count, rotary_width).astype(jnp.float32),
        query_places,
    ).astype(jnp.bfloat16)
    queries = jnp.concatenate([absorbed, turned], axis=2).reshape(
        local_tokens * head_count, latent_width + rotary_width
    )
    row_places = jnp.repeat(query_places, head_count)
    own_rows = latent_keys.shape[0]
    own_first = first_row + lax.axis_index("tp") * own_rows
    own_places = token_places(
        span_order, own_first + jnp.arange(own_rows, dtype=jnp.int32), span_len
    )
    own_turned = rotate_pairs(latent_keys[:, latent_width:].astype(jnp.float32), own_places).astype(
        jnp.bfloat16
    )
    own_keys = jnp.concatenate([latent_keys[:, :latent_width], own_turned], axis=1)
    latest = jnp.max(query_places)
    folder = make_folder(
        queries, row_places, latest, span_order, span_len, latent_width, score_scale
    )
    group_keys = gather_directly(own_keys, "tp", 0)
    final_state = folder(
        start_state(local_tokens * head_count, latent_width),
        gathered_by_axis(group_keys, CTX, (0, 1), 0),
        jnp.int32(0),
    )
    head_terms = project_out(
        final_state, local_tokens, head_count, latent_width, value_up, output_weight
    )
    return lax.psum_scatter(head_terms.astype(jnp.bfloat16), "tp", scatter_dimension=1, tiled=True)


def solution(mesh):
    finer = Mesh(mesh.devices.reshape(8, 4, mesh.shape["tp"]), ("ctx_0", "ctx_1", "tp"))
    in_specs = (
        P(CTX, "tp"),
        P(CTX, "tp"),
        P(CTX_TP, None),
        P(),
        P("tp", None, None),
        P("tp", None, None),
        P("tp", None),
    )
    out_specs = P(CTX, "tp")
    return jax.shard_map(
        on_device, mesh=finer, in_specs=in_specs, out_specs=out_specs, check_vma=False
    )
```

profile of v0, /device:TPU:2, one launch (start us, length us, event | category | flops | bytes accessed | tf_op | source)
XLA Modules:
  0.0 330.0 jit_solution(340173439288745712)
XLA Ops:
  6.6 0.7 slice_convert_fusion
  8.0 0.8 select_reduce_fusion.2
  9.1 33.5 %all_to_all.5 = bf16[16,8,576]{2,1,0:T(8,128)(2,1)S(1)} all-to-all(bf16[16,8,576]{2,1,0:T(8,128)(2,1)S(1)} %broadcast_in_dim.85), channel_id=1, replica_groups=mesh['ctx_0'=8,'ctx_1'=4,'tp'=16] {'tp'}, dimensions={0} | all-to-all | bytes 294912 | tf_op jit(solution)/shard_map/all_to_all | solution.py:26
  42.6 0.8 copy.38
  43.4 63.7 %all-gather.3.cloned.1.call-done = bf16[8,128,576]{1,2,0:T(8,128)(2,1)} async-done(((bf16[1,128,576]{1,2,0:T(8,128)(2,1)}), bf16[8,128,576]{1,2,0:T(8,128)(2,1)}) %all-gather.3.cloned.1.call-update) | async-done | bytes 1179664 | tf_op jit(solution)/shard_map/all_gather | solution.py:36
  107.2 0.9 select_reduce_fusion
  108.1 0.9 copy.42
  109.1 0.7 select_reduce_fusion.1
  110.1 1.3 fusion.13
  111.4 0.8 copy.43
  113.1 51.1 %all-gather.5.cloned.1.call-done = bf16[32,128,576]{1,2,0:T(8,128)(2,1)} async-done(((bf16[8,128,576]{1,2,0:T(8,128)(2,1)}), bf16[32,128,576]{1,2,0:T(8,128)(2,1)}) %all-gather.5.cloned.1.call-update) | async-done | bytes 4718608 | tf_op jit(solution)/shard_map/all_gather | solution.py:36
  164.2 7.7 %copy.49 = bf16[8,4,128,576]{3,2,1,0:T(8,128)(2,1)} copy(bf16[8,4,128,576]{2,3,0,1:T(8,128)(2,1)} %bitcast.30) | data formatting | bytes 9437184
  172.0 24.5 %while.15 = (s32[]{:T(128)}, f32[512]{0:T(512)S(1)}, f32[512]{0:T(512)S(1)}, f32[512,512]{1,0:T(8,128)S(1)}, s32[8,512]{1,0:T(8,128)S(1)}, /*index=5*/s32[]{:T(1...) while((s32[]{:T(128)}, f32[512]{0:T(512)S(1)}, ...), condition=%wide.region_10.11_spmd.clone, body=%wide.region_4.10_spmd.clone.sunk | while | flops 574096896 | bytes 8182519 | solution.py:133
  172.1 0.7 fusion.44
  173.9 3.0 conditional.3
  174.1 1.2 dynamic-slice_bitcast_fusion
  180.8 3.0 conditional.3
  181.0 1.2 dynamic-slice_bitcast_fusion
  185.7 3.0 conditional.3
  185.9 1.2 dynamic-slice_bitcast_fusion
  188.7 0.7 fusion.44
  190.7 0.7 fusion.44
  197.2 4.5 %convolution_convert_fusion = bf16[128,3584]{0,1:T(8,128)(2,1)} fusion(bf16[128,512]{0,1:T(8,128)(2,1)S(1)} %bitcast.32, bf16[512,3584]{1,0:T(8,128)(2,1)} %param.17), kind=kOutput, calls=%fused_computation.19 | convolution fusion | flops 470220800 | bytes 4718592 | tf_op jit(solution)/shard_map/dot_general | solution.py:158
  201.7 121.8 %reduce-scatter.2.cloned.1.call-done = bf16[128,224]{0,1:T(8,128)(2,1)} async-done(((bf16[128,3584]{0,1:T(8,128)(2,1)}), bf16[128,224]{0,1:T(8,128)(2,1)}) %reduce-scatter.2.cloned.1.call-update) | async-done | bytes 57360 | tf_op jit(solution)/shard_map/reduce_scatter | solution.py:209
  (78 shorter events, 12.1 us)
Async XLA Ops:
  6.5 103.5 %copy-start = (bf16[4,128,512]{2,1,0:T(8,128)(2,1)S(1)}, bf16[4,128,512]{2,1,0:T(8,128)(2,1)}, u32[]{:S(2)}) copy-start(bf16[4,128,512]{2,1,0:T(8,128)(2,1)} %param.15) | copy-start | bytes 1572868
  6.5 100.6 %all-gather.3.cloned.1.call-start = ((), (), s32[]{:S(2)}) async-start(), calls=%async_computation.2 | async-start | bytes 1327104 | tf_op jit(solution)/shard_map/all_gather | solution.py:36
  43.4 120.8 %all-gather.5.cloned.1.call-start = ((), (), s32[]{:S(2)}) async-start(), calls=%async_computation.3 | async-start | bytes 5898240 | tf_op jit(solution)/shard_map/all_gather | solution.py:36
  107.2 216.3 %reduce-scatter.2.cloned.1.call-start = ((), (), s32[]{:S(2)}) async-start(), calls=%async_computation.4 | async-start | bytes 974848 | tf_op jit(solution)/shard_map/reduce_scatter | solution.py:209
  172.0 24.8 %copy-start.1 = (bf16[4,512,128]{2,1,0:T(8,128)(2,1)S(1)}, bf16[4,512,128]{2,1,0:T(8,128)(2,1)}, u32[]{:S(2)}) copy-start(bf16[4,512,128]{2,1,0:T(8,128)(2,1)} %param.16) | copy-start | bytes 1572868
Sparse Core Ops, SparseCore 0:
  43.5 63.5 all-gather.2
  109.2 54.9 all-gather.4
  201.8 121.5 reduce-scatter.1
where the time goes:
time: 331 us; the launch traced here: 330 us
  waiting for transfers between devices  237 us (72%)
  blocking collectives  33.5 us (10%)
  local copies, waits for them, and re-layouts  15.6 us (5%)
  between operations  13.3 us (4%)
  other arithmetic  10.9 us (3%)
  matrix products  10.1 us (3%)
  loops' own time  10 us (3%)
    reduce_scatter x1, waiting for transfers between devices, on_device(): lax.psum_scatter(head_terms.astype(jnp.bfloat16), 'tp', scatter_dimension...  122 us
    all_gather x2, waiting for transfers between devices, all_blocks(): tiles = lax.all_gather(tiles, axes[k], axis=0, tiled=True)  115 us
    all_to_all x1, blocking collectives, sent_to_all(): return lax.all_to_all(copies, axis, split_axis=0, concat_axis=0, tiled=True)  33.5 us
    another operation x1, loops' own time, fold_piece(): lax.scan(step_block, carry_state, (stacked, stacked_places))  9.75 us
    unnamed x5, local copies, waits for them, and re-layouts  7.71 us
  transfers between devices with their start and end apart: 3, of which 3 were waited for; matrix products, arithmetic and copies ran while one was open for 2% of the time, Pallas kernels for 0%

commit v1 on v0

v1 whole, which is shorter than its diff:
```python
import functools
import math

import jax
import jax.numpy as jnp
import numpy as np
from jax import lax
from jax.experimental import pallas as pl
from jax.experimental.pallas import tpu as pltpu
from jax.sharding import Mesh
from jax.sharding import PartitionSpec as P

NZL, NX, NY, NZH, NC = 8, 4, 4, 2, 2
CTX = ("zl", "x")
TP = ("y", "zh", "c")

SPAN = 64
ROPE = 64
LAT = 512
NOPE = 128
VD = 128
HEADS = 4
KEYW = LAT + ROPE
QW = HEADS * (NOPE + ROPE)
OUTW = HEADS * VD + 128
BASE = 10000.0
LOW = -1e30
VMEM_LIMIT = 48 * 1024 * 1024


def rotary_tables():
    lane = np.arange(128)
    freq = BASE ** (-2.0 * (lane % 32) / ROPE)
    sign = np.where(lane % 64 < 32, -1.0, 1.0)
    start = (np.arange(64) * SPAN)[:, None] * freq[None, :]
    offset = np.arange(SPAN)[:, None] * freq[None, :]
    tables = [np.cos(start), sign * np.sin(start), np.cos(offset), sign * np.sin(offset)]
    return np.stack(tables).astype(np.float32)


def turn(values, cosine, signed_sine):
    lane = lax.broadcasted_iota(jnp.int32, values.shape, 1)
    partner = jnp.where(
        lane % 64 < 32, pltpu.roll(values, 96, axis=1), pltpu.roll(values, 32, axis=1)
    )
    return values * cosine + partner * signed_sine


def angle_of(tables_ref, span, offset_rows):
    cos_a = tables_ref[0, pl.ds(span, 1), :]
    sin_a = tables_ref[1, pl.ds(span, 1), :]
    cos_b = tables_ref[2, offset_rows, :]
    sin_b = tables_ref[3, offset_rows, :]
    return cos_a * cos_b - sin_a * sin_b, sin_a * cos_b + cos_a * sin_b


def prepare_kernel(where_ref, spans_ref, plain_ref, rotary_ref, keys_ref, tables_ref, kb_ref, q_ref):
    ctx = where_ref[0]
    tp = where_ref[1]
    own_span = spans_ref[ctx * 2 + tp // 8]
    first = pl.multiple_of((tp % 8) * 8, 8)
    cosine, sine = angle_of(tables_ref, own_span, pl.ds(first, 8))
    tail = keys_ref[:, LAT:].astype(jnp.float32)
    turned = turn(jnp.concatenate([tail, tail], axis=1), cosine, sine).astype(jnp.bfloat16)
    for k in range(kb_ref.shape[0]):
        kb_ref[k, :, :LAT] = keys_ref[:, :LAT]
        kb_ref[k, :, LAT:] = turned[:, :ROPE]
    q_ref[:, : HEADS * NOPE] = plain_ref[...]
    for s in range(2):
        cosine, sine = angle_of(tables_ref, spans_ref[ctx * 2 + s], pl.ds(0, SPAN))
        for j in range(HEADS * ROPE // 128):
            part = rotary_ref[s * SPAN : (s + 1) * SPAN, j * 128 : (j + 1) * 128]
            q_ref[s * SPAN : (s + 1) * SPAN, HEADS * NOPE + j * 128 : HEADS * NOPE + (j + 1) * 128] = turn(
                part.astype(jnp.float32), cosine, sine
            ).astype(jnp.bfloat16)


def prepare(where, spans, plain, rotary, keys):
    smem = pl.BlockSpec(memory_space=pltpu.SMEM)
    vmem = pl.BlockSpec(memory_space=pltpu.VMEM)
    return pl.pallas_call(
        prepare_kernel,
        out_shape=(
            jax.ShapeDtypeStruct((NZL * NZH, 8, KEYW), jnp.bfloat16),
            jax.ShapeDtypeStruct((2 * SPAN, QW), jnp.bfloat16),
        ),
        in_specs=[smem, smem, vmem, vmem, vmem, vmem],
        out_specs=(vmem, vmem),
    )(where, spans, plain, rotary, keys, jnp.asarray(rotary_tables()))


def attend_kernel(
    where_ref, spans_ref, q0, q1, q2, q3, own_ref, other_ref, kp_own_ref, kp_other_ref, up_ref, value_ref, out_ref, query
):
    zl = where_ref[0] // NX
    x = where_ref[0] % NX
    scale = math.log2(math.e) / math.sqrt(NOPE + ROPE)
    for k, block in enumerate((q0, q1, q2, q3)):
        source = (x + NX - k) % NX
        for s in range(2):
            rows = slice(s * SPAN, (s + 1) * SPAN)
            for h in range(HEADS):
                at = slice(h * SPAN, (h + 1) * SPAN)
                query[at, :LAT] = jnp.dot(
                    block[rows, h * NOPE : (h + 1) * NOPE], up_ref[h], preferred_element_type=jnp.float32
                ).astype(jnp.bfloat16)
                query[at, LAT:] = block[rows, HEADS * NOPE + h * ROPE : HEADS * NOPE + (h + 1) * ROPE]
            place = spans_ref[(zl * NX + source) * 2 + s] * SPAN + (
                lax.broadcasted_iota(jnp.int32, (HEADS * SPAN, 1), 0) % SPAN
            )
            dims = (((1,), (1,)), ((), ()))
            scores = []
            for keys, key_place in ((own_ref, kp_own_ref), (other_ref, kp_other_ref)):
                raw = lax.dot_general(query[...], keys[...], dims, preferred_element_type=jnp.float32)
                scores.append(jnp.where(key_place[...] <= place, raw * scale, LOW))
            highest = jnp.maximum(
                jnp.max(scores[0], axis=1, keepdims=True), jnp.max(scores[1], axis=1, keepdims=True)
            )
            total = jnp.zeros((HEADS * SPAN, 1), jnp.float32)
            context = jnp.zeros((HEADS * SPAN, LAT), jnp.float32)
            for score, keys in zip(scores, (own_ref, other_ref)):
                raised = jnp.exp2(score - highest)
                total = total + jnp.sum(raised, axis=1, keepdims=True)
                context = context + jnp.dot(
                    raised.astype(jnp.bfloat16), keys[:, :LAT], preferred_element_type=jnp.float32
                )
            context = (context / total).astype(jnp.bfloat16)
            log_sum = highest + jnp.log2(total)
            high = log_sum.astype(jnp.bfloat16).astype(jnp.float32)
            rest = log_sum - high
            middle = rest.astype(jnp.bfloat16).astype(jnp.float32)
            low = rest - middle
            lane = lax.broadcasted_iota(jnp.int32, (SPAN, 128), 1)
            packed = jnp.zeros((SPAN, 128), jnp.float32)
            for h in range(HEADS):
                at = slice(h * SPAN, (h + 1) * SPAN)
                out_ref[source, rows, h * VD : (h + 1) * VD] = jnp.dot(
                    context[at], value_ref[h], preferred_element_type=jnp.float32
                ).astype(jnp.bfloat16)
                for n, part in enumerate((high, middle, low)):
                    packed = jnp.where(lane == n * HEADS + h, part[at], packed)
            out_ref[source, rows, HEADS * VD :] = packed.astype(jnp.bfloat16)


def attend(where, spans, blocks, own, other, places, key_up, value_up):
    smem = pl.BlockSpec(memory_space=pltpu.SMEM)
    vmem = pl.BlockSpec(memory_space=pltpu.VMEM)
    return pl.pallas_call(
        attend_kernel,
        out_shape=jax.ShapeDtypeStruct((NX, 2 * SPAN, OUTW), jnp.bfloat16),
        in_specs=[smem, smem] + [vmem] * 10,
        out_specs=vmem,
        scratch_shapes=[pltpu.VMEM((HEADS * SPAN, KEYW), jnp.bfloat16)],
        compiler_params=pltpu.CompilerParams(vmem_limit_bytes=VMEM_LIMIT),
    )(where, spans, *blocks, own, other, *places, key_up, value_up)


def project_kernel(where_ref, parts_ref, weight_ref, send_ref, keep_ref, head_out):
    c = where_ref[1] % NC

    @pl.when(pl.program_id(0) == 0)
    def _():
        packed = [parts_ref[i, :, HEADS * VD :].astype(jnp.float32) for i in range(NX)]
        for h in range(HEADS):
            logs = [
                (p[:, h : h + 1] + p[:, HEADS + h : HEADS + h + 1]) + p[:, 2 * HEADS + h : 2 * HEADS + h + 1]
                for p in packed
            ]
            highest = functools.reduce(jnp.maximum, logs)
            shares = [jnp.exp2(v - highest) for v in logs]
            total = functools.reduce(jnp.add, shares)
            merged = functools.reduce(
                jnp.add,
                [
                    shares[i] * parts_ref[i, :, h * VD : (h + 1) * VD].astype(jnp.float32)
                    for i in range(NX)
                ],
            )
            head_out[:, h * VD : (h + 1) * VD] = (merged / total).astype(jnp.bfloat16)

    result = jnp.dot(head_out[...], weight_ref[...], preferred_element_type=jnp.float32).astype(jnp.bfloat16)
    width = result.shape[1] // (NZH * NC)
    for zh in range(NZH):
        even = result[:, 2 * zh * width : (2 * zh + 1) * width]
        odd = result[:, (2 * zh + 1) * width : (2 * zh + 2) * width]
        keep_ref[0, zh] = jnp.where(c == 0, even, odd)
        send_ref[0, zh] = jnp.where(c == 0, odd, even)


def project(where, parts, weight):
    rows = parts.shape[1]
    columns = weight.shape[1]
    step = columns // NY
    width = step // (NZH * NC)
    piece = jax.ShapeDtypeStruct((NY, NZH, rows, width), jnp.bfloat16)
    piece_spec = pl.BlockSpec((1, NZH, rows, width), lambda i: (i, 0, 0, 0))
    return pl.pallas_call(
        project_kernel,
        out_shape=(piece, piece),
        grid=(NY,),
        in_specs=[
            pl.BlockSpec(memory_space=pltpu.SMEM),
            pl.BlockSpec(parts.shape, lambda i: (0, 0, 0)),
            pl.BlockSpec((weight.shape[0], step), lambda i: (0, i)),
        ],
        out_specs=(piece_spec, piece_spec),
        scratch_shapes=[pltpu.VMEM((rows, HEADS * VD), jnp.bfloat16)],
        compiler_params=pltpu.CompilerParams(vmem_limit_bytes=VMEM_LIMIT),
    )(where, parts, weight)


def shifted(value, axis, size, by):
    return lax.ppermute(value, axis, [(i, (i + by) % size) for i in range(size)])


def swapped(value, axis):
    return shifted(value, axis, 2, 1)


def key_places(spans, x, c):
    row = jnp.arange(NY * NZL * NZH * 8, dtype=jnp.int32)
    y = row // (NZL * NZH * 8)
    zl = row // (NZH * 8) % NZL
    zh = row // 8 % NZH
    span = (zl * NX + x) * 2 + y // 2
    table = jnp.arange(spans.shape[0], dtype=jnp.int32)
    picked = jnp.sum(jnp.where(span[:, None] == table[None, :], spans[None, :], 0), axis=1)
    return (picked * SPAN + (y % 2) * 32 + zh * 16 + c * 8 + row % 8)[None, :]


def on_device(query_plain, query_rotary, latent_keys, span_order, key_up, value_up, output_weight):
    x = lax.axis_index("x")
    c = lax.axis_index("c")
    where = jnp.stack([lax.axis_index(CTX), lax.axis_index(TP)]).astype(jnp.int32)
    sent_keys, queries = prepare(where, span_order, query_plain, query_rotary, latent_keys)
    blocks = [queries] + [shifted(queries, "x", NX, k) for k in (1, 2, 3)]
    along_z = lax.all_to_all(sent_keys, ("zl", "zh"), split_axis=0, concat_axis=0, tiled=True)
    along_z = along_z.reshape(1, NZL * NZH * 8, KEYW)
    along_y = lax.all_to_all(
        jnp.broadcast_to(along_z, (NY, *along_z.shape[1:])), "y", split_axis=0, concat_axis=0, tiled=True
    )
    own = along_y.reshape(NY * NZL * NZH * 8, KEYW)
    other = swapped(own, "c")
    places = (key_places(span_order, x, c), key_places(span_order, x, 1 - c))
    parts = attend(where, span_order, blocks, own, other, places, key_up, value_up)
    parts = lax.all_to_all(parts, "x", split_axis=0, concat_axis=0, tiled=True)
    send, keep = project(where, parts, output_weight)
    both = (keep.astype(jnp.float32) + swapped(send, "c").astype(jnp.float32)).astype(jnp.bfloat16)
    over_y = lax.all_to_all(both, "y", split_axis=0, concat_axis=0, tiled=True)
    summed = jnp.sum(over_y.astype(jnp.float32), axis=0)
    zh = lax.axis_index("zh")
    mine = jnp.where(zh == 0, summed[0], summed[1])
    theirs = jnp.where(zh == 0, summed[1], summed[0]).astype(jnp.bfloat16)
    return (mine + swapped(theirs, "zh").astype(jnp.float32)).astype(jnp.bfloat16)


def solution(mesh):
    finer = Mesh(
        mesh.devices.reshape(NZL, NX, NY, NZH, NC), ("zl", "x", "y", "zh", "c")
    )
    in_specs = (
        P(CTX, TP),
        P(CTX, TP),
        P(CTX + TP, None),
        P(),
        P(TP, None, None),
        P(TP, None, None),
        P(TP, None),
    )
    return jax.shard_map(
        on_device, mesh=finer, in_specs=in_specs, out_specs=P(CTX, TP), check_vma=False
    )
```

time: 331 us -> 122 us (0.37)
  the two profiles are of different devices: /device:TPU:2 before, /device:TPU:32 now
where the time goes in v1:
time: 122 us; the launch traced here: 121 us
  blocking collectives  46.6 us (38%)
  waiting for transfers between devices  26.4 us (22%)
  starting transfers between devices  25.9 us (21%)
  Pallas kernels  15.7 us (13%)
  local copies, waits for them, and re-layouts  4.88 us (4%)
  other arithmetic  1.7 us (1%)
    all_to_all x1, blocking collectives, on_device(): lax.all_to_all(sent_keys, ('zl', 'zh'), split_axis=0, concat_axis=0, tile...  32 us
    ppermute x6, waiting for transfers between devices, shifted(): lax.ppermute(value, axis, [(i, (i + by) % size) for i in range(size)])  17.3 us
    ppermute x6, starting transfers between devices, shifted(): lax.ppermute(value, axis, [(i, (i + by) % size) for i in range(size)])  16.6 us
    all_to_all x1, blocking collectives, on_device(): parts = lax.all_to_all(parts, 'x', split_axis=0, concat_axis=0, tiled=True)  14.6 us
    pallas_call x1, Pallas kernels, attend(): pl.pallas_call(attend_kernel, out_shape=jax.ShapeDtypeStruct((NX, 2 * SPA...  10.4 us
    all_to_all x1, waiting for transfers between devices, on_device(): over_y = lax.all_to_all(both, 'y', split_axis=0, concat_axis=0, tiled=True)  9.08 us
    all_to_all x1, starting transfers between devices, on_device(): over_y = lax.all_to_all(both, 'y', split_axis=0, concat_axis=0, tiled=True)  4.79 us
    all_to_all x1, starting transfers between devices, on_device(): lax.all_to_all(jnp.broadcast_to(along_z, (NY, *along_z.shape[1:])), 'y',...  4.46 us
  transfers between devices with their start and end apart: 8, of which 4 were waited for; matrix products, arithmetic and copies ran while one was open for 2% of the time, Pallas kernels for 0%

profile of v1, /device:TPU:32, one launch (start us, length us, event | category | flops | bytes accessed | tf_op | source)
XLA Modules:
  0.0 121.4 jit_solution(6550262218914744024)
XLA Ops:
  0.0 0.7 pad_add_fusion.where_ref
  0.7 1.9 %shard_map.82 = (bf16[16,8,576]{2,1,0:T(8,128)(2,1)}, bf16[128,768]{1,0:T(8,128)(2,1)}) custom-call(s32[2]{0:T(128)} %pad_add_fusion.where_ref, s32[64]{0:T(128)} %spans_ref.3, bf16[128,512]{1,0:T(8,128)(2,1)} %plain_ref.1, bf16[128,256]{1,0:T(8,128)(2,1)} %rotary_ref.1, bf16[8,576]{1,0:T(8,128)(2,1)} %keys_ref.1, f32[4,64,128]{2,1,0:T(8,128)} %constant.146.clone.tables_ref), custom_call_target="tpu_custom_call" | custom-call | tf_op jit(solution)/shard_map/pallas_call | solution.py:81
  2.6 32.0 %all_to_all.20 = bf16[16,8,576]{2,1,0:T(8,128)(2,1)S(1)} all-to-all(bf16[16,8,576]{2,1,0:T(8,128)(2,1)} %get-tuple-element.10), channel_id=1, replica_groups=mesh['zl'=8,'x'=4,'y'=4,'zh'=2,'c'=2] {'zl','zh'}, dimensions={0} | all-to-all | bytes 294912 | tf_op jit(solution)/shard_map/all_to_all | solution.py:237
  34.7 0.9 broadcast_in_dim.32
  35.6 4.5 %all-to-all-start.1 = ((bf16[4,128,576]{1,2,0:T(8,128)(2,1)}), bf16[4,128,576]{1,2,0:T(8,128)(2,1)S(1)}, u32[]{:S(2)}, u32[]{:S(2)}) async-start(bf16[4,128,576]{1,2,0:T(8,128)(2,1)} %broadcast_in_dim.32), calls=%async_computation.1 | async-start | bytes 1179648 | tf_op jit(solution)/shard_map/all_to_all | solution.py:239
  40.1 4.7 %collective-permute-start.2 = (bf16[128,768]{1,0:T(8,128)(2,1)}, bf16[128,768]{1,0:T(8,128)(2,1)S(1)}, u32[]{:S(2)}, u32[]{:S(2)}) collective-permute-start(bf16[128,768]{1,0:T(8,128)(2,1)} %get-tuple-element.9.q0), channel_id=1, source_target_pairs={{0,48},{16,0},{32,16},{48,32},{1,49},{17,1},{33,17},{49,33},{2,50}... | collective-permute-start | bytes 589832 | tf_op jit(solution)/shard_map/ppermute | solution.py:213
  44.8 2.7 %collective-permute-start.1 = (bf16[128,768]{1,0:T(8,128)(2,1)}, bf16[128,768]{1,0:T(8,128)(2,1)S(1)}, u32[]{:S(2)}, u32[]{:S(2)}) collective-permute-start(bf16[128,768]{1,0:T(8,128)(2,1)} %get-tuple-element.9.q0), channel_id=1, source_target_pairs={{0,32},{16,48},{32,0},{48,16},{1,33},{17,49},{33,1},{49,17},{2,34}... | collective-permute-start | bytes 589832 | tf_op jit(solution)/shard_map/ppermute | solution.py:213
  47.5 2.8 %collective-permute-start = (bf16[128,768]{1,0:T(8,128)(2,1)}, bf16[128,768]{1,0:T(8,128)(2,1)S(1)}, u32[]{:S(2)}, u32[]{:S(2)}) collective-permute-start(bf16[128,768]{1,0:T(8,128)(2,1)} %get-tuple-element.9.q0), channel_id=1, source_target_pairs={{0,16},{16,32},{32,48},{48,0},{1,17},{17,33},{33,49},{49,1},{2,18}... | collective-permute-start | bytes 589832 | tf_op jit(solution)/shard_map/ppermute | solution.py:213
  50.3 0.8 select_reduce_fusion
  51.1 0.3 copy.17
  51.6 1.9 %collective-permute-start.3 = (bf16[512,576]{0,1:T(8,128)(2,1)S(1)}, bf16[512,576]{0,1:T(8,128)(2,1)}, u32[]{:S(2)}, u32[]{:S(2)}) collective-permute-start(bf16[512,576]{0,1:T(8,128)(2,1)S(1)} %copy.18), channel_id=1, source_target_pairs={{0,1},{1,0},{2,3},{3,2},{4,5},{5,4},{6,7},{7,6},{8,9},{9,8},{10,11... | collective-permute-start | bytes 1769480 | tf_op jit(solution)/shard_map/ppermute | solution.py:213
  53.6 2.0 %collective-permute-done.3 = bf16[512,576]{0,1:T(8,128)(2,1)} collective-permute-done((bf16[512,576]{0,1:T(8,128)(2,1)S(1)}, bf16[512,576]{0,1:T(8,128)(2,1)}, u32[]{:S(2)}, u32[]{:S(2)}) %collective-permute-start.3) | collective-permute-done | bytes 589856 | tf_op jit(solution)/shard_map/ppermute | solution.py:213
  55.6 1.4 %copy.19.other_ref = bf16[512,576]{1,0:T(8,128)(2,1)S(1)} copy(bf16[512,576]{0,1:T(8,128)(2,1)} %collective-permute-done.3) | data formatting | bytes 1179648 | tf_op jit(solution)/shard_map/ppermute | solution.py:213
  57.1 10.4 %shard_map.83 = bf16[4,128,640]{2,1,0:T(8,128)(2,1)S(1)} custom-call(s32[2]{0:T(128)S(1)} %copy-done.4, s32[64]{0:T(128)S(1)} %copy-done.5, bf16[128,768]{1,0:T(8,128)(2,1)S(1)} %copy-done.3, bf16[128,768]{1,0:T(8,128)(2,1)S(1)} %collective-permute-done.q1, bf16[128,768]{1,0:T(8,128)(2,1)S(1)} %collective-permute-done.1.q2, ...), custom_call_target="tpu_custom_call" | custom-call | tf_op jit(solution)/shard_map/pallas_call | solution.py:148
  67.5 14.6 %all_to_all.21.parts_ref = bf16[4,128,640]{2,1,0:T(8,128)(2,1)S(1)} all-to-all(bf16[4,128,640]{2,1,0:T(8,128)(2,1)S(1)} %shard_map.83), channel_id=1, replica_groups=mesh['zl'=8,'x'=4,'y'=4,'zh'=2,'c'=2] {'x'}, dimensions={0} | all-to-all | bytes 1310720 | tf_op jit(solution)/shard_map/all_to_all | solution.py:246
  82.1 3.4 %shard_map.84 = (bf16[4,2,128,224]{3,2,1,0:T(8,128)(2,1)S(1)}, bf16[4,2,128,224]{3,2,1,0:T(8,128)(2,1)S(1)}) custom-call(s32[2]{0:T(128)S(1)} %copy-done.4, bf16[4,128,640]{2,1,0:T(8,128)(2,1)S(1)} %all_to_all.21.parts_ref, bf16[512,3584]{1,0:T(8,128)(2,1)S(1)} %copy-done), custom_call_target="tpu_custom_call" | custom-call | tf_op jit(solution)/shard_map/pallas_call | solution.py:197
  85.6 1.9 %collective-permute-start.4 = (bf16[4,2,128,224]{3,2,1,0:T(8,128)(2,1)S(1)}, bf16[4,2,128,224]{3,2,1,0:T(8,128)(2,1)S(1)}, u32[]{:S(2)}, u32[]{:S(2)}) collective-permute-start(bf16[4,2,128,224]{3,2,1,0:T(8,128)(2,1)S(1)} %get-tuple-element.12), channel_id=1, source_target_pairs={{0,1},{1,0},{2,3},{3,2},{4,5},{5,4},{6,7},{7,6},{8,9},{9,8},{10,11... | collective-permute-start | bytes 1376264 | tf_op jit(solution)/shard_map/ppermute | solution.py:213
  87.5 1.9 %collective-permute-done.4 = bf16[4,2,128,224]{3,2,1,0:T(8,128)(2,1)S(1)} collective-permute-done((bf16[4,2,128,224]{3,2,1,0:T(8,128)(2,1)S(1)}, bf16[4,2,128,224]{3,2,1,0:T(8,128)(2,1)S(1)}, u32[]{:S(2)}, u32[]{:S(2)}) %collective-permute-start.4) | collective-permute-done | bytes 458784 | tf_op jit(solution)/shard_map/ppermute | solution.py:213
  89.5 1.0 copy.20
  90.5 4.8 %all-to-all-start.3 = ((bf16[4,2,128,224]{2,3,1,0:T(8,128)(2,1)}), bf16[4,2,128,224]{2,3,1,0:T(8,128)(2,1)S(1)}, u32[]{:S(2)}, u32[]{:S(2)}) async-start(bf16[4,2,128,224]{2,3,1,0:T(8,128)(2,1)} %copy.20), calls=%async_computation.3 | async-start | bytes 917504 | tf_op jit(solution)/shard_map/all_to_all | solution.py:249
  95.3 9.1 %all-to-all-done.3 = bf16[4,2,128,224]{2,3,1,0:T(8,128)(2,1)S(1)} async-done(((bf16[4,2,128,224]{2,3,1,0:T(8,128)(2,1)}), bf16[4,2,128,224]{2,3,1,0:T(8,128)(2,1)S(1)}, u32[]{:S(2)}, u32[]{:S(2)}) %all-to-all-start.3) | async-done | bytes 458784 | tf_op jit(solution)/shard_map/all_to_all | solution.py:249
  104.7 2.6 %collective-permute-start.5 = (bf16[128,224]{1,0:T(8,128)(2,1)S(1)}, bf16[128,224]{1,0:T(8,128)(2,1)S(1)}, u32[]{:S(2)}, u32[]{:S(2)}) collective-permute-start(bf16[128,224]{1,0:T(8,128)(2,1)S(1)} %fusion.1), channel_id=1, source_target_pairs={{0,2},{2,0},{1,3},{3,1},{4,6},{6,4},{5,7},{7,5},{8,10},{10,8},{9,1... | collective-permute-start | bytes 172040 | tf_op jit(solution)/shard_map/ppermute | solution.py:213
  107.3 13.4 %collective-permute-done.5 = bf16[128,224]{1,0:T(8,128)(2,1)S(1)} collective-permute-done((bf16[128,224]{1,0:T(8,128)(2,1)S(1)}, bf16[128,224]{1,0:T(8,128)(2,1)S(1)}, u32[]{:S(2)}, u32[]{:S(2)}) %collective-permute-start.5) | collective-permute-done | bytes 57376 | tf_op jit(solution)/shard_map/ppermute | solution.py:213
  120.7 0.7 copy.22
  (29 shorter events, 0.9 us)
Async XLA Ops:
  0.0 57.0 %copy-start.5 = (s32[64]{0:T(128)S(1)}, s32[64]{0:T(128)}, u32[]{:S(2)}) copy-start(s32[64]{0:T(128)} %spans_ref.3) | copy-start | bytes 772
  0.0 57.1 %copy-start.2 = (bf16[4,512,128]{2,1,0:T(8,128)(2,1)S(1)}, bf16[4,512,128]{2,1,0:T(8,128)(2,1)}, u32[]{:S(2)}) copy-start(bf16[4,512,128]{2,1,0:T(8,128)(2,1)} %value_ref.1) | copy-start | bytes 1572868
  0.0 57.1 %copy-start.1 = (bf16[4,128,512]{2,1,0:T(8,128)(2,1)S(1)}, bf16[4,128,512]{2,1,0:T(8,128)(2,1)}, u32[]{:S(2)}) copy-start(bf16[4,128,512]{2,1,0:T(8,128)(2,1)} %up_ref.1) | copy-start | bytes 1572868
  0.7 56.4 %copy-start.4 = (s32[2]{0:T(128)S(1)}, s32[2]{0:T(128)}, u32[]{:S(2)}) copy-start(s32[2]{0:T(128)} %pad_add_fusion.where_ref) | copy-start | bytes 28
  2.6 54.5 %copy-start.3 = (bf16[128,768]{1,0:T(8,128)(2,1)S(1)}, bf16[128,768]{1,0:T(8,128)(2,1)}, u32[]{:S(2)}) copy-start(bf16[128,768]{1,0:T(8,128)(2,1)} %get-tuple-element.9.q0) | copy-start | bytes 589828
  35.6 15.4 %all-to-all-start.1 = ((bf16[4,128,576]{1,2,0:T(8,128)(2,1)}), bf16[4,128,576]{1,2,0:T(8,128)(2,1)S(1)}, u32[]{:S(2)}, u32[]{:S(2)}) async-start(bf16[4,128,576]{1,2,0:T(8,128)(2,1)} %broadcast_in_dim.32), calls=%async_computation.1 | async-start | bytes 1179648 | tf_op jit(solution)/shard_map/all_to_all | solution.py:239
  40.1 16.9 %collective-permute-start.2 = (bf16[128,768]{1,0:T(8,128)(2,1)}, bf16[128,768]{1,0:T(8,128)(2,1)S(1)}, u32[]{:S(2)}, u32[]{:S(2)}) collective-permute-start(bf16[128,768]{1,0:T(8,128)(2,1)} %get-tuple-element.9.q0), channel_id=1, source_target_pairs={{0,48},{16,0},{32,16},{48,32},{1,49},{17,1},{33,17},{49,33},{2,50}... | collective-permute-start | bytes 589832 | tf_op jit(solution)/shard_map/ppermute | solution.py:213
  44.8 12.3 %collective-permute-start.1 = (bf16[128,768]{1,0:T(8,128)(2,1)}, bf16[128,768]{1,0:T(8,128)(2,1)S(1)}, u32[]{:S(2)}, u32[]{:S(2)}) collective-permute-start(bf16[128,768]{1,0:T(8,128)(2,1)} %get-tuple-element.9.q0), channel_id=1, source_target_pairs={{0,32},{16,48},{32,0},{48,16},{1,33},{17,49},{33,1},{49,17},{2,34}... | collective-permute-start | bytes 589832 | tf_op jit(solution)/shard_map/ppermute | solution.py:213
  47.5 9.6 %collective-permute-start = (bf16[128,768]{1,0:T(8,128)(2,1)}, bf16[128,768]{1,0:T(8,128)(2,1)S(1)}, u32[]{:S(2)}, u32[]{:S(2)}) collective-permute-start(bf16[128,768]{1,0:T(8,128)(2,1)} %get-tuple-element.9.q0), channel_id=1, source_target_pairs={{0,16},{16,32},{32,48},{48,0},{1,17},{17,33},{33,49},{49,1},{2,18}... | collective-permute-start | bytes 589832 | tf_op jit(solution)/shard_map/ppermute | solution.py:213
  51.6 4.0 %collective-permute-start.3 = (bf16[512,576]{0,1:T(8,128)(2,1)S(1)}, bf16[512,576]{0,1:T(8,128)(2,1)}, u32[]{:S(2)}, u32[]{:S(2)}) collective-permute-start(bf16[512,576]{0,1:T(8,128)(2,1)S(1)} %copy.18), channel_id=1, source_target_pairs={{0,1},{1,0},{2,3},{3,2},{4,5},{5,4},{6,7},{7,6},{8,9},{9,8},{10,11... | collective-permute-start | bytes 1769480 | tf_op jit(solution)/shard_map/ppermute | solution.py:213
  57.0 25.1 %copy-start = (bf16[512,3584]{1,0:T(8,128)(2,1)S(1)}, bf16[512,3584]{1,0:T(8,128)(2,1)}, u32[]{:S(2)}) copy-start(bf16[512,3584]{1,0:T(8,128)(2,1)} %weight_ref.1) | copy-start | bytes 11010052
  85.6 3.8 %collective-permute-start.4 = (bf16[4,2,128,224]{3,2,1,0:T(8,128)(2,1)S(1)}, bf16[4,2,128,224]{3,2,1,0:T(8,128)(2,1)S(1)}, u32[]{:S(2)}, u32[]{:S(2)}) collective-permute-start(bf16[4,2,128,224]{3,2,1,0:T(8,128)(2,1)S(1)} %get-tuple-element.12), channel_id=1, source_target_pairs={{0,1},{1,0},{2,3},{3,2},{4,5},{5,4},{6,7},{7,6},{8,9},{9,8},{10,11... | collective-permute-start | bytes 1376264 | tf_op jit(solution)/shard_map/ppermute | solution.py:213
  90.5 13.9 %all-to-all-start.3 = ((bf16[4,2,128,224]{2,3,1,0:T(8,128)(2,1)}), bf16[4,2,128,224]{2,3,1,0:T(8,128)(2,1)S(1)}, u32[]{:S(2)}, u32[]{:S(2)}) async-start(bf16[4,2,128,224]{2,3,1,0:T(8,128)(2,1)} %copy.20), calls=%async_computation.3 | async-start | bytes 917504 | tf_op jit(solution)/shard_map/all_to_all | solution.py:249
  104.7 16.0 %collective-permute-start.5 = (bf16[128,224]{1,0:T(8,128)(2,1)S(1)}, bf16[128,224]{1,0:T(8,128)(2,1)S(1)}, u32[]{:S(2)}, u32[]{:S(2)}) collective-permute-start(bf16[128,224]{1,0:T(8,128)(2,1)S(1)} %fusion.1), channel_id=1, source_target_pairs={{0,2},{2,0},{1,3},{3,1},{4,6},{6,4},{5,7},{7,5},{8,10},{10,8},{9,1... | collective-permute-start | bytes 172040 | tf_op jit(solution)/shard_map/ppermute | solution.py:213

commit v2 on v1

v2 whole, which is shorter than its diff:
```python
import functools
import math

import jax
import jax.numpy as jnp
import numpy as np
from jax import lax
from jax.experimental import pallas as pl
from jax.experimental.pallas import tpu as pltpu
from jax.sharding import Mesh
from jax.sharding import PartitionSpec as P

NZL, NX, NY, NZH, NC = 8, 4, 4, 2, 2
CTX = ("zl", "x")
TP = ("y", "zh", "c")

SPAN = 64
ROPE = 64
LAT = 512
NOPE = 128
VD = 128
HEADS = 4
KEYW = LAT + ROPE
ROWW = 640
GROUP = NZL * NZH
NSPAN = 2 * NZL
CHUNK = 256
QW = HEADS * (NOPE + ROPE)
OUTW = HEADS * VD + 128
BASE = 10000.0
LOW = -1e30
VMEM_LIMIT = 48 * 1024 * 1024


def rotary_tables():
    lane = np.arange(128)
    freq = BASE ** (-2.0 * (lane % 32) / ROPE)
    sign = np.where(lane % 64 < 32, -1.0, 1.0)
    start = (np.arange(64) * SPAN)[:, None] * freq[None, :]
    offset = np.arange(SPAN)[:, None] * freq[None, :]
    tables = [np.cos(start), sign * np.sin(start), np.cos(offset), sign * np.sin(offset)]
    return np.stack(tables).astype(np.float32)


def turn(values, cosine, signed_sine):
    lane = lax.broadcasted_iota(jnp.int32, values.shape, 1)
    partner = jnp.where(
        lane % 64 < 32, pltpu.roll(values, 96, axis=1), pltpu.roll(values, 32, axis=1)
    )
    return values * cosine + partner * signed_sine


def angle_of(tables_ref, span, offset_rows):
    cos_a = tables_ref[0, pl.ds(span, 1), :]
    sin_a = tables_ref[1, pl.ds(span, 1), :]
    cos_b = tables_ref[2, offset_rows, :]
    sin_b = tables_ref[3, offset_rows, :]
    return cos_a * cos_b - sin_a * sin_b, sin_a * cos_b + cos_a * sin_b


def own_ctx():
    return lax.axis_index("zl") * NX + lax.axis_index("x")


def own_tp():
    return (lax.axis_index("y") * NZH + lax.axis_index("zh")) * NC + lax.axis_index("c")


def keys_kernel(spans_ref, keys_ref, tables_ref, out_ref):
    tp = own_tp()
    span = spans_ref[own_ctx() * 2 + tp // 8]
    first = pl.multiple_of((tp % 8) * 8, 8)
    cosine, sine = angle_of(tables_ref, span, pl.ds(first, 8))
    tail = keys_ref[:, LAT:].astype(jnp.float32)
    turned = turn(jnp.concatenate([tail, tail], axis=1), cosine, sine).astype(jnp.bfloat16)
    for k in range(GROUP):
        out_ref[k, :, :LAT] = keys_ref[:, :LAT]
        out_ref[k, :, LAT:] = turned


def queries_kernel(spans_ref, plain_ref, rotary_ref, tables_ref, after_ref, out_ref):
    out_ref[:, : HEADS * NOPE] = plain_ref[...]
    for s in range(2):
        rows = slice(s * SPAN, (s + 1) * SPAN)
        cosine, sine = angle_of(tables_ref, spans_ref[own_ctx() * 2 + s], pl.ds(0, SPAN))
        for j in range(HEADS * ROPE // 128):
            part = rotary_ref[rows, j * 128 : (j + 1) * 128].astype(jnp.float32)
            at = HEADS * NOPE + j * 128
            out_ref[rows, at : at + 128] = turn(part, cosine, sine).astype(jnp.bfloat16)


SMEM = pl.BlockSpec(memory_space=pltpu.SMEM)
WHOLE = pl.BlockSpec(memory_space=pltpu.VMEM)


def attend_kernel(spans_ref, q0, q1, q2, q3, own_ref, other_ref, up_ref, value_ref, out_ref, query, sorted_keys, contexts):
    zl = lax.axis_index("zl")
    x = lax.axis_index("x")
    c = lax.axis_index("c")
    scale = math.log2(math.e) / math.sqrt(NOPE + ROPE)

    places = [spans_ref[((i // 2) * NX + x) * 2 + i % 2] for i in range(NSPAN)]

    def earlier(place):
        return functools.reduce(jnp.add, [(p < place).astype(jnp.int32) for p in places])

    for i in range(NSPAN):
        rank = earlier(places[i])
        for half, keys in enumerate((own_ref, other_ref)):
            for low in range(2):
                source = ((i % 2) * 2 + low) * GROUP * 8 + (i // 2) * NZH * 8
                target = pl.multiple_of(rank * SPAN + half * 32 + low * 16, 16)
                sorted_keys[pl.ds(target, 16), :] = keys[source : source + 16, :]

    blocks = (q0, q1, q2, q3)
    for h in range(HEADS):
        plain = jnp.concatenate([block[:, h * NOPE : (h + 1) * NOPE] for block in blocks], axis=0)
        absorbed = jnp.dot(plain, up_ref[h], preferred_element_type=jnp.float32).astype(jnp.bfloat16)
        first = HEADS * NOPE + h * ROPE
        at = slice(h * SPAN, (h + 1) * SPAN)
        for b in range(2 * NX):
            query[b, at, :LAT] = absorbed[b * SPAN : (b + 1) * SPAN]
            query[b, at, LAT:] = blocks[b // 2][(b % 2) * SPAN : (b % 2 + 1) * SPAN, first : first + ROPE]

    column = lax.broadcasted_iota(jnp.int32, (1, CHUNK), 1)
    core = jnp.where(column // 32 % 2 == 0, c, 1 - c)
    key_order = column // SPAN * SPAN + column // 16 % 2 * 32 + column // 8 % 2 * 16 + core * 8 + column % 8
    token = lax.broadcasted_iota(jnp.int32, (HEADS * SPAN, 1), 0) % SPAN
    lane = lax.broadcasted_iota(jnp.int32, (SPAN, 128), 1)
    dims = (((1,), (1,)), ((), ()))

    def one_span(b, carry):
        block = (x + NX - b // 2) % NX
        first_row = pl.multiple_of((b % 2) * SPAN, SPAN)
        below = earlier(spans_ref[(zl * NX + block) * 2 + b % 2])
        diagonal = block == x
        chunks = (below + diagonal.astype(jnp.int32) + CHUNK // SPAN - 1) // (CHUNK // SPAN)
        limit = below * SPAN + jnp.where(diagonal, token, -1)

        @pl.when(chunks == 0)
        def _():
            for h in range(HEADS):
                contexts[h, pl.ds(pl.multiple_of(b * SPAN, SPAN), SPAN), :] = jnp.zeros((SPAN, LAT), jnp.bfloat16)
            out_ref[block, pl.ds(first_row, SPAN), HEADS * VD :] = jnp.where(
                lane < HEADS, LOW, 0.0
            ).astype(jnp.bfloat16)

        for count in range(1, NSPAN * SPAN // CHUNK + 1):

            @pl.when(chunks == count)
            def _(count=count):
                rows = query[b]
                scores = []
                for n in range(count):
                    raw = lax.dot_general(
                        rows,
                        sorted_keys[n * CHUNK : (n + 1) * CHUNK, :KEYW],
                        dims,
                        preferred_element_type=jnp.float32,
                    ) * scale
                    if n == count - 1:
                        raw = jnp.where(key_order + n * CHUNK <= limit, raw, LOW)
                    scores.append(raw)
                highest = functools.reduce(jnp.maximum, [jnp.max(v, axis=1, keepdims=True) for v in scores])
                total = None
                context = None
                for n in range(count):
                    raised = jnp.exp2(scores[n] - highest)
                    part_sum = jnp.sum(raised, axis=1, keepdims=True)
                    part = jnp.dot(
                        raised.astype(jnp.bfloat16),
                        sorted_keys[n * CHUNK : (n + 1) * CHUNK, :LAT],
                        preferred_element_type=jnp.float32,
                    )
                    total = part_sum if total is None else total + part_sum
                    context = part if context is None else context + part
                context = (context * (1.0 / total)).astype(jnp.bfloat16)
                log_sum = highest + jnp.log2(total)
                high = log_sum.astype(jnp.bfloat16).astype(jnp.float32)
                rest = log_sum - high
                middle = rest.astype(jnp.bfloat16).astype(jnp.float32)
                packed = jnp.zeros((SPAN, 128), jnp.float32)
                for h in range(HEADS):
                    at = slice(h * SPAN, (h + 1) * SPAN)
                    contexts[h, pl.ds(pl.multiple_of(b * SPAN, SPAN), SPAN), :] = context[at]
                    for n, part in enumerate((high, middle, rest - middle)):
                        packed = jnp.where(lane == n * HEADS + h, part[at], packed)
                out_ref[block, pl.ds(first_row, SPAN), HEADS * VD :] = packed.astype(jnp.bfloat16)

        return carry

    lax.fori_loop(0, 2 * NX, one_span, 0)

    for h in range(HEADS):
        values = jnp.dot(contexts[h], value_ref[h], preferred_element_type=jnp.float32).astype(jnp.bfloat16)
        for k in range(NX):
            out_ref[(x + NX - k) % NX, :, h * VD : (h + 1) * VD] = values[k * 2 * SPAN : (k + 1) * 2 * SPAN]


def attend(spans, blocks, own, other, key_up, value_up):
    return pl.pallas_call(
        attend_kernel,
        out_shape=jax.ShapeDtypeStruct((NX, 2 * SPAN, OUTW), jnp.bfloat16),
        in_specs=[SMEM] + [WHOLE] * 8,
        out_specs=WHOLE,
        scratch_shapes=[
            pltpu.VMEM((2 * NX, HEADS * SPAN, KEYW), jnp.bfloat16),
            pltpu.VMEM((NSPAN * SPAN, ROWW), jnp.bfloat16),
            pltpu.VMEM((HEADS, NX * 2 * SPAN, LAT), jnp.bfloat16),
        ],
        compiler_params=pltpu.CompilerParams(vmem_limit_bytes=VMEM_LIMIT),
    )(spans, *blocks, own, other, key_up, value_up)


def project_kernel(parts_ref, weight_ref, send_ref, keep_ref):
    c = lax.axis_index("c")
    packed = [parts_ref[i, :, HEADS * VD :].astype(jnp.float32) for i in range(NX)]
    heads = []
    for h in range(HEADS):
        logs = [
            (p[:, h : h + 1] + p[:, HEADS + h : HEADS + h + 1]) + p[:, 2 * HEADS + h : 2 * HEADS + h + 1]
            for p in packed
        ]
        highest = functools.reduce(jnp.maximum, logs)
        shares = [jnp.exp2(v - highest) for v in logs]
        inverse = 1.0 / functools.reduce(jnp.add, shares)
        merged = functools.reduce(
            jnp.add,
            [
                (shares[i] * inverse) * parts_ref[i, :, h * VD : (h + 1) * VD].astype(jnp.float32)
                for i in range(NX)
            ],
        )
        heads.append(merged.astype(jnp.bfloat16))
    head_out = jnp.concatenate(heads, axis=1)
    step = weight_ref.shape[1] // NY
    width = step // (NZH * NC)
    for y in range(NY):
        result = jnp.dot(
            head_out, weight_ref[:, y * step : (y + 1) * step], preferred_element_type=jnp.float32
        ).T.astype(jnp.bfloat16)
        for zh in range(NZH):
            even = result[2 * zh * width : (2 * zh + 1) * width]
            odd = result[(2 * zh + 1) * width : (2 * zh + 2) * width]
            keep_ref[y, zh] = jnp.where(c == 0, even, odd)
            send_ref[y, zh] = jnp.where(c == 0, odd, even)


def project(parts, weight):
    rows = parts.shape[1]
    width = weight.shape[1] // (NY * NZH * NC)
    piece = jax.ShapeDtypeStruct((NY, NZH, width, rows), jnp.bfloat16)
    return pl.pallas_call(
        project_kernel,
        out_shape=(piece, piece),
        in_specs=[WHOLE, WHOLE],
        out_specs=(WHOLE, WHOLE),
        compiler_params=pltpu.CompilerParams(vmem_limit_bytes=VMEM_LIMIT),
    )(parts, weight)


def swapped(value, axis):
    return lax.ppermute(value, axis, [(0, 1), (1, 0)])


def exchanged(value, axis):
    return lax.all_to_all(value, axis, split_axis=0, concat_axis=0, tiled=True)


def on_device(query_plain, query_rotary, latent_keys, span_order, key_up, value_up, output_weight):
    zh = lax.axis_index("zh")
    tables = jnp.asarray(rotary_tables())
    sent_keys = pl.pallas_call(
        keys_kernel,
        out_shape=jax.ShapeDtypeStruct((GROUP, 8, ROWW), jnp.bfloat16),
        in_specs=[SMEM, WHOLE, WHOLE],
        out_specs=WHOLE,
    )(span_order, latent_keys, tables)
    queries = pl.pallas_call(
        queries_kernel,
        out_shape=jax.ShapeDtypeStruct((2 * SPAN, QW), jnp.bfloat16),
        in_specs=[SMEM, WHOLE, WHOLE, WHOLE, pl.BlockSpec(memory_space=pl.ANY)],
        out_specs=WHOLE,
    )(span_order, query_plain, query_rotary, tables, sent_keys)
    along_z = exchanged(sent_keys, ("zl", "zh")).reshape(GROUP * 8, ROWW)
    blocks = [queries] + [
        lax.ppermute(queries, "x", [(i, (i + k) % NX) for i in range(NX)]) for k in range(1, NX)
    ]
    along_z, *blocks = lax.optimization_barrier((along_z, *blocks))
    own = exchanged(jnp.broadcast_to(along_z[None], (NY, GROUP * 8, ROWW)), "y").reshape(NY * GROUP * 8, ROWW)
    other = swapped(own, "c")
    parts = attend(span_order, blocks, own, other, key_up, value_up)
    send, keep = project(exchanged(parts, "x"), output_weight)
    both = (keep.astype(jnp.float32) + swapped(send, "c").astype(jnp.float32)).astype(jnp.bfloat16)
    over_y = exchanged(both, "y").astype(jnp.float32)
    mine = jnp.sum(lax.dynamic_index_in_dim(over_y, zh, 1, keepdims=False), axis=0)
    theirs = jnp.sum(lax.dynamic_index_in_dim(over_y, 1 - zh, 1, keepdims=False), axis=0).astype(jnp.bfloat16)
    return (mine + swapped(theirs, "zh").astype(jnp.float32)).astype(jnp.bfloat16).T


def solution(mesh):
    finer = Mesh(
        mesh.devices.reshape(NZL, NX, NY, NZH, NC), ("zl", "x", "y", "zh", "c")
    )
    in_specs = (
        P(CTX, TP),
        P(CTX, TP),
        P(CTX + TP, None),
        P(),
        P(TP, None, None),
        P(TP, None, None),
        P(TP, None),
    )
    return jax.shard_map(
        on_device, mesh=finer, in_specs=in_specs, out_specs=P(CTX, TP), check_vma=False
    )
```

time: 122 us -> 116 us (0.951)
  the two profiles are of different devices: /device:TPU:32 before, /device:TPU:160 now
where the time goes in v2:
time: 116 us; the launch traced here: 115 us
  starting transfers between devices  38.4 us (33%)
  blocking collectives  29.5 us (25%)
  waiting for transfers between devices  27.5 us (24%)
  Pallas kernels  16.6 us (14%)
  local copies, waits for them, and re-layouts  1.65 us (1%)
  other arithmetic  1.64 us (1%)
    all_to_all x2, blocking collectives, exchanged(): return lax.all_to_all(value, axis, split_axis=0, concat_axis=0, tiled=True)  29.5 us
    all_to_all x2, starting transfers between devices, exchanged(): return lax.all_to_all(value, axis, split_axis=0, concat_axis=0, tiled=True)  16.9 us
    ppermute x3, waiting for transfers between devices, swapped(): return lax.ppermute(value, axis, [(0, 1), (1, 0)])  13.5 us
    pallas_call x1, Pallas kernels, attend(): pl.pallas_call(attend_kernel, out_shape=jax.ShapeDtypeStruct((NX, 2 * SPA...  11.7 us
    ppermute x3, starting transfers between devices, on_device(): lax.ppermute(queries, 'x', [(i, (i + k) % NX) for i in range(NX)])  11.4 us
    ppermute x3, starting transfers between devices, swapped(): return lax.ppermute(value, axis, [(0, 1), (1, 0)])  10.2 us
    all_to_all x2, waiting for transfers between devices, exchanged(): return lax.all_to_all(value, axis, split_axis=0, concat_axis=0, tiled=True)  9.32 us
    ppermute x3, waiting for transfers between devices, on_device(): lax.ppermute(queries, 'x', [(i, (i + k) % NX) for i in range(NX)])  4.69 us
  transfers between devices with their start and end apart: 8, of which 6 were waited for; matrix products, arithmetic and copies ran while one was open for 0% of the time, Pallas kernels for 2%

profile of v2, /device:TPU:160, one launch (start us, length us, event | category | flops | bytes accessed | tf_op | source)
XLA Modules:
  0.0 115.3 jit_solution(10527770745301507162)
XLA Ops:
  0.0 1.8 %shard_map.82.after_ref = bf16[16,8,640]{2,1,0:T(8,128)(2,1)} custom-call(s32[64]{0:T(128)} %spans_ref.5, bf16[8,576]{1,0:T(8,128)(2,1)} %keys_ref.1, f32[4,64,128]{2,1,0:T(8,128)} %constant.20.clone.tables_ref), custom_call_target="tpu_custom_call" | custom-call | tf_op jit(solution)/shard_map/pallas_call | solution.py:273
  1.8 13.4 %all-to-all-start = ((bf16[16,8,640]{2,1,0:T(8,128)(2,1)}), bf16[16,8,640]{2,1,0:T(8,128)(2,1)S(1)}, u32[]{:S(2)}, u32[]{:S(2)}) async-start(bf16[16,8,640]{2,1,0:T(8,128)(2,1)} %shard_map.82.after_ref), calls=%async_computation | async-start | bytes 327680 | tf_op jit(solution)/shard_map/all_to_all | solution.py:267
  15.2 1.8 %shard_map.83.q0 = bf16[128,768]{1,0:T(8,128)(2,1)} custom-call(s32[64]{0:T(128)} %spans_ref.5, bf16[128,512]{1,0:T(8,128)(2,1)} %plain_ref.1, bf16[128,256]{1,0:T(8,128)(2,1)} %rotary_ref.1, f32[4,64,128]{2,1,0:T(8,128)} %constant.20.clone.tables_ref, bf16[16,8,640]{2,1,0:T(8,128)(2,1)} %shard_map.82.after_ref), custom_call_target="tpu_custom_call" | custom-call | tf_op jit(solution)/shard_map/pallas_call | solution.py:279
  17.0 3.4 %collective-permute-start = (bf16[128,768]{1,0:T(8,128)(2,1)}, bf16[128,768]{1,0:T(8,128)(2,1)S(1)}, u32[]{:S(2)}, u32[]{:S(2)}) collective-permute-start(bf16[128,768]{1,0:T(8,128)(2,1)} %shard_map.83.q0), channel_id=1, source_target_pairs={{0,16},{16,32},{32,48},{48,0},{1,17},{17,33},{33,49},{49,1},{2,18}... | collective-permute-start | bytes 589832 | tf_op jit(solution)/shard_map/ppermute | solution.py:287
  20.4 4.6 %collective-permute-start.1 = (bf16[128,768]{1,0:T(8,128)(2,1)}, bf16[128,768]{1,0:T(8,128)(2,1)S(1)}, u32[]{:S(2)}, u32[]{:S(2)}) collective-permute-start(bf16[128,768]{1,0:T(8,128)(2,1)} %shard_map.83.q0), channel_id=1, source_target_pairs={{0,32},{16,48},{32,0},{48,16},{1,33},{17,49},{33,1},{49,17},{2,34}... | collective-permute-start | bytes 589832 | tf_op jit(solution)/shard_map/ppermute | solution.py:287
  25.1 3.3 %collective-permute-start.2 = (bf16[128,768]{1,0:T(8,128)(2,1)}, bf16[128,768]{1,0:T(8,128)(2,1)S(1)}, u32[]{:S(2)}, u32[]{:S(2)}) collective-permute-start(bf16[128,768]{1,0:T(8,128)(2,1)} %shard_map.83.q0), channel_id=1, source_target_pairs={{0,48},{16,0},{32,16},{48,32},{1,49},{17,1},{33,17},{49,33},{2,50}... | collective-permute-start | bytes 589832 | tf_op jit(solution)/shard_map/ppermute | solution.py:287
  28.4 3.2 %collective-permute-done.1.q2 = bf16[128,768]{1,0:T(8,128)(2,1)S(1)} collective-permute-done((bf16[128,768]{1,0:T(8,128)(2,1)}, bf16[128,768]{1,0:T(8,128)(2,1)S(1)}, u32[]{:S(2)}, u32[]{:S(2)}) %collective-permute-start.1) | collective-permute-done | bytes 196640 | tf_op jit(solution)/shard_map/ppermute | solution.py:287
  31.6 1.5 %collective-permute-done.2.q3 = bf16[128,768]{1,0:T(8,128)(2,1)S(1)} collective-permute-done((bf16[128,768]{1,0:T(8,128)(2,1)}, bf16[128,768]{1,0:T(8,128)(2,1)S(1)}, u32[]{:S(2)}, u32[]{:S(2)}) %collective-permute-start.2) | collective-permute-done | bytes 196640 | tf_op jit(solution)/shard_map/ppermute | solution.py:287
  33.2 13.8 %all_to_all.20 = bf16[4,128,640]{2,1,0:T(8,128)(2,1)S(1)} all-to-all(bf16[4,128,640]{2,1,0:T(8,128)(2,1)S(1)} %broadcast_in_dim.2), channel_id=1, replica_groups=mesh['zl'=8,'x'=4,'y'=4,'zh'=2,'c'=2] {'y'}, dimensions={0} | all-to-all | bytes 1310720 | tf_op jit(solution)/shard_map/all_to_all | solution.py:267
  47.0 1.9 %collective-permute-start.3 = (bf16[512,640]{1,0:T(8,128)(2,1)S(1)}, bf16[512,640]{1,0:T(8,128)(2,1)S(1)}, u32[]{:S(2)}, u32[]{:S(2)}) collective-permute-start(bf16[512,640]{1,0:T(8,128)(2,1)S(1)} %bitcast.4), channel_id=1, source_target_pairs={{0,1},{1,0},{2,3},{3,2},{4,5},{5,4},{6,7},{7,6},{8,9},{9,8},{10,11... | collective-permute-start | bytes 1966088 | tf_op jit(solution)/shard_map/ppermute | solution.py:263
  48.9 2.1 %collective-permute-done.3.other_ref = bf16[512,640]{1,0:T(8,128)(2,1)S(1)} collective-permute-done((bf16[512,640]{1,0:T(8,128)(2,1)S(1)}, bf16[512,640]{1,0:T(8,128)(2,1)S(1)}, u32[]{:S(2)}, u32[]{:S(2)}) %collective-permute-start.3) | collective-permute-done | bytes 655392 | tf_op jit(solution)/shard_map/ppermute | solution.py:263
  50.9 0.9 copy-done.1
  51.9 0.7 copy-done.4
  52.5 11.7 %shard_map.84 = bf16[4,128,640]{2,1,0:T(8,128)(2,1)S(1)} custom-call(s32[64]{0:T(128)S(1)} %copy-done.4, bf16[128,768]{1,0:T(8,128)(2,1)S(1)} %copy-done.1, bf16[128,768]{1,0:T(8,128)(2,1)S(1)} %collective-permute-done.q1, bf16[128,768]{1,0:T(8,128)(2,1)S(1)} %collective-permute-done.1.q2, bf16[128,768]{1,0:T(8,128)(2,1)S(1)} %collective-permute-done.2.q3, ...), custom_call_target="tpu_custom_call" | custom-call | tf_op jit(solution)/shard_map/pallas_call | solution.py:201
  64.2 15.7 %all_to_all.21.parts_ref = bf16[4,128,640]{2,1,0:T(8,128)(2,1)S(1)} all-to-all(bf16[4,128,640]{2,1,0:T(8,128)(2,1)S(1)} %shard_map.84), channel_id=1, replica_groups=mesh['zl'=8,'x'=4,'y'=4,'zh'=2,'c'=2] {'x'}, dimensions={0} | all-to-all | bytes 1310720 | tf_op jit(solution)/shard_map/all_to_all | solution.py:267
  79.9 1.3 %shard_map.85 = (bf16[4,2,224,128]{3,2,1,0:T(8,128)(2,1)S(1)}, bf16[4,2,224,128]{3,2,1,0:T(8,128)(2,1)S(1)}) custom-call(bf16[4,128,640]{2,1,0:T(8,128)(2,1)S(1)} %all_to_all.21.parts_ref, bf16[512,3584]{1,0:T(8,128)(2,1)S(1)} %copy-done), custom_call_target="tpu_custom_call" | custom-call | tf_op jit(solution)/shard_map/pallas_call | solution.py:253
  81.2 1.9 %collective-permute-start.4 = (bf16[4,2,224,128]{3,2,1,0:T(8,128)(2,1)S(1)}, bf16[4,2,224,128]{3,2,1,0:T(8,128)(2,1)S(1)}, u32[]{:S(2)}, u32[]{:S(2)}) collective-permute-start(bf16[4,2,224,128]{3,2,1,0:T(8,128)(2,1)S(1)} %get-tuple-element.18), channel_id=1, source_target_pairs={{0,1},{1,0},{2,3},{3,2},{4,5},{5,4},{6,7},{7,6},{8,9},{9,8},{10,11... | collective-permute-start | bytes 1376264 | tf_op jit(solution)/shard_map/ppermute | solution.py:263
  83.1 1.8 %collective-permute-done.4 = bf16[4,2,224,128]{3,2,1,0:T(8,128)(2,1)S(1)} collective-permute-done((bf16[4,2,224,128]{3,2,1,0:T(8,128)(2,1)S(1)}, bf16[4,2,224,128]{3,2,1,0:T(8,128)(2,1)S(1)}, u32[]{:S(2)}, u32[]{:S(2)}) %collective-permute-start.4) | collective-permute-done | bytes 458784 | tf_op jit(solution)/shard_map/ppermute | solution.py:263
  84.9 0.9 add_convert_fusion
  85.8 3.5 %all-to-all-start.3 = ((bf16[4,2,224,128]{3,2,1,0:T(8,128)(2,1)}), bf16[4,2,224,128]{3,2,1,0:T(8,128)(2,1)S(1)}, u32[]{:S(2)}, u32[]{:S(2)}) async-start(bf16[4,2,224,128]{3,2,1,0:T(8,128)(2,1)} %add_convert_fusion), calls=%async_computation.3 | async-start | bytes 917504 | tf_op jit(solution)/shard_map/all_to_all | solution.py:267
  89.3 9.3 %all-to-all-done.3 = bf16[4,2,224,128]{3,2,1,0:T(8,128)(2,1)S(1)} async-done(((bf16[4,2,224,128]{3,2,1,0:T(8,128)(2,1)}), bf16[4,2,224,128]{3,2,1,0:T(8,128)(2,1)S(1)}, u32[]{:S(2)}, u32[]{:S(2)}) %all-to-all-start.3) | async-done | bytes 458784 | tf_op jit(solution)/shard_map/all_to_all | solution.py:267
  98.7 6.4 %collective-permute-start.5 = (bf16[224,128]{1,0:T(8,128)(2,1)S(1)}, bf16[224,128]{1,0:T(8,128)(2,1)S(1)}, u32[]{:S(2)}, u32[]{:S(2)}) collective-permute-start(bf16[224,128]{1,0:T(8,128)(2,1)S(1)} %get-tuple-element.19), channel_id=1, source_target_pairs={{0,2},{2,0},{1,3},{3,1},{4,6},{6,4},{5,7},{7,5},{8,10},{10,8},{9,1... | collective-permute-start | bytes 172040 | tf_op jit(solution)/shard_map/ppermute | solution.py:263
  105.1 9.6 %collective-permute-done.5 = bf16[224,128]{1,0:T(8,128)(2,1)S(1)} collective-permute-done((bf16[224,128]{1,0:T(8,128)(2,1)S(1)}, bf16[224,128]{1,0:T(8,128)(2,1)S(1)}, u32[]{:S(2)}, u32[]{:S(2)}) %collective-permute-start.5) | collective-permute-done | bytes 57376 | tf_op jit(solution)/shard_map/ppermute | solution.py:263
  114.7 0.6 fusion
  (13 shorter events, 0.2 us)
Async XLA Ops:
  0.0 50.9 %copy-start.2 = (bf16[4,128,512]{2,1,0:T(8,128)(2,1)S(1)}, bf16[4,128,512]{2,1,0:T(8,128)(2,1)}, u32[]{:S(2)}) copy-start(bf16[4,128,512]{2,1,0:T(8,128)(2,1)} %up_ref.1) | copy-start | bytes 1572868
  0.0 50.9 %copy-start.3 = (bf16[4,512,128]{2,1,0:T(8,128)(2,1)S(1)}, bf16[4,512,128]{2,1,0:T(8,128)(2,1)}, u32[]{:S(2)}) copy-start(bf16[4,512,128]{2,1,0:T(8,128)(2,1)} %value_ref.1) | copy-start | bytes 1572868
  1.8 31.3 %all-to-all-start = ((bf16[16,8,640]{2,1,0:T(8,128)(2,1)}), bf16[16,8,640]{2,1,0:T(8,128)(2,1)S(1)}, u32[]{:S(2)}, u32[]{:S(2)}) async-start(bf16[16,8,640]{2,1,0:T(8,128)(2,1)} %shard_map.82.after_ref), calls=%async_computation | async-start | bytes 327680 | tf_op jit(solution)/shard_map/all_to_all | solution.py:267
  17.0 11.4 %collective-permute-start = (bf16[128,768]{1,0:T(8,128)(2,1)}, bf16[128,768]{1,0:T(8,128)(2,1)S(1)}, u32[]{:S(2)}, u32[]{:S(2)}) collective-permute-start(bf16[128,768]{1,0:T(8,128)(2,1)} %shard_map.83.q0), channel_id=1, source_target_pairs={{0,16},{16,32},{32,48},{48,0},{1,17},{17,33},{33,49},{49,1},{2,18}... | collective-permute-start | bytes 589832 | tf_op jit(solution)/shard_map/ppermute | solution.py:287
  20.4 11.2 %collective-permute-start.1 = (bf16[128,768]{1,0:T(8,128)(2,1)}, bf16[128,768]{1,0:T(8,128)(2,1)S(1)}, u32[]{:S(2)}, u32[]{:S(2)}) collective-permute-start(bf16[128,768]{1,0:T(8,128)(2,1)} %shard_map.83.q0), channel_id=1, source_target_pairs={{0,32},{16,48},{32,0},{48,16},{1,33},{17,49},{33,1},{49,17},{2,34}... | collective-permute-start | bytes 589832 | tf_op jit(solution)/shard_map/ppermute | solution.py:287
  25.1 8.0 %collective-permute-start.2 = (bf16[128,768]{1,0:T(8,128)(2,1)}, bf16[128,768]{1,0:T(8,128)(2,1)S(1)}, u32[]{:S(2)}, u32[]{:S(2)}) collective-permute-start(bf16[128,768]{1,0:T(8,128)(2,1)} %shard_map.83.q0), channel_id=1, source_target_pairs={{0,48},{16,0},{32,16},{48,32},{1,49},{17,1},{33,17},{49,33},{2,50}... | collective-permute-start | bytes 589832 | tf_op jit(solution)/shard_map/ppermute | solution.py:287
  33.1 46.8 %copy-start = (bf16[512,3584]{1,0:T(8,128)(2,1)S(1)}, bf16[512,3584]{1,0:T(8,128)(2,1)}, u32[]{:S(2)}) copy-start(bf16[512,3584]{1,0:T(8,128)(2,1)} %weight_ref.1) | copy-start | bytes 11010052
  47.0 4.0 %collective-permute-start.3 = (bf16[512,640]{1,0:T(8,128)(2,1)S(1)}, bf16[512,640]{1,0:T(8,128)(2,1)S(1)}, u32[]{:S(2)}, u32[]{:S(2)}) collective-permute-start(bf16[512,640]{1,0:T(8,128)(2,1)S(1)} %bitcast.4), channel_id=1, source_target_pairs={{0,1},{1,0},{2,3},{3,2},{4,5},{5,4},{6,7},{7,6},{8,9},{9,8},{10,11... | collective-permute-start | bytes 1966088 | tf_op jit(solution)/shard_map/ppermute | solution.py:263
  50.9 0.9 copy-start.1
  51.9 0.7 copy-start.4
  81.2 3.7 %collective-permute-start.4 = (bf16[4,2,224,128]{3,2,1,0:T(8,128)(2,1)S(1)}, bf16[4,2,224,128]{3,2,1,0:T(8,128)(2,1)S(1)}, u32[]{:S(2)}, u32[]{:S(2)}) collective-permute-start(bf16[4,2,224,128]{3,2,1,0:T(8,128)(2,1)S(1)} %get-tuple-element.18), channel_id=1, source_target_pairs={{0,1},{1,0},{2,3},{3,2},{4,5},{5,4},{6,7},{7,6},{8,9},{9,8},{10,11... | collective-permute-start | bytes 1376264 | tf_op jit(solution)/shard_map/ppermute | solution.py:263
  85.8 12.8 %all-to-all-start.3 = ((bf16[4,2,224,128]{3,2,1,0:T(8,128)(2,1)}), bf16[4,2,224,128]{3,2,1,0:T(8,128)(2,1)S(1)}, u32[]{:S(2)}, u32[]{:S(2)}) async-start(bf16[4,2,224,128]{3,2,1,0:T(8,128)(2,1)} %add_convert_fusion), calls=%async_computation.3 | async-start | bytes 917504 | tf_op jit(solution)/shard_map/all_to_all | solution.py:267
  98.7 16.0 %collective-permute-start.5 = (bf16[224,128]{1,0:T(8,128)(2,1)S(1)}, bf16[224,128]{1,0:T(8,128)(2,1)S(1)}, u32[]{:S(2)}, u32[]{:S(2)}) collective-permute-start(bf16[224,128]{1,0:T(8,128)(2,1)S(1)} %get-tuple-element.19), channel_id=1, source_target_pairs={{0,2},{2,0},{1,3},{3,1},{4,6},{6,4},{5,7},{7,5},{8,10},{10,8},{9,1... | collective-permute-start | bytes 172040 | tf_op jit(solution)/shard_map/ppermute | solution.py:263

commit v3 on v2

v3 whole, which is shorter than its diff:
```python
import functools
import math

import jax
import jax.numpy as jnp
import numpy as np
from jax import lax
from jax.experimental import pallas as pl
from jax.experimental.pallas import tpu as pltpu
from jax.sharding import Mesh
from jax.sharding import PartitionSpec as P

NZL, NX, NY, NZH, NC = 8, 4, 4, 2, 2
CTX = ("zl", "x")
TP = ("y", "zh", "c")

SPAN = 64
ROPE = 64
LAT = 512
NOPE = 128
VD = 128
HEADS = 4
KEYW = LAT + ROPE
ROWW = 640
GROUP = NZL * NZH
NSPAN = 2 * NZL
CHUNK = 256
GROUPED = 4
QW = HEADS * (NOPE + ROPE)
PARTROWS = HEADS * (VD + 16)
BASE = 10000.0
LOW = -1e30
SCALE = math.log2(math.e) / math.sqrt(NOPE + ROPE)
VMEM_LIMIT = 48 * 1024 * 1024


def rotary_tables():
    lane = np.arange(128)
    freq = BASE ** (-2.0 * (lane % 32) / ROPE)
    sign = np.where(lane % 64 < 32, -1.0, 1.0)
    start = (np.arange(64) * SPAN)[:, None] * freq[None, :]
    offset = np.arange(SPAN)[:, None] * freq[None, :]
    tables = [np.cos(start), sign * np.sin(start), np.cos(offset), sign * np.sin(offset)]
    return np.stack(tables).astype(np.float32)


def turn(values, cosine, signed_sine):
    lane = lax.broadcasted_iota(jnp.int32, values.shape, 1)
    partner = jnp.where(
        lane % 64 < 32, pltpu.roll(values, 96, axis=1), pltpu.roll(values, 32, axis=1)
    )
    return values * cosine + partner * signed_sine


def angle_of(tables_ref, span, offset_rows):
    cos_a = tables_ref[0, pl.ds(span, 1), :]
    sin_a = tables_ref[1, pl.ds(span, 1), :]
    cos_b = tables_ref[2, offset_rows, :]
    sin_b = tables_ref[3, offset_rows, :]
    return cos_a * cos_b - sin_a * sin_b, sin_a * cos_b + cos_a * sin_b


def own_ctx():
    return lax.axis_index("zl") * NX + lax.axis_index("x")


def own_tp():
    return (lax.axis_index("y") * NZH + lax.axis_index("zh")) * NC + lax.axis_index("c")


def keys_kernel(spans_ref, keys_ref, tables_ref, out_ref):
    tp = own_tp()
    span = spans_ref[own_ctx() * 2 + tp // 8]
    first = pl.multiple_of((tp % 8) * 8, 8)
    cosine, sine = angle_of(tables_ref, span, pl.ds(first, 8))
    tail = keys_ref[:, LAT:].astype(jnp.float32)
    turned = turn(jnp.concatenate([tail, tail], axis=1), cosine, sine).astype(jnp.bfloat16)
    for k in range(GROUP):
        out_ref[k, :, :LAT] = keys_ref[:, :LAT]
        out_ref[k, :, LAT:] = turned


def queries_kernel(spans_ref, plain_ref, rotary_ref, tables_ref, after_ref, out_ref, kept_spans_ref):
    out_ref[:, : HEADS * NOPE] = plain_ref[...]
    for s in range(2):
        rows = slice(s * SPAN, (s + 1) * SPAN)
        cosine, sine = angle_of(tables_ref, spans_ref[own_ctx() * 2 + s], pl.ds(0, SPAN))
        for j in range(HEADS * ROPE // 128):
            part = rotary_ref[rows, j * 128 : (j + 1) * 128].astype(jnp.float32)
            at = HEADS * NOPE + j * 128
            out_ref[rows, at : at + 128] = (turn(part, cosine, sine) * SCALE).astype(jnp.bfloat16)
    for i in range(kept_spans_ref.shape[0]):
        kept_spans_ref[i] = spans_ref[i]


SMEM = pl.BlockSpec(memory_space=pltpu.SMEM)
WHOLE = pl.BlockSpec(memory_space=pltpu.VMEM)


def absorb_kernel(q0, q1, q2, q3, up_ref, value_ref, query, turned_value):
    blocks = (q0, q1, q2, q3)
    for h in range(HEADS):
        plain = jnp.concatenate([block[:, h * NOPE : (h + 1) * NOPE] for block in blocks], axis=0)
        absorbed = (jnp.dot(plain, up_ref[h], preferred_element_type=jnp.float32) * SCALE).astype(jnp.bfloat16)
        first = HEADS * NOPE + h * ROPE
        at = slice(h * SPAN, (h + 1) * SPAN)
        for b in range(2 * NX):
            query[b, at, :LAT] = absorbed[b * SPAN : (b + 1) * SPAN]
            query[b, at, LAT:] = blocks[b // 2][(b % 2) * SPAN : (b % 2 + 1) * SPAN, first : first + ROPE]
    for h in range(HEADS):
        turned_value[h] = value_ref[h].T


def absorb(blocks, key_up, value_up):
    return pl.pallas_call(
        absorb_kernel,
        out_shape=(
            jax.ShapeDtypeStruct((2 * NX, HEADS * SPAN, KEYW), jnp.bfloat16),
            jax.ShapeDtypeStruct((HEADS, VD, LAT), jnp.bfloat16),
        ),
        in_specs=[WHOLE] * 6,
        out_specs=(WHOLE, WHOLE),
        compiler_params=pltpu.CompilerParams(vmem_limit_bytes=VMEM_LIMIT),
    )(*blocks, key_up, value_up)


def attend_kernel(
    spans_ref, query, own_ref, other_ref, value_ref, out_ref, sorted_keys, latent, contexts, order
):
    zl = lax.axis_index("zl")
    x = lax.axis_index("x")
    c = lax.axis_index("c")

    places = [spans_ref[((i // 2) * NX + x) * 2 + i % 2] for i in range(NSPAN)]

    def earlier(place, among):
        return functools.reduce(jnp.add, [(p < place).astype(jnp.int32) for p in among])

    for i in range(NSPAN):
        rank = earlier(places[i], places)
        for half, keys in enumerate((own_ref, other_ref)):
            for low in range(2):
                source = ((i % 2) * 2 + low) * GROUP * 8 + (i // 2) * NZH * 8
                target = pl.multiple_of(rank * SPAN + half * 32 + low * 16, 16)
                sorted_keys[pl.ds(target, 16), :] = keys[source : source + 16, :]

    asking = [spans_ref[(zl * NX + (x + NX - b // 2) % NX) * 2 + b % 2] for b in range(2 * NX)]
    for b in range(2 * NX):
        order[earlier(asking[b], asking)] = b

    for n in range(NSPAN * SPAN // CHUNK):
        at = slice(n * CHUNK, (n + 1) * CHUNK)
        latent[:, at] = sorted_keys[at, :LAT].T

    row = lax.broadcasted_iota(jnp.int32, (CHUNK, HEADS * SPAN), 0)
    core = jnp.where(row // 32 % 2 == 0, c, 1 - c)
    key_order = row // SPAN * SPAN + row // 16 % 2 * 32 + row // 8 % 2 * 16 + core * 8 + row % 8
    token = lax.broadcasted_iota(jnp.int32, (1, HEADS * SPAN), 1) % SPAN
    dims = (((1,), (1,)), ((), ()))

    def some_spans(turn_of, carry):
        spans = [order[GROUPED * turn_of + i] for i in range(GROUPED)]
        limits = []
        for b in spans:
            source = (x + NX - b // 2) % NX
            below = earlier(spans_ref[(zl * NX + source) * 2 + b % 2], places)
            limits.append(below * SPAN + jnp.where(source == x, token, -1))
            needed = below + (source == x).astype(jnp.int32)
        chunks = jnp.maximum((needed + CHUNK // SPAN - 1) // (CHUNK // SPAN), 1)

        for count in range(1, NSPAN * SPAN // CHUNK + 1):

            @pl.when(chunks == count)
            def _(count=count):
                products = [
                    [
                        lax.dot_general(
                            sorted_keys[n * CHUNK : (n + 1) * CHUNK, :KEYW],
                            query[b],
                            dims,
                            preferred_element_type=jnp.float32,
                        )
                        for n in range(count)
                    ]
                    for b in spans
                ]
                for b, limit, scores in zip(spans, limits, products):
                    scores = [
                        jnp.where(key_order <= limit - n * CHUNK, score, LOW) for n, score in enumerate(scores)
                    ]
                    highest = functools.reduce(jnp.maximum, [jnp.max(v, axis=0, keepdims=True) for v in scores])
                    raised = [jnp.exp2(score - highest) for score in scores]
                    total = functools.reduce(jnp.add, [jnp.sum(v, axis=0, keepdims=True) for v in raised])
                    context = jnp.dot(
                        latent[:, : count * CHUNK],
                        jnp.concatenate([v.astype(jnp.bfloat16) for v in raised], axis=0),
                        preferred_element_type=jnp.float32,
                    )
                    contexts[b, :LAT, :] = (context * (1.0 / total)).astype(jnp.bfloat16)
                    log_sum = highest + jnp.log2(total)
                    high = log_sum.astype(jnp.bfloat16).astype(jnp.float32)
                    rest = log_sum - high
                    middle = rest.astype(jnp.bfloat16).astype(jnp.float32)
                    place = lax.broadcasted_iota(jnp.int32, (16, HEADS * SPAN), 0)
                    packed = jnp.where(place == 0, high, jnp.where(place == 1, middle, rest - middle))
                    contexts[b, LAT:, :] = packed.astype(jnp.bfloat16)

        return carry

    lax.fori_loop(0, 2 * NX // GROUPED, some_spans, 0)

    for h in range(HEADS):
        at = slice(h * SPAN, (h + 1) * SPAN)
        joined = jnp.concatenate([contexts[b, :LAT, at] for b in range(2 * NX)], axis=1)
        values = jnp.dot(value_ref[h], joined, preferred_element_type=jnp.float32).astype(jnp.bfloat16)
        logs = jnp.concatenate([contexts[b, LAT:, at] for b in range(2 * NX)], axis=1)
        for k in range(NX):
            tokens = slice(k * 2 * SPAN, (k + 1) * 2 * SPAN)
            out_ref[(x + NX - k) % NX, h * VD : (h + 1) * VD, :] = values[:, tokens]
            out_ref[(x + NX - k) % NX, HEADS * VD + h * 16 : HEADS * VD + (h + 1) * 16, :] = logs[:, tokens]


def attend(spans, query, own, other, turned_value):
    return pl.pallas_call(
        attend_kernel,
        out_shape=jax.ShapeDtypeStruct((NX, PARTROWS, 2 * SPAN), jnp.bfloat16),
        in_specs=[SMEM] + [WHOLE] * 4,
        out_specs=WHOLE,
        scratch_shapes=[
            pltpu.VMEM((NSPAN * SPAN, ROWW), jnp.bfloat16),
            pltpu.VMEM((LAT, NSPAN * SPAN), jnp.bfloat16),
            pltpu.VMEM((2 * NX, LAT + 16, HEADS * SPAN), jnp.bfloat16),
            pltpu.SMEM((2 * NX,), jnp.int32),
        ],
        compiler_params=pltpu.CompilerParams(vmem_limit_bytes=VMEM_LIMIT),
    )(spans, query, own, other, turned_value)


def project_kernel(parts_ref, weight_ref, send_ref, keep_ref):
    c = lax.axis_index("c")
    heads = []
    for h in range(HEADS):
        at = HEADS * VD + h * 16
        packed = [parts_ref[i, at : at + 16, :].astype(jnp.float32) for i in range(NX)]
        logs = [(p[0:1] + p[1:2]) + p[2:3] for p in packed]
        highest = functools.reduce(jnp.maximum, logs)
        shares = [jnp.exp2(v - highest) for v in logs]
        inverse = 1.0 / functools.reduce(jnp.add, shares)
        merged = functools.reduce(
            jnp.add,
            [
                (shares[i] * inverse) * parts_ref[i, h * VD : (h + 1) * VD, :].astype(jnp.float32)
                for i in range(NX)
            ],
        )
        heads.append(merged.T.astype(jnp.bfloat16))
    head_out = jnp.concatenate(heads, axis=1)
    step = weight_ref.shape[1] // NY
    width = step // (NZH * NC)
    for y in range(NY):
        result = jnp.dot(
            head_out, weight_ref[:, y * step : (y + 1) * step], preferred_element_type=jnp.float32
        ).T.astype(jnp.bfloat16)
        for zh in range(NZH):
            even = result[2 * zh * width : (2 * zh + 1) * width]
            odd = result[(2 * zh + 1) * width : (2 * zh + 2) * width]
            keep_ref[y, zh] = jnp.where(c == 0, even, odd)
            send_ref[y, zh] = jnp.where(c == 0, odd, even)


def project(parts, weight):
    width = weight.shape[1] // (NY * NZH * NC)
    piece = jax.ShapeDtypeStruct((NY, NZH, width, 2 * SPAN), jnp.bfloat16)
    return pl.pallas_call(
        project_kernel,
        out_shape=(piece, piece),
        in_specs=[WHOLE, WHOLE],
        out_specs=(WHOLE, WHOLE),
        compiler_params=pltpu.CompilerParams(vmem_limit_bytes=VMEM_LIMIT),
    )(parts, weight)


def swapped(value, axis):
    return lax.ppermute(value, axis, [(0, 1), (1, 0)])


def exchanged(value, axis):
    return lax.all_to_all(value, axis, split_axis=0, concat_axis=0, tiled=True)


def on_device(query_plain, query_rotary, latent_keys, span_order, key_up, value_up, output_weight):
    zh = lax.axis_index("zh")
    tables = jnp.asarray(rotary_tables())
    sent_keys = pl.pallas_call(
        keys_kernel,
        out_shape=jax.ShapeDtypeStruct((GROUP, 8, ROWW), jnp.bfloat16),
        in_specs=[SMEM, WHOLE, WHOLE],
        out_specs=WHOLE,
    )(span_order, latent_keys, tables)
    rows = jax.ShapeDtypeStruct((2 * SPAN, QW), jnp.bfloat16)
    queries, kept_spans = pl.pallas_call(
        queries_kernel,
        out_shape=(rows, jax.ShapeDtypeStruct(span_order.shape, span_order.dtype)),
        in_specs=[SMEM, WHOLE, WHOLE, WHOLE, pl.BlockSpec(memory_space=pl.ANY)],
        out_specs=(WHOLE, SMEM),
    )(span_order, query_plain, query_rotary, tables, sent_keys)
    along_z = exchanged(sent_keys, ("zl", "zh")).reshape(GROUP * 8, ROWW)
    blocks = [queries] + [
        lax.ppermute(queries, "x", [(i, (i + k) % NX) for i in range(NX)]) for k in range(1, NX)
    ]
    along_z, blocks[1] = lax.optimization_barrier((along_z, blocks[1]))
    own = exchanged(jnp.broadcast_to(along_z[None], (NY, GROUP * 8, ROWW)), "y").reshape(NY * GROUP * 8, ROWW)
    own, blocks[2], blocks[3] = lax.optimization_barrier((own, blocks[2], blocks[3]))
    other = swapped(own, "c")
    query, turned_value = absorb(blocks, key_up, value_up)
    parts = attend(kept_spans, query, own, other, turned_value)
    send, keep = project(exchanged(parts, "x"), output_weight)
    both = (keep.astype(jnp.float32) + swapped(send, "c").astype(jnp.float32)).astype(jnp.bfloat16)
    over_y = exchanged(both, "y").astype(jnp.float32)
    mine = jnp.sum(lax.dynamic_index_in_dim(over_y, zh, 1, keepdims=False), axis=0)
    theirs = jnp.sum(lax.dynamic_index_in_dim(over_y, 1 - zh, 1, keepdims=False), axis=0).astype(jnp.bfloat16)
    return (mine + swapped(theirs, "zh").astype(jnp.float32)).astype(jnp.bfloat16).T


def solution(mesh):
    finer = Mesh(
        mesh.devices.reshape(NZL, NX, NY, NZH, NC), ("zl", "x", "y", "zh", "c")
    )
    in_specs = (
        P(CTX, TP),
        P(CTX, TP),
        P(CTX + TP, None),
        P(),
        P(TP, None, None),
        P(TP, None, None),
        P(TP, None),
    )
    return jax.shard_map(
        on_device, mesh=finer, in_specs=in_specs, out_specs=P(CTX, TP), check_vma=False
    )
```

time: 116 us -> 117 us (level)
  the two profiles are of different devices: /device:TPU:160 before, /device:TPU:2 now
where the time goes in v3:
time: 117 us; the launch traced here: 116 us
  starting transfers between devices  46 us (39%)
  waiting for transfers between devices  36.5 us (31%)
  blocking collectives  15.2 us (13%)
  Pallas kernels  12.8 us (11%)
  local copies, waits for them, and re-layouts  3.91 us (3%)
  other arithmetic  1.64 us (1%)
    all_to_all x3, starting transfers between devices, exchanged(): return lax.all_to_all(value, axis, split_axis=0, concat_axis=0, tiled=True)  24.4 us
    all_to_all x3, waiting for transfers between devices, exchanged(): return lax.all_to_all(value, axis, split_axis=0, concat_axis=0, tiled=True)  15.4 us
    all_to_all x1, blocking collectives, exchanged(): return lax.all_to_all(value, axis, split_axis=0, concat_axis=0, tiled=True)  15.2 us
    ppermute x3, waiting for transfers between devices, swapped(): return lax.ppermute(value, axis, [(0, 1), (1, 0)])  11.7 us
    ppermute x3, starting transfers between devices, swapped(): return lax.ppermute(value, axis, [(0, 1), (1, 0)])  10.8 us
    ppermute x3, starting transfers between devices, on_device(): lax.ppermute(queries, 'x', [(i, (i + k) % NX) for i in range(NX)])  10.8 us
    ppermute x3, waiting for transfers between devices, on_device(): lax.ppermute(queries, 'x', [(i, (i + k) % NX) for i in range(NX)])  9.48 us
    pallas_call x1, Pallas kernels, attend(): pl.pallas_call(attend_kernel, out_shape=jax.ShapeDtypeStruct((NX, PARTROW...  7.55 us
  transfers between devices with their start and end apart: 9, of which 7 were waited for; matrix products, arithmetic and copies ran while one was open for 0% of the time, Pallas kernels for 2%

profile of v3, /device:TPU:2, one launch (start us, length us, event | category | flops | bytes accessed | tf_op | source)
XLA Modules:
  0.0 116.2 jit_solution(6733032342497014383)
XLA Ops:
  0.0 1.7 %shard_map.82.after_ref = bf16[16,8,640]{2,1,0:T(8,128)(2,1)} custom-call(s32[64]{0:T(128)} %spans_ref.3, bf16[8,576]{1,0:T(8,128)(2,1)} %keys_ref.1, f32[4,64,128]{2,1,0:T(8,128)} %constant.20.clone.tables_ref), custom_call_target="tpu_custom_call" | custom-call | tf_op jit(solution)/shard_map/pallas_call | solution.py:294
  1.7 15.2 %all-to-all-start = ((bf16[16,8,640]{2,1,0:T(8,128)(2,1)}), bf16[16,8,640]{2,1,0:T(8,128)(2,1)S(1)}, u32[]{:S(2)}, u32[]{:S(2)}) async-start(bf16[16,8,640]{2,1,0:T(8,128)(2,1)} %shard_map.82.after_ref), calls=%async_computation | async-start | bytes 327680 | tf_op jit(solution)/shard_map/all_to_all | solution.py:288
  16.9 1.8 %shard_map.83 = (bf16[128,768]{1,0:T(8,128)(2,1)}, s32[64]{0:T(128)}) custom-call(s32[64]{0:T(128)} %spans_ref.3, bf16[128,512]{1,0:T(8,128)(2,1)} %plain_ref.1, bf16[128,256]{1,0:T(8,128)(2,1)} %rotary_ref.1, f32[4,64,128]{2,1,0:T(8,128)} %constant.20.clone.tables_ref, bf16[16,8,640]{2,1,0:T(8,128)(2,1)} %shard_map.82.after_ref), custom_call_target="tpu_custom_call" | custom-call | tf_op jit(solution)/shard_map/pallas_call | solution.py:301
  18.8 3.4 %collective-permute-start = (bf16[128,768]{1,0:T(8,128)(2,1)}, bf16[128,768]{1,0:T(8,128)(2,1)S(1)}, u32[]{:S(2)}, u32[]{:S(2)}) collective-permute-start(bf16[128,768]{1,0:T(8,128)(2,1)} %get-tuple-element.17.q0), channel_id=1, source_target_pairs={{0,16},{16,32},{32,48},{48,0},{1,17},{17,33},{33,49},{49,1},{2,18}... | collective-permute-start | bytes 589832 | tf_op jit(solution)/shard_map/ppermute | solution.py:309
  22.2 5.1 %collective-permute-done.q1 = bf16[128,768]{1,0:T(8,128)(2,1)S(1)} collective-permute-done((bf16[128,768]{1,0:T(8,128)(2,1)}, bf16[128,768]{1,0:T(8,128)(2,1)S(1)}, u32[]{:S(2)}, u32[]{:S(2)}) %collective-permute-start) | collective-permute-done | bytes 196640 | tf_op jit(solution)/shard_map/ppermute | solution.py:309
  27.2 6.3 %all-to-all-done = bf16[16,8,640]{2,1,0:T(8,128)(2,1)S(1)} async-done(((bf16[16,8,640]{2,1,0:T(8,128)(2,1)}), bf16[16,8,640]{2,1,0:T(8,128)(2,1)S(1)}, u32[]{:S(2)}, u32[]{:S(2)}) %all-to-all-start) | async-done | bytes 163872 | tf_op jit(solution)/shard_map/all_to_all | solution.py:288
  34.4 4.5 %all-to-all-start.1 = ((bf16[4,128,640]{2,1,0:T(8,128)(2,1)}), bf16[4,128,640]{2,1,0:T(8,128)(2,1)S(1)}, u32[]{:S(2)}, u32[]{:S(2)}) async-start(bf16[4,128,640]{2,1,0:T(8,128)(2,1)} %broadcast_in_dim.2), calls=%async_computation.1 | async-start | bytes 1310720 | tf_op jit(solution)/shard_map/all_to_all | solution.py:288
  38.9 4.0 %collective-permute-start.1 = (bf16[128,768]{1,0:T(8,128)(2,1)}, bf16[128,768]{1,0:T(8,128)(2,1)S(1)}, u32[]{:S(2)}, u32[]{:S(2)}) collective-permute-start(bf16[128,768]{1,0:T(8,128)(2,1)} %get-tuple-element.17.q0), channel_id=1, source_target_pairs={{0,32},{16,48},{32,0},{48,16},{1,33},{17,49},{33,1},{49,17},{2,34}... | collective-permute-start | bytes 589832 | tf_op jit(solution)/shard_map/ppermute | solution.py:309
  42.9 3.3 %collective-permute-start.2 = (bf16[128,768]{1,0:T(8,128)(2,1)}, bf16[128,768]{1,0:T(8,128)(2,1)S(1)}, u32[]{:S(2)}, u32[]{:S(2)}) collective-permute-start(bf16[128,768]{1,0:T(8,128)(2,1)} %get-tuple-element.17.q0), channel_id=1, source_target_pairs={{0,48},{16,0},{32,16},{48,32},{1,49},{17,1},{33,17},{49,33},{2,50}... | collective-permute-start | bytes 589832 | tf_op jit(solution)/shard_map/ppermute | solution.py:309
  46.3 2.0 %collective-permute-done.1.q2 = bf16[128,768]{1,0:T(8,128)(2,1)S(1)} collective-permute-done((bf16[128,768]{1,0:T(8,128)(2,1)}, bf16[128,768]{1,0:T(8,128)(2,1)S(1)}, u32[]{:S(2)}, u32[]{:S(2)}) %collective-permute-start.1) | collective-permute-done | bytes 196640 | tf_op jit(solution)/shard_map/ppermute | solution.py:309
  48.3 2.4 %collective-permute-done.2.q3 = bf16[128,768]{1,0:T(8,128)(2,1)S(1)} collective-permute-done((bf16[128,768]{1,0:T(8,128)(2,1)}, bf16[128,768]{1,0:T(8,128)(2,1)S(1)}, u32[]{:S(2)}, u32[]{:S(2)}) %collective-permute-start.2) | collective-permute-done | bytes 196640 | tf_op jit(solution)/shard_map/ppermute | solution.py:309
  50.7 2.2 %collective-permute-start.3 = (bf16[512,640]{1,0:T(8,128)(2,1)S(1)}, bf16[512,640]{1,0:T(8,128)(2,1)S(1)}, u32[]{:S(2)}, u32[]{:S(2)}) collective-permute-start(bf16[512,640]{1,0:T(8,128)(2,1)S(1)} %bitcast.4), channel_id=1, source_target_pairs={{0,1},{1,0},{2,3},{3,2},{4,5},{5,4},{6,7},{7,6},{8,9},{9,8},{10,11... | collective-permute-start | bytes 1966088 | tf_op jit(solution)/shard_map/ppermute | solution.py:284
  52.9 1.0 copy-done.1
  53.9 1.0 copy-done.2
  55.0 0.9 copy-done.3
  56.7 7.6 %shard_map.85 = bf16[4,576,128]{2,1,0:T(8,128)(2,1)S(1)} custom-call(s32[64]{0:T(128)S(1)} %copy-done.4, bf16[8,256,576]{2,1,0:T(8,128)(2,1)S(1)} %get-tuple-element.22.query, bf16[512,640]{1,0:T(8,128)(2,1)S(1)} %bitcast.5, bf16[512,640]{1,0:T(8,128)(2,1)S(1)} %collective-permute-done.3.other_ref, bf16[4,128,512]{2,1,0:T(8,128)(2,1)S(1)} %get-tuple-element.24.value_ref), custom_call_target="tpu_custom_call" | custom-call | tf_op jit(solution)/shard_map/pallas_call | solution.py:224
  64.3 15.2 %all_to_all.20.parts_ref = bf16[4,576,128]{2,1,0:T(8,128)(2,1)S(1)} all-to-all(bf16[4,576,128]{2,1,0:T(8,128)(2,1)S(1)} %shard_map.85), channel_id=1, replica_groups=mesh['zl'=8,'x'=4,'y'=4,'zh'=2,'c'=2] {'x'}, dimensions={0} | all-to-all | bytes 1179648 | tf_op jit(solution)/shard_map/all_to_all | solution.py:288
  79.5 0.9 shard_map.86
  80.4 1.9 %collective-permute-start.4 = (bf16[4,2,224,128]{3,2,1,0:T(8,128)(2,1)S(1)}, bf16[4,2,224,128]{3,2,1,0:T(8,128)(2,1)S(1)}, u32[]{:S(2)}, u32[]{:S(2)}) collective-permute-start(bf16[4,2,224,128]{3,2,1,0:T(8,128)(2,1)S(1)} %get-tuple-element.26), channel_id=1, source_target_pairs={{0,1},{1,0},{2,3},{3,2},{4,5},{5,4},{6,7},{7,6},{8,9},{9,8},{10,11... | collective-permute-start | bytes 1376264 | tf_op jit(solution)/shard_map/ppermute | solution.py:284
  82.3 1.8 %collective-permute-done.4 = bf16[4,2,224,128]{3,2,1,0:T(8,128)(2,1)S(1)} collective-permute-done((bf16[4,2,224,128]{3,2,1,0:T(8,128)(2,1)S(1)}, bf16[4,2,224,128]{3,2,1,0:T(8,128)(2,1)S(1)}, u32[]{:S(2)}, u32[]{:S(2)}) %collective-permute-start.4) | collective-permute-done | bytes 458784 | tf_op jit(solution)/shard_map/ppermute | solution.py:284
  85.0 4.7 %all-to-all-start.3 = ((bf16[4,2,224,128]{3,2,1,0:T(8,128)(2,1)}), bf16[4,2,224,128]{3,2,1,0:T(8,128)(2,1)S(1)}, u32[]{:S(2)}, u32[]{:S(2)}) async-start(bf16[4,2,224,128]{3,2,1,0:T(8,128)(2,1)} %add_convert_fusion), calls=%async_computation.3 | async-start | bytes 917504 | tf_op jit(solution)/shard_map/all_to_all | solution.py:288
  89.7 9.1 %all-to-all-done.3 = bf16[4,2,224,128]{3,2,1,0:T(8,128)(2,1)S(1)} async-done(((bf16[4,2,224,128]{3,2,1,0:T(8,128)(2,1)}), bf16[4,2,224,128]{3,2,1,0:T(8,128)(2,1)S(1)}, u32[]{:S(2)}, u32[]{:S(2)}) %all-to-all-start.3) | async-done | bytes 458784 | tf_op jit(solution)/shard_map/all_to_all | solution.py:288
  98.9 6.7 %collective-permute-start.5 = (bf16[224,128]{1,0:T(8,128)(2,1)S(1)}, bf16[224,128]{1,0:T(8,128)(2,1)S(1)}, u32[]{:S(2)}, u32[]{:S(2)}) collective-permute-start(bf16[224,128]{1,0:T(8,128)(2,1)S(1)} %get-tuple-element.27), channel_id=1, source_target_pairs={{0,2},{2,0},{1,3},{3,1},{4,6},{6,4},{5,7},{7,5},{8,10},{10,8},{9,1... | collective-permute-start | bytes 172040 | tf_op jit(solution)/shard_map/ppermute | solution.py:284
  105.7 9.9 %collective-permute-done.5 = bf16[224,128]{1,0:T(8,128)(2,1)S(1)} collective-permute-done((bf16[224,128]{1,0:T(8,128)(2,1)S(1)}, bf16[224,128]{1,0:T(8,128)(2,1)S(1)}, u32[]{:S(2)}, u32[]{:S(2)}) %collective-permute-start.5) | collective-permute-done | bytes 57376 | tf_op jit(solution)/shard_map/ppermute | solution.py:284
  (15 shorter events, 3.3 us)
Async XLA Ops:
  1.7 31.8 %all-to-all-start = ((bf16[16,8,640]{2,1,0:T(8,128)(2,1)}), bf16[16,8,640]{2,1,0:T(8,128)(2,1)S(1)}, u32[]{:S(2)}, u32[]{:S(2)}) async-start(bf16[16,8,640]{2,1,0:T(8,128)(2,1)} %shard_map.82.after_ref), calls=%async_computation | async-start | bytes 327680 | tf_op jit(solution)/shard_map/all_to_all | solution.py:288
  18.8 37.9 %copy-start.4 = (s32[64]{0:T(128)S(1)}, s32[64]{0:T(128)}, u32[]{:S(2)}) copy-start(s32[64]{0:T(128)} %get-tuple-element.16.spans_ref) | copy-start | bytes 772
  18.8 8.5 %collective-permute-start = (bf16[128,768]{1,0:T(8,128)(2,1)}, bf16[128,768]{1,0:T(8,128)(2,1)S(1)}, u32[]{:S(2)}, u32[]{:S(2)}) collective-permute-start(bf16[128,768]{1,0:T(8,128)(2,1)} %get-tuple-element.17.q0), channel_id=1, source_target_pairs={{0,16},{16,32},{32,48},{48,0},{1,17},{17,33},{33,49},{49,1},{2,18}... | collective-permute-start | bytes 589832 | tf_op jit(solution)/shard_map/ppermute | solution.py:309
  34.4 16.3 %all-to-all-start.1 = ((bf16[4,128,640]{2,1,0:T(8,128)(2,1)}), bf16[4,128,640]{2,1,0:T(8,128)(2,1)S(1)}, u32[]{:S(2)}, u32[]{:S(2)}) async-start(bf16[4,128,640]{2,1,0:T(8,128)(2,1)} %broadcast_in_dim.2), calls=%async_computation.1 | async-start | bytes 1310720 | tf_op jit(solution)/shard_map/all_to_all | solution.py:288
  38.9 9.4 %collective-permute-start.1 = (bf16[128,768]{1,0:T(8,128)(2,1)}, bf16[128,768]{1,0:T(8,128)(2,1)S(1)}, u32[]{:S(2)}, u32[]{:S(2)}) collective-permute-start(bf16[128,768]{1,0:T(8,128)(2,1)} %get-tuple-element.17.q0), channel_id=1, source_target_pairs={{0,32},{16,48},{32,0},{48,16},{1,33},{17,49},{33,1},{49,17},{2,34}... | collective-permute-start | bytes 589832 | tf_op jit(solution)/shard_map/ppermute | solution.py:309
  42.9 7.8 %collective-permute-start.2 = (bf16[128,768]{1,0:T(8,128)(2,1)}, bf16[128,768]{1,0:T(8,128)(2,1)S(1)}, u32[]{:S(2)}, u32[]{:S(2)}) collective-permute-start(bf16[128,768]{1,0:T(8,128)(2,1)} %get-tuple-element.17.q0), channel_id=1, source_target_pairs={{0,48},{16,0},{32,16},{48,32},{1,49},{17,1},{33,17},{49,33},{2,50}... | collective-permute-start | bytes 589832 | tf_op jit(solution)/shard_map/ppermute | solution.py:309
  50.7 28.8 %copy-start = (bf16[512,3584]{1,0:T(8,128)(2,1)S(1)}, bf16[512,3584]{1,0:T(8,128)(2,1)}, u32[]{:S(2)}) copy-start(bf16[512,3584]{1,0:T(8,128)(2,1)} %weight_ref.1) | copy-start | bytes 11010052
  50.7 6.0 %collective-permute-start.3 = (bf16[512,640]{1,0:T(8,128)(2,1)S(1)}, bf16[512,640]{1,0:T(8,128)(2,1)S(1)}, u32[]{:S(2)}, u32[]{:S(2)}) collective-permute-start(bf16[512,640]{1,0:T(8,128)(2,1)S(1)} %bitcast.4), channel_id=1, source_target_pairs={{0,1},{1,0},{2,3},{3,2},{4,5},{5,4},{6,7},{7,6},{8,9},{9,8},{10,11... | collective-permute-start | bytes 1966088 | tf_op jit(solution)/shard_map/ppermute | solution.py:284
  52.9 1.0 copy-start.1
  53.9 1.0 copy-start.2
  55.0 0.9 copy-start.3
  80.4 3.7 %collective-permute-start.4 = (bf16[4,2,224,128]{3,2,1,0:T(8,128)(2,1)S(1)}, bf16[4,2,224,128]{3,2,1,0:T(8,128)(2,1)S(1)}, u32[]{:S(2)}, u32[]{:S(2)}) collective-permute-start(bf16[4,2,224,128]{3,2,1,0:T(8,128)(2,1)S(1)} %get-tuple-element.26), channel_id=1, source_target_pairs={{0,1},{1,0},{2,3},{3,2},{4,5},{5,4},{6,7},{7,6},{8,9},{9,8},{10,11... | collective-permute-start | bytes 1376264 | tf_op jit(solution)/shard_map/ppermute | solution.py:284
  85.0 13.8 %all-to-all-start.3 = ((bf16[4,2,224,128]{3,2,1,0:T(8,128)(2,1)}), bf16[4,2,224,128]{3,2,1,0:T(8,128)(2,1)S(1)}, u32[]{:S(2)}, u32[]{:S(2)}) async-start(bf16[4,2,224,128]{3,2,1,0:T(8,128)(2,1)} %add_convert_fusion), calls=%async_computation.3 | async-start | bytes 917504 | tf_op jit(solution)/shard_map/all_to_all | solution.py:288
  98.9 16.6 %collective-permute-start.5 = (bf16[224,128]{1,0:T(8,128)(2,1)S(1)}, bf16[224,128]{1,0:T(8,128)(2,1)S(1)}, u32[]{:S(2)}, u32[]{:S(2)}) collective-permute-start(bf16[224,128]{1,0:T(8,128)(2,1)S(1)} %get-tuple-element.27), channel_id=1, source_target_pairs={{0,2},{2,0},{1,3},{3,1},{4,6},{6,4},{5,7},{7,5},{8,10},{10,8},{9,1... | collective-permute-start | bytes 172040 | tf_op jit(solution)/shard_map/ppermute | solution.py:284

commit v4 on v3

--- a/solution.py
+++ b/solution.py
@@ -27,7 +27,7 @@
 CHUNK = 256
 GROUPED = 4
 QW = HEADS * (NOPE + ROPE)
-PARTROWS = HEADS * (VD + 16)
+PARTROWS = HEADS * VD + 16
 BASE = 10000.0
 LOW = -1e30
 SCALE = math.log2(math.e) / math.sqrt(NOPE + ROPE)
@@ -95,9 +95,18 @@
 
 SMEM = pl.BlockSpec(memory_space=pltpu.SMEM)
 WHOLE = pl.BlockSpec(memory_space=pltpu.VMEM)
-
-
-def absorb_kernel(q0, q1, q2, q3, up_ref, value_ref, query, turned_value):
+HBM = pl.BlockSpec(memory_space=pltpu.HBM)
+
+
+def absorb_kernel(q0_hbm, q1, q2, q3, up_hbm, value_hbm, query, turned_value, q0, up_ref, value_ref, arrived):
+    fetches = [
+        pltpu.make_async_copy(source, target, arrived.at[i])
+        for i, (source, target) in enumerate(((q0_hbm, q0), (up_hbm, up_ref), (value_hbm, value_ref)))
+    ]
+    for fetch in fetches:
+        fetch.start()
+    for fetch in fetches:
+        fetch.wait()
     blocks = (q0, q1, q2, q3)
     for h in range(HEADS):
         plain = jnp.concatenate([block[:, h * NOPE : (h + 1) * NOPE] for block in blocks], axis=0)
@@ -111,6 +120,10 @@
         turned_value[h] = value_ref[h].T
 
 
+def in_hbm(value):
+    return pltpu.with_memory_space_constraint(value, pltpu.HBM)
+
+
 def absorb(blocks, key_up, value_up):
     return pl.pallas_call(
         absorb_kernel,
@@ -118,10 +131,16 @@
             jax.ShapeDtypeStruct((2 * NX, HEADS * SPAN, KEYW), jnp.bfloat16),
             jax.ShapeDtypeStruct((HEADS, VD, LAT), jnp.bfloat16),
         ),
-        in_specs=[WHOLE] * 6,
+        in_specs=[HBM] + [WHOLE] * 3 + [HBM] * 2,
         out_specs=(WHOLE, WHOLE),
+        scratch_shapes=[
+            pltpu.VMEM(blocks[0].shape, jnp.bfloat16),
+            pltpu.VMEM(key_up.shape, jnp.bfloat16),
+            pltpu.VMEM(value_up.shape, jnp.bfloat16),
+            pltpu.SemaphoreType.DMA((3,)),
+        ],
         compiler_params=pltpu.CompilerParams(vmem_limit_bytes=VMEM_LIMIT),
-    )(*blocks, key_up, value_up)
+    )(in_hbm(blocks[0]), *blocks[1:], in_hbm(key_up), in_hbm(value_up))
 
 
 def attend_kernel(
@@ -156,6 +175,7 @@
     core = jnp.where(row // 32 % 2 == 0, c, 1 - c)
     key_order = row // SPAN * SPAN + row // 16 % 2 * 32 + row // 8 % 2 * 16 + core * 8 + row % 8
     token = lax.broadcasted_iota(jnp.int32, (1, HEADS * SPAN), 1) % SPAN
+    head = lax.broadcasted_iota(jnp.int32, (16, HEADS * SPAN), 1) // SPAN
     dims = (((1,), (1,)), ((), ()))
 
     def some_spans(turn_of, carry):
@@ -202,7 +222,8 @@
                     rest = log_sum - high
                     middle = rest.astype(jnp.bfloat16).astype(jnp.float32)
                     place = lax.broadcasted_iota(jnp.int32, (16, HEADS * SPAN), 0)
-                    packed = jnp.where(place == 0, high, jnp.where(place == 1, middle, rest - middle))
+                    packed = jnp.where(place < HEADS, high, jnp.where(place < 2 * HEADS, middle, rest - middle))
+                    packed = jnp.where((place < 3 * HEADS) & (place % HEADS == head), packed, 0.0)
                     contexts[b, LAT:, :] = packed.astype(jnp.bfloat16)
 
         return carry
@@ -213,11 +234,21 @@
         at = slice(h * SPAN, (h + 1) * SPAN)
         joined = jnp.concatenate([contexts[b, :LAT, at] for b in range(2 * NX)], axis=1)
         values = jnp.dot(value_ref[h], joined, preferred_element_type=jnp.float32).astype(jnp.bfloat16)
-        logs = jnp.concatenate([contexts[b, LAT:, at] for b in range(2 * NX)], axis=1)
         for k in range(NX):
             tokens = slice(k * 2 * SPAN, (k + 1) * 2 * SPAN)
             out_ref[(x + NX - k) % NX, h * VD : (h + 1) * VD, :] = values[:, tokens]
-            out_ref[(x + NX - k) % NX, HEADS * VD + h * 16 : HEADS * VD + (h + 1) * 16, :] = logs[:, tokens]
+    for k in range(NX):
+        logs = [
+            functools.reduce(
+                jnp.add,
+                [
+                    contexts[b, LAT:, h * SPAN : (h + 1) * SPAN].astype(jnp.float32)
+                    for h in range(HEADS)
+                ],
+            )
+            for b in (2 * k, 2 * k + 1)
+        ]
+        out_ref[(x + NX - k) % NX, HEADS * VD :, :] = jnp.concatenate(logs, axis=1).astype(jnp.bfloat16)
 
 
 def attend(spans, query, own, other, turned_value):
@@ -239,10 +270,9 @@
 def project_kernel(parts_ref, weight_ref, send_ref, keep_ref):
     c = lax.axis_index("c")
     heads = []
+    packed = [parts_ref[i, HEADS * VD :, :].astype(jnp.float32) for i in range(NX)]
     for h in range(HEADS):
-        at = HEADS * VD + h * 16
-        packed = [parts_ref[i, at : at + 16, :].astype(jnp.float32) for i in range(NX)]
-        logs = [(p[0:1] + p[1:2]) + p[2:3] for p in packed]
+        logs = [(p[h : h + 1] + p[HEADS + h : HEADS + h + 1]) + p[2 * HEADS + h : 2 * HEADS + h + 1] for p in packed]
         highest = functools.reduce(jnp.maximum, logs)
         shares = [jnp.exp2(v - highest) for v in logs]
         inverse = 1.0 / functools.reduce(jnp.add, shares)
@@ -308,9 +338,9 @@
     blocks = [queries] + [
         lax.ppermute(queries, "x", [(i, (i + k) % NX) for i in range(NX)]) for k in range(1, NX)
     ]
-    along_z, blocks[1] = lax.optimization_barrier((along_z, blocks[1]))
+    along_z, blocks[1], blocks[3] = lax.optimization_barrier((along_z, blocks[1], blocks[3]))
     own = exchanged(jnp.broadcast_to(along_z[None], (NY, GROUP * 8, ROWW)), "y").reshape(NY * GROUP * 8, ROWW)
-    own, blocks[2], blocks[3] = lax.optimization_barrier((own, blocks[2], blocks[3]))
+    own, blocks[2] = lax.optimization_barrier((own, blocks[2]))
     other = swapped(own, "c")
     query, turned_value = absorb(blocks, key_up, value_up)
     parts = attend(kept_spans, query, own, other, turned_value)

time: 117 us -> 113 us (0.966)
  the two profiles are of different devices: /device:TPU:2 before, /device:TPU:32 now
where the time goes in v4:
time: 113 us; the launch traced here: 112 us
  starting transfers between devices  47.9 us (42%)
  waiting for transfers between devices  33.4 us (30%)
  blocking collectives  14.4 us (13%)
  Pallas kernels  14 us (12%)
  other arithmetic  1.66 us (1%)
    all_to_all x3, starting transfers between devices, exchanged(): return lax.all_to_all(value, axis, split_axis=0, concat_axis=0, tiled=True)  24.5 us
    all_to_all x1, blocking collectives, exchanged(): return lax.all_to_all(value, axis, split_axis=0, concat_axis=0, tiled=True)  14.4 us
    all_to_all x3, waiting for transfers between devices, exchanged(): return lax.all_to_all(value, axis, split_axis=0, concat_axis=0, tiled=True)  12.6 us
    ppermute x3, waiting for transfers between devices, swapped(): return lax.ppermute(value, axis, [(0, 1), (1, 0)])  12.2 us
    ppermute x3, starting transfers between devices, on_device(): lax.ppermute(queries, 'x', [(i, (i + k) % NX) for i in range(NX)])  12 us
    ppermute x3, starting transfers between devices, swapped(): return lax.ppermute(value, axis, [(0, 1), (1, 0)])  11.5 us
    ppermute x3, waiting for transfers between devices, on_device(): lax.ppermute(queries, 'x', [(i, (i + k) % NX) for i in range(NX)])  8.58 us
    pallas_call x1, Pallas kernels, attend(): pl.pallas_call(attend_kernel, out_shape=jax.ShapeDtypeStruct((NX, PARTROW...  7.48 us
  transfers between devices with their start and end apart: 9, of which 7 were waited for; matrix products, arithmetic and copies ran while one was open for 0% of the time, Pallas kernels for 3%

profile of v4, /device:TPU:32, one launch (start us, length us, event | category | flops | bytes accessed | tf_op | source)
XLA Modules:
  0.0 112.5 jit_solution(6040616825961998352)
XLA Ops:
  0.0 1.7 %shard_map.82.after_ref = bf16[16,8,640]{2,1,0:T(8,128)(2,1)} custom-call(s32[64]{0:T(128)} %spans_ref.3, bf16[8,576]{1,0:T(8,128)(2,1)} %keys_ref.1, f32[4,64,128]{2,1,0:T(8,128)} %constant.20.clone.tables_ref), custom_call_target="tpu_custom_call" | custom-call | tf_op jit(solution)/shard_map/pallas_call | solution.py:324
  1.7 15.2 %all-to-all-start = ((bf16[16,8,640]{2,1,0:T(8,128)(2,1)}), bf16[16,8,640]{2,1,0:T(8,128)(2,1)S(1)}, u32[]{:S(2)}, u32[]{:S(2)}) async-start(bf16[16,8,640]{2,1,0:T(8,128)(2,1)} %shard_map.82.after_ref), calls=%async_computation | async-start | bytes 327680 | tf_op jit(solution)/shard_map/all_to_all | solution.py:318
  17.0 1.8 %shard_map.83 = (bf16[128,768]{1,0:T(8,128)(2,1)}, s32[64]{0:T(128)}) custom-call(s32[64]{0:T(128)} %spans_ref.3, bf16[128,512]{1,0:T(8,128)(2,1)} %plain_ref.1, bf16[128,256]{1,0:T(8,128)(2,1)} %rotary_ref.1, f32[4,64,128]{2,1,0:T(8,128)} %constant.20.clone.tables_ref, bf16[16,8,640]{2,1,0:T(8,128)(2,1)} %shard_map.82.after_ref), custom_call_target="tpu_custom_call" | custom-call | tf_op jit(solution)/shard_map/pallas_call | solution.py:331
  18.8 3.4 %collective-permute-start = (bf16[128,768]{1,0:T(8,128)(2,1)}, bf16[128,768]{1,0:T(8,128)(2,1)S(1)}, u32[]{:S(2)}, u32[]{:S(2)}) collective-permute-start(bf16[128,768]{1,0:T(8,128)(2,1)} %get-tuple-element.17.q0_hbm), channel_id=1, source_target_pairs={{0,16},{16,32},{32,48},{48,0},{1,17},{17,33},{33,49},{49,1},{2,18}... | collective-permute-start | bytes 589832 | tf_op jit(solution)/shard_map/ppermute | solution.py:339
  22.2 3.7 %collective-permute-start.1 = (bf16[128,768]{1,0:T(8,128)(2,1)}, bf16[128,768]{1,0:T(8,128)(2,1)S(1)}, u32[]{:S(2)}, u32[]{:S(2)}) collective-permute-start(bf16[128,768]{1,0:T(8,128)(2,1)} %get-tuple-element.17.q0_hbm), channel_id=1, source_target_pairs={{0,48},{16,0},{32,16},{48,32},{1,49},{17,1},{33,17},{49,33},{2,50}... | collective-permute-start | bytes 589832 | tf_op jit(solution)/shard_map/ppermute | solution.py:339
  25.9 2.3 %collective-permute-done.q1 = bf16[128,768]{1,0:T(8,128)(2,1)S(1)} collective-permute-done((bf16[128,768]{1,0:T(8,128)(2,1)}, bf16[128,768]{1,0:T(8,128)(2,1)S(1)}, u32[]{:S(2)}, u32[]{:S(2)}) %collective-permute-start) | collective-permute-done | bytes 196640 | tf_op jit(solution)/shard_map/ppermute | solution.py:339
  28.2 1.9 %collective-permute-done.1.q3 = bf16[128,768]{1,0:T(8,128)(2,1)S(1)} collective-permute-done((bf16[128,768]{1,0:T(8,128)(2,1)}, bf16[128,768]{1,0:T(8,128)(2,1)S(1)}, u32[]{:S(2)}, u32[]{:S(2)}) %collective-permute-start.1) | collective-permute-done | bytes 196640 | tf_op jit(solution)/shard_map/ppermute | solution.py:339
  30.1 3.5 %all-to-all-done = bf16[16,8,640]{2,1,0:T(8,128)(2,1)S(1)} async-done(((bf16[16,8,640]{2,1,0:T(8,128)(2,1)}), bf16[16,8,640]{2,1,0:T(8,128)(2,1)S(1)}, u32[]{:S(2)}, u32[]{:S(2)}) %all-to-all-start) | async-done | bytes 163872 | tf_op jit(solution)/shard_map/all_to_all | solution.py:318
  33.6 0.9 broadcast_in_dim.2
  34.5 4.5 %all-to-all-start.1 = ((bf16[4,128,640]{2,1,0:T(8,128)(2,1)}), bf16[4,128,640]{2,1,0:T(8,128)(2,1)S(1)}, u32[]{:S(2)}, u32[]{:S(2)}) async-start(bf16[4,128,640]{2,1,0:T(8,128)(2,1)} %broadcast_in_dim.2), calls=%async_computation.1 | async-start | bytes 1310720 | tf_op jit(solution)/shard_map/all_to_all | solution.py:318
  38.9 4.9 %collective-permute-start.2 = (bf16[128,768]{1,0:T(8,128)(2,1)}, bf16[128,768]{1,0:T(8,128)(2,1)S(1)}, u32[]{:S(2)}, u32[]{:S(2)}) collective-permute-start(bf16[128,768]{1,0:T(8,128)(2,1)} %get-tuple-element.17.q0_hbm), channel_id=1, source_target_pairs={{0,32},{16,48},{32,0},{48,16},{1,33},{17,49},{33,1},{49,17},{2,34}... | collective-permute-start | bytes 589832 | tf_op jit(solution)/shard_map/ppermute | solution.py:339
  43.9 4.3 %collective-permute-done.2.q2 = bf16[128,768]{1,0:T(8,128)(2,1)S(1)} collective-permute-done((bf16[128,768]{1,0:T(8,128)(2,1)}, bf16[128,768]{1,0:T(8,128)(2,1)S(1)}, u32[]{:S(2)}, u32[]{:S(2)}) %collective-permute-start.2) | collective-permute-done | bytes 196640 | tf_op jit(solution)/shard_map/ppermute | solution.py:339
  48.2 2.2 %collective-permute-start.3 = (bf16[512,640]{1,0:T(8,128)(2,1)S(1)}, bf16[512,640]{1,0:T(8,128)(2,1)S(1)}, u32[]{:S(2)}, u32[]{:S(2)}) collective-permute-start(bf16[512,640]{1,0:T(8,128)(2,1)S(1)} %bitcast.4), channel_id=1, source_target_pairs={{0,1},{1,0},{2,3},{3,2},{4,5},{5,4},{6,7},{7,6},{8,9},{9,8},{10,11... | collective-permute-start | bytes 1966088 | tf_op jit(solution)/shard_map/ppermute | solution.py:314
  50.4 2.1 %shard_map.84 = (bf16[8,256,576]{2,1,0:T(8,128)(2,1)S(1)}, bf16[4,128,512]{2,1,0:T(8,128)(2,1)S(1)}) custom-call(bf16[128,768]{1,0:T(8,128)(2,1)} %get-tuple-element.17.q0_hbm, bf16[128,768]{1,0:T(8,128)(2,1)S(1)} %collective-permute-done.q1, bf16[128,768]{1,0:T(8,128)(2,1)S(1)} %collective-permute-done.2.q2, ...), custom_call_target="tpu_custom_call" | custom-call | tf_op jit(solution)/shard_map/pallas_call | solution.py:128
  52.5 7.5 %shard_map.85 = bf16[4,528,128]{2,1,0:T(8,128)(2,1)S(1)} custom-call(s32[64]{0:T(128)S(1)} %copy-done.1, bf16[8,256,576]{2,1,0:T(8,128)(2,1)S(1)} %get-tuple-element.22.query, bf16[512,640]{1,0:T(8,128)(2,1)S(1)} %bitcast.5, bf16[512,640]{1,0:T(8,128)(2,1)S(1)} %collective-permute-done.3.other_ref, bf16[4,128,512]{2,1,0:T(8,128)(2,1)S(1)} %get-tuple-element.24.value_ref), custom_call_target="tpu_custom_call" | custom-call | tf_op jit(solution)/shard_map/pallas_call | solution.py:255
  60.0 14.4 %all_to_all.20.parts_ref = bf16[4,528,128]{2,1,0:T(8,128)(2,1)S(1)} all-to-all(bf16[4,528,128]{2,1,0:T(8,128)(2,1)S(1)} %shard_map.85), channel_id=1, replica_groups=mesh['zl'=8,'x'=4,'y'=4,'zh'=2,'c'=2] {'x'}, dimensions={0} | all-to-all | bytes 1081344 | tf_op jit(solution)/shard_map/all_to_all | solution.py:318
  74.4 0.9 shard_map.86
  75.3 1.9 %collective-permute-start.4 = (bf16[4,2,224,128]{3,2,1,0:T(8,128)(2,1)S(1)}, bf16[4,2,224,128]{3,2,1,0:T(8,128)(2,1)S(1)}, u32[]{:S(2)}, u32[]{:S(2)}) collective-permute-start(bf16[4,2,224,128]{3,2,1,0:T(8,128)(2,1)S(1)} %get-tuple-element.26), channel_id=1, source_target_pairs={{0,1},{1,0},{2,3},{3,2},{4,5},{5,4},{6,7},{7,6},{8,9},{9,8},{10,11... | collective-permute-start | bytes 1376264 | tf_op jit(solution)/shard_map/ppermute | solution.py:314
  77.2 1.8 %collective-permute-done.4 = bf16[4,2,224,128]{3,2,1,0:T(8,128)(2,1)S(1)} collective-permute-done((bf16[4,2,224,128]{3,2,1,0:T(8,128)(2,1)S(1)}, bf16[4,2,224,128]{3,2,1,0:T(8,128)(2,1)S(1)}, u32[]{:S(2)}, u32[]{:S(2)}) %collective-permute-start.4) | collective-permute-done | bytes 458784 | tf_op jit(solution)/shard_map/ppermute | solution.py:314
  79.0 0.9 add_convert_fusion
  79.9 4.8 %all-to-all-start.3 = ((bf16[4,2,224,128]{3,2,1,0:T(8,128)(2,1)}), bf16[4,2,224,128]{3,2,1,0:T(8,128)(2,1)S(1)}, u32[]{:S(2)}, u32[]{:S(2)}) async-start(bf16[4,2,224,128]{3,2,1,0:T(8,128)(2,1)} %add_convert_fusion), calls=%async_computation.3 | async-start | bytes 917504 | tf_op jit(solution)/shard_map/all_to_all | solution.py:318
  84.7 9.1 %all-to-all-done.3 = bf16[4,2,224,128]{3,2,1,0:T(8,128)(2,1)S(1)} async-done(((bf16[4,2,224,128]{3,2,1,0:T(8,128)(2,1)}), bf16[4,2,224,128]{3,2,1,0:T(8,128)(2,1)S(1)}, u32[]{:S(2)}, u32[]{:S(2)}) %all-to-all-start.3) | async-done | bytes 458784 | tf_op jit(solution)/shard_map/all_to_all | solution.py:318
  93.9 7.4 %collective-permute-start.5 = (bf16[224,128]{1,0:T(8,128)(2,1)S(1)}, bf16[224,128]{1,0:T(8,128)(2,1)S(1)}, u32[]{:S(2)}, u32[]{:S(2)}) collective-permute-start(bf16[224,128]{1,0:T(8,128)(2,1)S(1)} %get-tuple-element.27), channel_id=1, source_target_pairs={{0,2},{2,0},{1,3},{3,1},{4,6},{6,4},{5,7},{7,5},{8,10},{10,8},{9,1... | collective-permute-start | bytes 172040 | tf_op jit(solution)/shard_map/ppermute | solution.py:314
  101.4 10.5 %collective-permute-done.5 = bf16[224,128]{1,0:T(8,128)(2,1)S(1)} collective-permute-done((bf16[224,128]{1,0:T(8,128)(2,1)S(1)}, bf16[224,128]{1,0:T(8,128)(2,1)S(1)}, u32[]{:S(2)}, u32[]{:S(2)}) %collective-permute-start.5) | collective-permute-done | bytes 57376 | tf_op jit(solution)/shard_map/ppermute | solution.py:314
  (9 shorter events, 0.8 us)
Async XLA Ops:
  1.7 31.8 %all-to-all-start = ((bf16[16,8,640]{2,1,0:T(8,128)(2,1)}), bf16[16,8,640]{2,1,0:T(8,128)(2,1)S(1)}, u32[]{:S(2)}, u32[]{:S(2)}) async-start(bf16[16,8,640]{2,1,0:T(8,128)(2,1)} %shard_map.82.after_ref), calls=%async_computation | async-start | bytes 327680 | tf_op jit(solution)/shard_map/all_to_all | solution.py:318
  18.8 33.7 %copy-start.1 = (s32[64]{0:T(128)S(1)}, s32[64]{0:T(128)}, u32[]{:S(2)}) copy-start(s32[64]{0:T(128)} %get-tuple-element.16.spans_ref) | copy-start | bytes 772
  18.8 9.4 %collective-permute-start = (bf16[128,768]{1,0:T(8,128)(2,1)}, bf16[128,768]{1,0:T(8,128)(2,1)S(1)}, u32[]{:S(2)}, u32[]{:S(2)}) collective-permute-start(bf16[128,768]{1,0:T(8,128)(2,1)} %get-tuple-element.17.q0_hbm), channel_id=1, source_target_pairs={{0,16},{16,32},{32,48},{48,0},{1,17},{17,33},{33,49},{49,1},{2,18}... | collective-permute-start | bytes 589832 | tf_op jit(solution)/shard_map/ppermute | solution.py:339
  22.2 7.9 %collective-permute-start.1 = (bf16[128,768]{1,0:T(8,128)(2,1)}, bf16[128,768]{1,0:T(8,128)(2,1)S(1)}, u32[]{:S(2)}, u32[]{:S(2)}) collective-permute-start(bf16[128,768]{1,0:T(8,128)(2,1)} %get-tuple-element.17.q0_hbm), channel_id=1, source_target_pairs={{0,48},{16,0},{32,16},{48,32},{1,49},{17,1},{33,17},{49,33},{2,50}... | collective-permute-start | bytes 589832 | tf_op jit(solution)/shard_map/ppermute | solution.py:339
  34.5 13.7 %all-to-all-start.1 = ((bf16[4,128,640]{2,1,0:T(8,128)(2,1)}), bf16[4,128,640]{2,1,0:T(8,128)(2,1)S(1)}, u32[]{:S(2)}, u32[]{:S(2)}) async-start(bf16[4,128,640]{2,1,0:T(8,128)(2,1)} %broadcast_in_dim.2), calls=%async_computation.1 | async-start | bytes 1310720 | tf_op jit(solution)/shard_map/all_to_all | solution.py:318
  38.9 9.3 %collective-permute-start.2 = (bf16[128,768]{1,0:T(8,128)(2,1)}, bf16[128,768]{1,0:T(8,128)(2,1)S(1)}, u32[]{:S(2)}, u32[]{:S(2)}) collective-permute-start(bf16[128,768]{1,0:T(8,128)(2,1)} %get-tuple-element.17.q0_hbm), channel_id=1, source_target_pairs={{0,32},{16,48},{32,0},{48,16},{1,33},{17,49},{33,1},{49,17},{2,34}... | collective-permute-start | bytes 589832 | tf_op jit(solution)/shard_map/ppermute | solution.py:339
  48.2 26.2 %copy-start = (bf16[512,3584]{1,0:T(8,128)(2,1)S(1)}, bf16[512,3584]{1,0:T(8,128)(2,1)}, u32[]{:S(2)}) copy-start(bf16[512,3584]{1,0:T(8,128)(2,1)} %weight_ref.1) | copy-start | bytes 11010052
  48.2 4.3 %collective-permute-start.3 = (bf16[512,640]{1,0:T(8,128)(2,1)S(1)}, bf16[512,640]{1,0:T(8,128)(2,1)S(1)}, u32[]{:S(2)}, u32[]{:S(2)}) collective-permute-start(bf16[512,640]{1,0:T(8,128)(2,1)S(1)} %bitcast.4), channel_id=1, source_target_pairs={{0,1},{1,0},{2,3},{3,2},{4,5},{5,4},{6,7},{7,6},{8,9},{9,8},{10,11... | collective-permute-start | bytes 1966088 | tf_op jit(solution)/shard_map/ppermute | solution.py:314
  75.3 3.7 %collective-permute-start.4 = (bf16[4,2,224,128]{3,2,1,0:T(8,128)(2,1)S(1)}, bf16[4,2,224,128]{3,2,1,0:T(8,128)(2,1)S(1)}, u32[]{:S(2)}, u32[]{:S(2)}) collective-permute-start(bf16[4,2,224,128]{3,2,1,0:T(8,128)(2,1)S(1)} %get-tuple-element.26), channel_id=1, source_target_pairs={{0,1},{1,0},{2,3},{3,2},{4,5},{5,4},{6,7},{7,6},{8,9},{9,8},{10,11... | collective-permute-start | bytes 1376264 | tf_op jit(solution)/shard_map/ppermute | solution.py:314
  79.9 13.9 %all-to-all-start.3 = ((bf16[4,2,224,128]{3,2,1,0:T(8,128)(2,1)}), bf16[4,2,224,128]{3,2,1,0:T(8,128)(2,1)S(1)}, u32[]{:S(2)}, u32[]{:S(2)}) async-start(bf16[4,2,224,128]{3,2,1,0:T(8,128)(2,1)} %add_convert_fusion), calls=%async_computation.3 | async-start | bytes 917504 | tf_op jit(solution)/shard_map/all_to_all | solution.py:318
  93.9 17.9 %collective-permute-start.5 = (bf16[224,128]{1,0:T(8,128)(2,1)S(1)}, bf16[224,128]{1,0:T(8,128)(2,1)S(1)}, u32[]{:S(2)}, u32[]{:S(2)}) collective-permute-start(bf16[224,128]{1,0:T(8,128)(2,1)S(1)} %get-tuple-element.27), channel_id=1, source_target_pairs={{0,2},{2,0},{1,3},{3,1},{4,6},{6,4},{5,7},{7,5},{8,10},{10,8},{9,1... | collective-permute-start | bytes 172040 | tf_op jit(solution)/shard_map/ppermute | solution.py:314

commit v5 on v4

--- a/solution.py
+++ b/solution.py
@@ -319,7 +319,6 @@
 
 
 def on_device(query_plain, query_rotary, latent_keys, span_order, key_up, value_up, output_weight):
-    zh = lax.axis_index("zh")
     tables = jnp.asarray(rotary_tables())
     sent_keys = pl.pallas_call(
         keys_kernel,
@@ -346,10 +345,8 @@
     parts = attend(kept_spans, query, own, other, turned_value)
     send, keep = project(exchanged(parts, "x"), output_weight)
     both = (keep.astype(jnp.float32) + swapped(send, "c").astype(jnp.float32)).astype(jnp.bfloat16)
-    over_y = exchanged(both, "y").astype(jnp.float32)
-    mine = jnp.sum(lax.dynamic_index_in_dim(over_y, zh, 1, keepdims=False), axis=0)
-    theirs = jnp.sum(lax.dynamic_index_in_dim(over_y, 1 - zh, 1, keepdims=False), axis=0).astype(jnp.bfloat16)
-    return (mine + swapped(theirs, "zh").astype(jnp.float32)).astype(jnp.bfloat16).T
+    pieces = exchanged(both.reshape(NY * NZH, *both.shape[2:]), ("y", "zh"))
+    return jnp.sum(pieces.astype(jnp.float32), axis=0).astype(jnp.bfloat16).T
 
 
 def solution(mesh):

time: 113 us -> 123 us (1.088)
  blocking collectives: 14.4 us -> 57 us
  waiting for transfers between devices: 33.4 us -> 13.9 us
  starting transfers between devices: 47.9 us -> 35.7 us
    all_to_all x1 -> x2, blocking collectives: 14.4 us -> 57 us  [exchanged(): return lax.all_to_all(value, axis, split_axis=0, concat_axis=0, tiled=True)]
    ppermute x3 -> x2, waiting for transfers between devices: 12.2 us -> 1.78 us  [swapped(): return lax.ppermute(value, axis, [(0, 1), (1, 0)])]
    all_to_all x3 -> x2, waiting for transfers between devices: 12.6 us -> 3.48 us  [exchanged(): return lax.all_to_all(value, axis, split_axis=0, concat_axis=0, tiled=True)]
    ppermute x3 -> x2, starting transfers between devices: 11.5 us -> 4.09 us  [swapped(): return lax.ppermute(value, axis, [(0, 1), (1, 0)])]
    all_to_all x3 -> x2, starting transfers between devices: 24.5 us -> 19.7 us  [exchanged(): return lax.all_to_all(value, axis, split_axis=0, concat_axis=0, tiled=True)]
  transfers between devices with their start and end apart: 9 -> 7, of which waited for: 7 -> 5; matrix products, arithmetic and copies ran while one was open for 0% -> 0% of each run, Pallas kernels for 3% -> 3%
where the time goes in v5:
time: 123 us; the launch traced here: 122 us
  blocking collectives  57 us (46%)
  starting transfers between devices  35.7 us (29%)
  Pallas kernels  14 us (11%)
  waiting for transfers between devices  13.9 us (11%)
    all_to_all x2, blocking collectives, exchanged(): return lax.all_to_all(value, axis, split_axis=0, concat_axis=0, tiled=True)  57 us
    all_to_all x2, starting transfers between devices, exchanged(): return lax.all_to_all(value, axis, split_axis=0, concat_axis=0, tiled=True)  19.7 us
    ppermute x3, starting transfers between devices, on_device(): lax.ppermute(queries, 'x', [(i, (i + k) % NX) for i in range(NX)])  12 us
    ppermute x3, waiting for transfers between devices, on_device(): lax.ppermute(queries, 'x', [(i, (i + k) % NX) for i in range(NX)])  8.58 us
    pallas_call x1, Pallas kernels, attend(): pl.pallas_call(attend_kernel, out_shape=jax.ShapeDtypeStruct((NX, PARTROW...  7.49 us
    ppermute x2, starting transfers between devices, swapped(): return lax.ppermute(value, axis, [(0, 1), (1, 0)])  4.09 us
    all_to_all x2, waiting for transfers between devices, exchanged(): return lax.all_to_all(value, axis, split_axis=0, concat_axis=0, tiled=True)  3.48 us
  transfers between devices with their start and end apart: 7, of which 5 were waited for; matrix products, arithmetic and copies ran while one was open for 0% of the time, Pallas kernels for 3%

profile of v5, /device:TPU:32, one launch (start us, length us, event | category | flops | bytes accessed | tf_op | source)
XLA Modules:
  0.0 122.4 jit_solution(13233676797912822170)
XLA Ops:
  0.0 1.7 %shard_map.82.after_ref = bf16[16,8,640]{2,1,0:T(8,128)(2,1)} custom-call(s32[64]{0:T(128)} %spans_ref.3, bf16[8,576]{1,0:T(8,128)(2,1)} %keys_ref.1, f32[4,64,128]{2,1,0:T(8,128)} %constant.5.clone.tables_ref), custom_call_target="tpu_custom_call" | custom-call | tf_op jit(solution)/shard_map/pallas_call | solution.py:323
  1.7 15.2 %all-to-all-start = ((bf16[16,8,640]{2,1,0:T(8,128)(2,1)}), bf16[16,8,640]{2,1,0:T(8,128)(2,1)S(1)}, u32[]{:S(2)}, u32[]{:S(2)}) async-start(bf16[16,8,640]{2,1,0:T(8,128)(2,1)} %shard_map.82.after_ref), calls=%async_computation | async-start | bytes 327680 | tf_op jit(solution)/shard_map/all_to_all | solution.py:318
  16.9 1.8 %shard_map.83 = (bf16[128,768]{1,0:T(8,128)(2,1)}, s32[64]{0:T(128)}) custom-call(s32[64]{0:T(128)} %spans_ref.3, bf16[128,512]{1,0:T(8,128)(2,1)} %plain_ref.1, bf16[128,256]{1,0:T(8,128)(2,1)} %rotary_ref.1, f32[4,64,128]{2,1,0:T(8,128)} %constant.5.clone.tables_ref, bf16[16,8,640]{2,1,0:T(8,128)(2,1)} %shard_map.82.after_ref), custom_call_target="tpu_custom_call" | custom-call | tf_op jit(solution)/shard_map/pallas_call | solution.py:330
  18.8 0.0 copy-start.1
  18.8 3.4 %collective-permute-start = (bf16[128,768]{1,0:T(8,128)(2,1)}, bf16[128,768]{1,0:T(8,128)(2,1)S(1)}, u32[]{:S(2)}, u32[]{:S(2)}) collective-permute-start(bf16[128,768]{1,0:T(8,128)(2,1)} %get-tuple-element.17.q0_hbm), channel_id=1, source_target_pairs={{0,16},{16,32},{32,48},{48,0},{1,17},{17,33},{33,49},{49,1},{2,18}... | collective-permute-start | bytes 589832 | tf_op jit(solution)/shard_map/ppermute | solution.py:338
  22.2 3.7 %collective-permute-start.1 = (bf16[128,768]{1,0:T(8,128)(2,1)}, bf16[128,768]{1,0:T(8,128)(2,1)S(1)}, u32[]{:S(2)}, u32[]{:S(2)}) collective-permute-start(bf16[128,768]{1,0:T(8,128)(2,1)} %get-tuple-element.17.q0_hbm), channel_id=1, source_target_pairs={{0,48},{16,0},{32,16},{48,32},{1,49},{17,1},{33,17},{49,33},{2,50}... | collective-permute-start | bytes 589832 | tf_op jit(solution)/shard_map/ppermute | solution.py:338
  25.8 2.3 %collective-permute-done.q1 = bf16[128,768]{1,0:T(8,128)(2,1)S(1)} collective-permute-done((bf16[128,768]{1,0:T(8,128)(2,1)}, bf16[128,768]{1,0:T(8,128)(2,1)S(1)}, u32[]{:S(2)}, u32[]{:S(2)}) %collective-permute-start) | collective-permute-done | bytes 196640 | tf_op jit(solution)/shard_map/ppermute | solution.py:338
  28.2 1.9 %collective-permute-done.1.q3 = bf16[128,768]{1,0:T(8,128)(2,1)S(1)} collective-permute-done((bf16[128,768]{1,0:T(8,128)(2,1)}, bf16[128,768]{1,0:T(8,128)(2,1)S(1)}, u32[]{:S(2)}, u32[]{:S(2)}) %collective-permute-start.1) | collective-permute-done | bytes 196640 | tf_op jit(solution)/shard_map/ppermute | solution.py:338
  30.1 3.5 %all-to-all-done = bf16[16,8,640]{2,1,0:T(8,128)(2,1)S(1)} async-done(((bf16[16,8,640]{2,1,0:T(8,128)(2,1)}), bf16[16,8,640]{2,1,0:T(8,128)(2,1)S(1)}, u32[]{:S(2)}, u32[]{:S(2)}) %all-to-all-start) | async-done | bytes 163872 | tf_op jit(solution)/shard_map/all_to_all | solution.py:318
  33.6 0.9 broadcast_in_dim.2
  34.5 4.5 %all-to-all-start.1 = ((bf16[4,128,640]{2,1,0:T(8,128)(2,1)}), bf16[4,128,640]{2,1,0:T(8,128)(2,1)S(1)}, u32[]{:S(2)}, u32[]{:S(2)}) async-start(bf16[4,128,640]{2,1,0:T(8,128)(2,1)} %broadcast_in_dim.2), calls=%async_computation.1 | async-start | bytes 1310720 | tf_op jit(solution)/shard_map/all_to_all | solution.py:318
  38.9 4.9 %collective-permute-start.2 = (bf16[128,768]{1,0:T(8,128)(2,1)}, bf16[128,768]{1,0:T(8,128)(2,1)S(1)}, u32[]{:S(2)}, u32[]{:S(2)}) collective-permute-start(bf16[128,768]{1,0:T(8,128)(2,1)} %get-tuple-element.17.q0_hbm), channel_id=1, source_target_pairs={{0,32},{16,48},{32,0},{48,16},{1,33},{17,49},{33,1},{49,17},{2,34}... | collective-permute-start | bytes 589832 | tf_op jit(solution)/shard_map/ppermute | solution.py:338
  43.9 4.3 %collective-permute-done.2.q2 = bf16[128,768]{1,0:T(8,128)(2,1)S(1)} collective-permute-done((bf16[128,768]{1,0:T(8,128)(2,1)}, bf16[128,768]{1,0:T(8,128)(2,1)S(1)}, u32[]{:S(2)}, u32[]{:S(2)}) %collective-permute-start.2) | collective-permute-done | bytes 196640 | tf_op jit(solution)/shard_map/ppermute | solution.py:338
  48.2 0.0 all-to-all-done.1
  48.2 2.2 %collective-permute-start.3 = (bf16[512,640]{1,0:T(8,128)(2,1)S(1)}, bf16[512,640]{1,0:T(8,128)(2,1)S(1)}, u32[]{:S(2)}, u32[]{:S(2)}) collective-permute-start(bf16[512,640]{1,0:T(8,128)(2,1)S(1)} %bitcast.4), channel_id=1, source_target_pairs={{0,1},{1,0},{2,3},{3,2},{4,5},{5,4},{6,7},{7,6},{8,9},{9,8},{10,11... | collective-permute-start | bytes 1966088 | tf_op jit(solution)/shard_map/ppermute | solution.py:314
  50.4 2.1 %shard_map.84 = (bf16[8,256,576]{2,1,0:T(8,128)(2,1)S(1)}, bf16[4,128,512]{2,1,0:T(8,128)(2,1)S(1)}) custom-call(bf16[128,768]{1,0:T(8,128)(2,1)} %get-tuple-element.17.q0_hbm, bf16[128,768]{1,0:T(8,128)(2,1)S(1)} %collective-permute-done.q1, bf16[128,768]{1,0:T(8,128)(2,1)S(1)} %collective-permute-done.2.q2, ...), custom_call_target="tpu_custom_call" | custom-call | tf_op jit(solution)/shard_map/pallas_call | solution.py:128
  52.5 7.5 %shard_map.85 = bf16[4,528,128]{2,1,0:T(8,128)(2,1)S(1)} custom-call(s32[64]{0:T(128)S(1)} %copy-done.1, bf16[8,256,576]{2,1,0:T(8,128)(2,1)S(1)} %get-tuple-element.22.query, bf16[512,640]{1,0:T(8,128)(2,1)S(1)} %bitcast.5, bf16[512,640]{1,0:T(8,128)(2,1)S(1)} %collective-permute-done.3.other_ref, bf16[4,128,512]{2,1,0:T(8,128)(2,1)S(1)} %get-tuple-element.24.value_ref), custom_call_target="tpu_custom_call" | custom-call | tf_op jit(solution)/shard_map/pallas_call | solution.py:255
  60.0 14.4 %all_to_all.20.parts_ref = bf16[4,528,128]{2,1,0:T(8,128)(2,1)S(1)} all-to-all(bf16[4,528,128]{2,1,0:T(8,128)(2,1)S(1)} %shard_map.85), channel_id=1, replica_groups=mesh['zl'=8,'x'=4,'y'=4,'zh'=2,'c'=2] {'x'}, dimensions={0} | all-to-all | bytes 1081344 | tf_op jit(solution)/shard_map/all_to_all | solution.py:318
  74.4 0.9 shard_map.86
  75.3 1.9 %collective-permute-start.4 = (bf16[4,2,224,128]{3,2,1,0:T(8,128)(2,1)S(1)}, bf16[4,2,224,128]{3,2,1,0:T(8,128)(2,1)S(1)}, u32[]{:S(2)}, u32[]{:S(2)}) collective-permute-start(bf16[4,2,224,128]{3,2,1,0:T(8,128)(2,1)S(1)} %get-tuple-element.26), channel_id=1, source_target_pairs={{0,1},{1,0},{2,3},{3,2},{4,5},{5,4},{6,7},{7,6},{8,9},{9,8},{10,11... | collective-permute-start | bytes 1376264 | tf_op jit(solution)/shard_map/ppermute | solution.py:314
  77.2 1.8 %collective-permute-done.4 = bf16[4,2,224,128]{3,2,1,0:T(8,128)(2,1)S(1)} collective-permute-done((bf16[4,2,224,128]{3,2,1,0:T(8,128)(2,1)S(1)}, bf16[4,2,224,128]{3,2,1,0:T(8,128)(2,1)S(1)}, u32[]{:S(2)}, u32[]{:S(2)}) %collective-permute-start.4) | collective-permute-done | bytes 458784 | tf_op jit(solution)/shard_map/ppermute | solution.py:314
  79.0 0.1 add_convert_fusion
  79.1 42.6 %all_to_all.21 = bf16[8,224,128]{2,1,0:T(8,128)(2,1)S(1)} all-to-all(bf16[8,224,128]{2,1,0:T(8,128)(2,1)S(1)} %bitcast.6), channel_id=1, replica_groups=mesh['zl'=8,'x'=4,'y'=4,'zh'=2,'c'=2] {'y','zh'}, dimensions={0} | all-to-all | bytes 917504 | tf_op jit(solution)/shard_map/all_to_all | solution.py:318
  121.7 0.7 reduce_sum.12
  (4 shorter events, 0.0 us)
Async XLA Ops:
  1.7 31.8 %all-to-all-start = ((bf16[16,8,640]{2,1,0:T(8,128)(2,1)}), bf16[16,8,640]{2,1,0:T(8,128)(2,1)S(1)}, u32[]{:S(2)}, u32[]{:S(2)}) async-start(bf16[16,8,640]{2,1,0:T(8,128)(2,1)} %shard_map.82.after_ref), calls=%async_computation | async-start | bytes 327680 | tf_op jit(solution)/shard_map/all_to_all | solution.py:318
  18.8 33.7 %copy-start.1 = (s32[64]{0:T(128)S(1)}, s32[64]{0:T(128)}, u32[]{:S(2)}) copy-start(s32[64]{0:T(128)} %get-tuple-element.16.spans_ref) | copy-start | bytes 772
  18.8 9.4 %collective-permute-start = (bf16[128,768]{1,0:T(8,128)(2,1)}, bf16[128,768]{1,0:T(8,128)(2,1)S(1)}, u32[]{:S(2)}, u32[]{:S(2)}) collective-permute-start(bf16[128,768]{1,0:T(8,128)(2,1)} %get-tuple-element.17.q0_hbm), channel_id=1, source_target_pairs={{0,16},{16,32},{32,48},{48,0},{1,17},{17,33},{33,49},{49,1},{2,18}... | collective-permute-start | bytes 589832 | tf_op jit(solution)/shard_map/ppermute | solution.py:338
  22.2 7.9 %collective-permute-start.1 = (bf16[128,768]{1,0:T(8,128)(2,1)}, bf16[128,768]{1,0:T(8,128)(2,1)S(1)}, u32[]{:S(2)}, u32[]{:S(2)}) collective-permute-start(bf16[128,768]{1,0:T(8,128)(2,1)} %get-tuple-element.17.q0_hbm), channel_id=1, source_target_pairs={{0,48},{16,0},{32,16},{48,32},{1,49},{17,1},{33,17},{49,33},{2,50}... | collective-permute-start | bytes 589832 | tf_op jit(solution)/shard_map/ppermute | solution.py:338
  34.5 13.7 %all-to-all-start.1 = ((bf16[4,128,640]{2,1,0:T(8,128)(2,1)}), bf16[4,128,640]{2,1,0:T(8,128)(2,1)S(1)}, u32[]{:S(2)}, u32[]{:S(2)}) async-start(bf16[4,128,640]{2,1,0:T(8,128)(2,1)} %broadcast_in_dim.2), calls=%async_computation.1 | async-start | bytes 1310720 | tf_op jit(solution)/shard_map/all_to_all | solution.py:318
  38.9 9.3 %collective-permute-start.2 = (bf16[128,768]{1,0:T(8,128)(2,1)}, bf16[128,768]{1,0:T(8,128)(2,1)S(1)}, u32[]{:S(2)}, u32[]{:S(2)}) collective-permute-start(bf16[128,768]{1,0:T(8,128)(2,1)} %get-tuple-element.17.q0_hbm), channel_id=1, source_target_pairs={{0,32},{16,48},{32,0},{48,16},{1,33},{17,49},{33,1},{49,17},{2,34}... | collective-permute-start | bytes 589832 | tf_op jit(solution)/shard_map/ppermute | solution.py:338
  48.2 26.2 %copy-start = (bf16[512,3584]{1,0:T(8,128)(2,1)S(1)}, bf16[512,3584]{1,0:T(8,128)(2,1)}, u32[]{:S(2)}) copy-start(bf16[512,3584]{1,0:T(8,128)(2,1)} %weight_ref.1) | copy-start | bytes 11010052
  48.2 4.3 %collective-permute-start.3 = (bf16[512,640]{1,0:T(8,128)(2,1)S(1)}, bf16[512,640]{1,0:T(8,128)(2,1)S(1)}, u32[]{:S(2)}, u32[]{:S(2)}) collective-permute-start(bf16[512,640]{1,0:T(8,128)(2,1)S(1)} %bitcast.4), channel_id=1, source_target_pairs={{0,1},{1,0},{2,3},{3,2},{4,5},{5,4},{6,7},{7,6},{8,9},{9,8},{10,11... | collective-permute-start | bytes 1966088 | tf_op jit(solution)/shard_map/ppermute | solution.py:314
  75.3 3.7 %collective-permute-start.4 = (bf16[4,2,224,128]{3,2,1,0:T(8,128)(2,1)S(1)}, bf16[4,2,224,128]{3,2,1,0:T(8,128)(2,1)S(1)}, u32[]{:S(2)}, u32[]{:S(2)}) collective-permute-start(bf16[4,2,224,128]{3,2,1,0:T(8,128)(2,1)S(1)} %get-tuple-element.26), channel_id=1, source_target_pairs={{0,1},{1,0},{2,3},{3,2},{4,5},{5,4},{6,7},{7,6},{8,9},{9,8},{10,11... | collective-permute-start | bytes 1376264 | tf_op jit(solution)/shard_map/ppermute | solution.py:314

commit v6 on v4

--- a/solution.py
+++ b/solution.py
@@ -310,6 +310,10 @@
     )(parts, weight)
 
 
+def shifted(value, by):
+    return lax.ppermute(value, "x", [(i, (i + by) % NX) for i in range(NX)])
+
+
 def swapped(value, axis):
     return lax.ppermute(value, axis, [(0, 1), (1, 0)])
 
@@ -335,10 +339,9 @@
         out_specs=(WHOLE, SMEM),
     )(span_order, query_plain, query_rotary, tables, sent_keys)
     along_z = exchanged(sent_keys, ("zl", "zh")).reshape(GROUP * 8, ROWW)
-    blocks = [queries] + [
-        lax.ppermute(queries, "x", [(i, (i + k) % NX) for i in range(NX)]) for k in range(1, NX)
-    ]
+    blocks = [queries, shifted(queries, 1), None, shifted(queries, NX - 1)]
     along_z, blocks[1], blocks[3] = lax.optimization_barrier((along_z, blocks[1], blocks[3]))
+    blocks[2] = shifted(blocks[1], 1)
     own = exchanged(jnp.broadcast_to(along_z[None], (NY, GROUP * 8, ROWW)), "y").reshape(NY * GROUP * 8, ROWW)
     own, blocks[2] = lax.optimization_barrier((own, blocks[2]))
     other = swapped(own, "c")

time: 113 us -> 109 us (0.965)
  starting transfers between devices: 47.9 us -> 46 us
  waiting for transfers between devices: 33.4 us -> 31.9 us
    ppermute x3, waiting for transfers between devices: 12.2 us -> 9.59 us  [swapped(): return lax.ppermute(value, axis, [(0, 1), (1, 0)])]
    ppermute x3, starting transfers between devices: 12 us -> 10.4 us  [shifted(): return lax.ppermute(value, 'x', [(i, (i + by) % NX) for i in range(NX)])]
    all_to_all x3, starting transfers between devices: 24.5 us -> 23.2 us  [exchanged(): return lax.all_to_all(value, axis, split_axis=0, concat_axis=0, tiled=True)]
  transfers between devices with their start and end apart: 9 -> 9, of which waited for: 7 -> 7; matrix products, arithmetic and copies ran while one was open for 0% -> 0% of each run, Pallas kernels for 3% -> 4%
where the time goes in v6:
time: 109 us
  starting transfers between devices  46 us (42%)
  waiting for transfers between devices  31.9 us (29%)
  blocking collectives  14.2 us (13%)
  Pallas kernels  14 us (13%)
  other arithmetic  1.66 us (2%)
    all_to_all x3, starting transfers between devices, exchanged(): return lax.all_to_all(value, axis, split_axis=0, concat_axis=0, tiled=True)  23.2 us
    all_to_all x1, blocking collectives, exchanged(): return lax.all_to_all(value, axis, split_axis=0, concat_axis=0, tiled=True)  14.2 us
    all_to_all x3, waiting for transfers between devices, exchanged(): return lax.all_to_all(value, axis, split_axis=0, concat_axis=0, tiled=True)  12.7 us
    ppermute x3, starting transfers between devices, swapped(): return lax.ppermute(value, axis, [(0, 1), (1, 0)])  12.3 us
    ppermute x3, starting transfers between devices, shifted(): return lax.ppermute(value, 'x', [(i, (i + by) % NX) for i in range(NX)])  10.4 us
    ppermute x3, waiting for transfers between devices, shifted(): return lax.ppermute(value, 'x', [(i, (i + by) % NX) for i in range(NX)])  9.61 us
    ppermute x3, waiting for transfers between devices, swapped(): return lax.ppermute(value, axis, [(0, 1), (1, 0)])  9.59 us
    pallas_call x1, Pallas kernels, attend(): pl.pallas_call(attend_kernel, out_shape=jax.ShapeDtypeStruct((NX, PARTROW...  7.48 us
  transfers between devices with their start and end apart: 9, of which 7 were waited for; matrix products, arithmetic and copies ran while one was open for 0% of the time, Pallas kernels for 4%

profile of v6, /device:TPU:32, one launch (start us, length us, event | category | flops | bytes accessed | tf_op | source)
XLA Modules:
  0.0 108.8 jit_solution(16956535810517680652)
XLA Ops:
  0.0 1.7 %shard_map.82.after_ref = bf16[16,8,640]{2,1,0:T(8,128)(2,1)} custom-call(s32[64]{0:T(128)} %spans_ref.3, bf16[8,576]{1,0:T(8,128)(2,1)} %keys_ref.1, f32[4,64,128]{2,1,0:T(8,128)} %constant.20.clone.tables_ref), custom_call_target="tpu_custom_call" | custom-call | tf_op jit(solution)/shard_map/pallas_call | solution.py:328
  1.7 15.2 %all-to-all-start = ((bf16[16,8,640]{2,1,0:T(8,128)(2,1)}), bf16[16,8,640]{2,1,0:T(8,128)(2,1)S(1)}, u32[]{:S(2)}, u32[]{:S(2)}) async-start(bf16[16,8,640]{2,1,0:T(8,128)(2,1)} %shard_map.82.after_ref), calls=%async_computation | async-start | bytes 327680 | tf_op jit(solution)/shard_map/all_to_all | solution.py:322
  17.0 1.8 %shard_map.83 = (bf16[128,768]{1,0:T(8,128)(2,1)}, s32[64]{0:T(128)}) custom-call(s32[64]{0:T(128)} %spans_ref.3, bf16[128,512]{1,0:T(8,128)(2,1)} %plain_ref.1, bf16[128,256]{1,0:T(8,128)(2,1)} %rotary_ref.1, f32[4,64,128]{2,1,0:T(8,128)} %constant.20.clone.tables_ref, bf16[16,8,640]{2,1,0:T(8,128)(2,1)} %shard_map.82.after_ref), custom_call_target="tpu_custom_call" | custom-call | tf_op jit(solution)/shard_map/pallas_call | solution.py:335
  18.8 3.4 %collective-permute-start = (bf16[128,768]{1,0:T(8,128)(2,1)}, bf16[128,768]{1,0:T(8,128)(2,1)S(1)}, u32[]{:S(2)}, u32[]{:S(2)}) collective-permute-start(bf16[128,768]{1,0:T(8,128)(2,1)} %get-tuple-element.17.q0_hbm), channel_id=1, source_target_pairs={{0,16},{16,32},{32,48},{48,0},{1,17},{17,33},{33,49},{49,1},{2,18}... | collective-permute-start | bytes 589832 | tf_op jit(solution)/shard_map/ppermute | solution.py:314
  22.2 3.7 %collective-permute-start.1 = (bf16[128,768]{1,0:T(8,128)(2,1)}, bf16[128,768]{1,0:T(8,128)(2,1)S(1)}, u32[]{:S(2)}, u32[]{:S(2)}) collective-permute-start(bf16[128,768]{1,0:T(8,128)(2,1)} %get-tuple-element.17.q0_hbm), channel_id=1, source_target_pairs={{0,48},{16,0},{32,16},{48,32},{1,49},{17,1},{33,17},{49,33},{2,50}... | collective-permute-start | bytes 589832 | tf_op jit(solution)/shard_map/ppermute | solution.py:314
  25.9 2.3 %collective-permute-done.q1 = bf16[128,768]{1,0:T(8,128)(2,1)S(1)} collective-permute-done((bf16[128,768]{1,0:T(8,128)(2,1)}, bf16[128,768]{1,0:T(8,128)(2,1)S(1)}, u32[]{:S(2)}, u32[]{:S(2)}) %collective-permute-start) | collective-permute-done | bytes 196640 | tf_op jit(solution)/shard_map/ppermute | solution.py:314
  28.2 1.9 %collective-permute-done.1.q3 = bf16[128,768]{1,0:T(8,128)(2,1)S(1)} collective-permute-done((bf16[128,768]{1,0:T(8,128)(2,1)}, bf16[128,768]{1,0:T(8,128)(2,1)S(1)}, u32[]{:S(2)}, u32[]{:S(2)}) %collective-permute-start.1) | collective-permute-done | bytes 196640 | tf_op jit(solution)/shard_map/ppermute | solution.py:314
  30.1 3.5 %all-to-all-done = bf16[16,8,640]{2,1,0:T(8,128)(2,1)S(1)} async-done(((bf16[16,8,640]{2,1,0:T(8,128)(2,1)}), bf16[16,8,640]{2,1,0:T(8,128)(2,1)S(1)}, u32[]{:S(2)}, u32[]{:S(2)}) %all-to-all-start) | async-done | bytes 163872 | tf_op jit(solution)/shard_map/all_to_all | solution.py:322
  33.6 0.9 broadcast_in_dim.2
  34.5 4.5 %all-to-all-start.1 = ((bf16[4,128,640]{2,1,0:T(8,128)(2,1)}), bf16[4,128,640]{2,1,0:T(8,128)(2,1)S(1)}, u32[]{:S(2)}, u32[]{:S(2)}) async-start(bf16[4,128,640]{2,1,0:T(8,128)(2,1)} %broadcast_in_dim.2), calls=%async_computation.1 | async-start | bytes 1310720 | tf_op jit(solution)/shard_map/all_to_all | solution.py:322
  38.9 3.4 %collective-permute-start.2 = (bf16[128,768]{1,0:T(8,128)(2,1)S(1)}, bf16[128,768]{1,0:T(8,128)(2,1)S(1)}, u32[]{:S(2)}, u32[]{:S(2)}) collective-permute-start(bf16[128,768]{1,0:T(8,128)(2,1)S(1)} %collective-permute-done.q1), channel_id=1, source_target_pairs={{0,16},{16,32},{32,48},{48,0},{1,17},{17,33},{33,49},{49,1},{2,18}... | collective-permute-start | bytes 589832 | tf_op jit(solution)/shard_map/ppermute | solution.py:314
  42.3 5.4 %collective-permute-done.2.q2 = bf16[128,768]{1,0:T(8,128)(2,1)S(1)} collective-permute-done((bf16[128,768]{1,0:T(8,128)(2,1)S(1)}, bf16[128,768]{1,0:T(8,128)(2,1)S(1)}, u32[]{:S(2)}, u32[]{:S(2)}) %collective-permute-start.2) | collective-permute-done | bytes 196640 | tf_op jit(solution)/shard_map/ppermute | solution.py:314
  47.7 2.2 %collective-permute-start.3 = (bf16[512,640]{1,0:T(8,128)(2,1)S(1)}, bf16[512,640]{1,0:T(8,128)(2,1)S(1)}, u32[]{:S(2)}, u32[]{:S(2)}) collective-permute-start(bf16[512,640]{1,0:T(8,128)(2,1)S(1)} %bitcast.4), channel_id=1, source_target_pairs={{0,1},{1,0},{2,3},{3,2},{4,5},{5,4},{6,7},{7,6},{8,9},{9,8},{10,11... | collective-permute-start | bytes 1966088 | tf_op jit(solution)/shard_map/ppermute | solution.py:318
  49.9 2.1 %shard_map.84 = (bf16[8,256,576]{2,1,0:T(8,128)(2,1)S(1)}, bf16[4,128,512]{2,1,0:T(8,128)(2,1)S(1)}) custom-call(bf16[128,768]{1,0:T(8,128)(2,1)} %get-tuple-element.17.q0_hbm, bf16[128,768]{1,0:T(8,128)(2,1)S(1)} %collective-permute-done.q1, bf16[128,768]{1,0:T(8,128)(2,1)S(1)} %collective-permute-done.2.q2, ...), custom_call_target="tpu_custom_call" | custom-call | tf_op jit(solution)/shard_map/pallas_call | solution.py:128
  52.0 7.5 %shard_map.85 = bf16[4,528,128]{2,1,0:T(8,128)(2,1)S(1)} custom-call(s32[64]{0:T(128)S(1)} %copy-done.1, bf16[8,256,576]{2,1,0:T(8,128)(2,1)S(1)} %get-tuple-element.22.query, bf16[512,640]{1,0:T(8,128)(2,1)S(1)} %bitcast.5, bf16[512,640]{1,0:T(8,128)(2,1)S(1)} %collective-permute-done.3.other_ref, bf16[4,128,512]{2,1,0:T(8,128)(2,1)S(1)} %get-tuple-element.24.value_ref), custom_call_target="tpu_custom_call" | custom-call | tf_op jit(solution)/shard_map/pallas_call | solution.py:255
  59.5 14.2 %all_to_all.20.parts_ref = bf16[4,528,128]{2,1,0:T(8,128)(2,1)S(1)} all-to-all(bf16[4,528,128]{2,1,0:T(8,128)(2,1)S(1)} %shard_map.85), channel_id=1, replica_groups=mesh['zl'=8,'x'=4,'y'=4,'zh'=2,'c'=2] {'x'}, dimensions={0} | all-to-all | bytes 1081344 | tf_op jit(solution)/shard_map/all_to_all | solution.py:322
  73.7 0.9 shard_map.86
  74.6 1.9 %collective-permute-start.4 = (bf16[4,2,224,128]{3,2,1,0:T(8,128)(2,1)S(1)}, bf16[4,2,224,128]{3,2,1,0:T(8,128)(2,1)S(1)}, u32[]{:S(2)}, u32[]{:S(2)}) collective-permute-start(bf16[4,2,224,128]{3,2,1,0:T(8,128)(2,1)S(1)} %get-tuple-element.26), channel_id=1, source_target_pairs={{0,1},{1,0},{2,3},{3,2},{4,5},{5,4},{6,7},{7,6},{8,9},{9,8},{10,11... | collective-permute-start | bytes 1376264 | tf_op jit(solution)/shard_map/ppermute | solution.py:318
  76.5 1.8 %collective-permute-done.4 = bf16[4,2,224,128]{3,2,1,0:T(8,128)(2,1)S(1)} collective-permute-done((bf16[4,2,224,128]{3,2,1,0:T(8,128)(2,1)S(1)}, bf16[4,2,224,128]{3,2,1,0:T(8,128)(2,1)S(1)}, u32[]{:S(2)}, u32[]{:S(2)}) %collective-permute-start.4) | collective-permute-done | bytes 458784 | tf_op jit(solution)/shard_map/ppermute | solution.py:318
  78.3 0.9 add_convert_fusion
  79.2 3.6 %all-to-all-start.3 = ((bf16[4,2,224,128]{3,2,1,0:T(8,128)(2,1)}), bf16[4,2,224,128]{3,2,1,0:T(8,128)(2,1)S(1)}, u32[]{:S(2)}, u32[]{:S(2)}) async-start(bf16[4,2,224,128]{3,2,1,0:T(8,128)(2,1)} %add_convert_fusion), calls=%async_computation.3 | async-start | bytes 917504 | tf_op jit(solution)/shard_map/all_to_all | solution.py:322
  82.8 9.2 %all-to-all-done.3 = bf16[4,2,224,128]{3,2,1,0:T(8,128)(2,1)S(1)} async-done(((bf16[4,2,224,128]{3,2,1,0:T(8,128)(2,1)}), bf16[4,2,224,128]{3,2,1,0:T(8,128)(2,1)S(1)}, u32[]{:S(2)}, u32[]{:S(2)}) %all-to-all-start.3) | async-done | bytes 458784 | tf_op jit(solution)/shard_map/all_to_all | solution.py:322
  92.1 8.2 %collective-permute-start.5 = (bf16[224,128]{1,0:T(8,128)(2,1)S(1)}, bf16[224,128]{1,0:T(8,128)(2,1)S(1)}, u32[]{:S(2)}, u32[]{:S(2)}) collective-permute-start(bf16[224,128]{1,0:T(8,128)(2,1)S(1)} %get-tuple-element.27), channel_id=1, source_target_pairs={{0,2},{2,0},{1,3},{3,1},{4,6},{6,4},{5,7},{7,5},{8,10},{10,8},{9,1... | collective-permute-start | bytes 172040 | tf_op jit(solution)/shard_map/ppermute | solution.py:318
  100.3 7.8 %collective-permute-done.5 = bf16[224,128]{1,0:T(8,128)(2,1)S(1)} collective-permute-done((bf16[224,128]{1,0:T(8,128)(2,1)S(1)}, bf16[224,128]{1,0:T(8,128)(2,1)S(1)}, u32[]{:S(2)}, u32[]{:S(2)}) %collective-permute-start.5) | collective-permute-done | bytes 57376 | tf_op jit(solution)/shard_map/ppermute | solution.py:318
  (9 shorter events, 0.8 us)
Async XLA Ops:
  1.7 31.8 %all-to-all-start = ((bf16[16,8,640]{2,1,0:T(8,128)(2,1)}), bf16[16,8,640]{2,1,0:T(8,128)(2,1)S(1)}, u32[]{:S(2)}, u32[]{:S(2)}) async-start(bf16[16,8,640]{2,1,0:T(8,128)(2,1)} %shard_map.82.after_ref), calls=%async_computation | async-start | bytes 327680 | tf_op jit(solution)/shard_map/all_to_all | solution.py:322
  18.8 33.2 %copy-start.1 = (s32[64]{0:T(128)S(1)}, s32[64]{0:T(128)}, u32[]{:S(2)}) copy-start(s32[64]{0:T(128)} %get-tuple-element.16.spans_ref) | copy-start | bytes 772
  18.8 9.4 %collective-permute-start = (bf16[128,768]{1,0:T(8,128)(2,1)}, bf16[128,768]{1,0:T(8,128)(2,1)S(1)}, u32[]{:S(2)}, u32[]{:S(2)}) collective-permute-start(bf16[128,768]{1,0:T(8,128)(2,1)} %get-tuple-element.17.q0_hbm), channel_id=1, source_target_pairs={{0,16},{16,32},{32,48},{48,0},{1,17},{17,33},{33,49},{49,1},{2,18}... | collective-permute-start | bytes 589832 | tf_op jit(solution)/shard_map/ppermute | solution.py:314
  22.2 7.9 %collective-permute-start.1 = (bf16[128,768]{1,0:T(8,128)(2,1)}, bf16[128,768]{1,0:T(8,128)(2,1)S(1)}, u32[]{:S(2)}, u32[]{:S(2)}) collective-permute-start(bf16[128,768]{1,0:T(8,128)(2,1)} %get-tuple-element.17.q0_hbm), channel_id=1, source_target_pairs={{0,48},{16,0},{32,16},{48,32},{1,49},{17,1},{33,17},{49,33},{2,50}... | collective-permute-start | bytes 589832 | tf_op jit(solution)/shard_map/ppermute | solution.py:314
  34.5 13.2 %all-to-all-start.1 = ((bf16[4,128,640]{2,1,0:T(8,128)(2,1)}), bf16[4,128,640]{2,1,0:T(8,128)(2,1)S(1)}, u32[]{:S(2)}, u32[]{:S(2)}) async-start(bf16[4,128,640]{2,1,0:T(8,128)(2,1)} %broadcast_in_dim.2), calls=%async_computation.1 | async-start | bytes 1310720 | tf_op jit(solution)/shard_map/all_to_all | solution.py:322
  38.9 8.8 %collective-permute-start.2 = (bf16[128,768]{1,0:T(8,128)(2,1)S(1)}, bf16[128,768]{1,0:T(8,128)(2,1)S(1)}, u32[]{:S(2)}, u32[]{:S(2)}) collective-permute-start(bf16[128,768]{1,0:T(8,128)(2,1)S(1)} %collective-permute-done.q1), channel_id=1, source_target_pairs={{0,16},{16,32},{32,48},{48,0},{1,17},{17,33},{33,49},{49,1},{2,18}... | collective-permute-start | bytes 589832 | tf_op jit(solution)/shard_map/ppermute | solution.py:314
  47.7 26.0 %copy-start = (bf16[512,3584]{1,0:T(8,128)(2,1)S(1)}, bf16[512,3584]{1,0:T(8,128)(2,1)}, u32[]{:S(2)}) copy-start(bf16[512,3584]{1,0:T(8,128)(2,1)} %weight_ref.1) | copy-start | bytes 11010052
  47.7 4.3 %collective-permute-start.3 = (bf16[512,640]{1,0:T(8,128)(2,1)S(1)}, bf16[512,640]{1,0:T(8,128)(2,1)S(1)}, u32[]{:S(2)}, u32[]{:S(2)}) collective-permute-start(bf16[512,640]{1,0:T(8,128)(2,1)S(1)} %bitcast.4), channel_id=1, source_target_pairs={{0,1},{1,0},{2,3},{3,2},{4,5},{5,4},{6,7},{7,6},{8,9},{9,8},{10,11... | collective-permute-start | bytes 1966088 | tf_op jit(solution)/shard_map/ppermute | solution.py:318
  74.6 3.7 %collective-permute-start.4 = (bf16[4,2,224,128]{3,2,1,0:T(8,128)(2,1)S(1)}, bf16[4,2,224,128]{3,2,1,0:T(8,128)(2,1)S(1)}, u32[]{:S(2)}, u32[]{:S(2)}) collective-permute-start(bf16[4,2,224,128]{3,2,1,0:T(8,128)(2,1)S(1)} %get-tuple-element.26), channel_id=1, source_target_pairs={{0,1},{1,0},{2,3},{3,2},{4,5},{5,4},{6,7},{7,6},{8,9},{9,8},{10,11... | collective-permute-start | bytes 1376264 | tf_op jit(solution)/shard_map/ppermute | solution.py:318
  79.2 12.8 %all-to-all-start.3 = ((bf16[4,2,224,128]{3,2,1,0:T(8,128)(2,1)}), bf16[4,2,224,128]{3,2,1,0:T(8,128)(2,1)S(1)}, u32[]{:S(2)}, u32[]{:S(2)}) async-start(bf16[4,2,224,128]{3,2,1,0:T(8,128)(2,1)} %add_convert_fusion), calls=%async_computation.3 | async-start | bytes 917504 | tf_op jit(solution)/shard_map/all_to_all | solution.py:322
  92.1 16.0 %collective-permute-start.5 = (bf16[224,128]{1,0:T(8,128)(2,1)S(1)}, bf16[224,128]{1,0:T(8,128)(2,1)S(1)}, u32[]{:S(2)}, u32[]{:S(2)}) collective-permute-start(bf16[224,128]{1,0:T(8,128)(2,1)S(1)} %get-tuple-element.27), channel_id=1, source_target_pairs={{0,2},{2,0},{1,3},{3,1},{4,6},{6,4},{5,7},{7,5},{8,10},{10,8},{9,1... | collective-permute-start | bytes 172040 | tf_op jit(solution)/shard_map/ppermute | solution.py:318

commit v7 on v6

--- a/solution.py
+++ b/solution.py
@@ -115,9 +115,10 @@
         at = slice(h * SPAN, (h + 1) * SPAN)
         for b in range(2 * NX):
             query[b, at, :LAT] = absorbed[b * SPAN : (b + 1) * SPAN]
-            query[b, at, LAT:] = blocks[b // 2][(b % 2) * SPAN : (b % 2 + 1) * SPAN, first : first + ROPE]
+            part = blocks[b // 2][(b % 2) * SPAN : (b % 2 + 1) * SPAN, first : first + ROPE]
+            query[b, at, LAT:] = jnp.concatenate([part, part], axis=1)
     for h in range(HEADS):
-        turned_value[h] = value_ref[h].T
+        turned_value[h // 2, (h % 2) * VD : (h % 2 + 1) * VD, :] = value_ref[h].T
 
 
 def in_hbm(value):
@@ -128,8 +129,8 @@
     return pl.pallas_call(
         absorb_kernel,
         out_shape=(
-            jax.ShapeDtypeStruct((2 * NX, HEADS * SPAN, KEYW), jnp.bfloat16),
-            jax.ShapeDtypeStruct((HEADS, VD, LAT), jnp.bfloat16),
+            jax.ShapeDtypeStruct((2 * NX, HEADS * SPAN, ROWW), jnp.bfloat16),
+            jax.ShapeDtypeStruct((HEADS // 2, 2 * VD, LAT), jnp.bfloat16),
         ),
         in_specs=[HBM] + [WHOLE] * 3 + [HBM] * 2,
         out_specs=(WHOLE, WHOLE),
@@ -159,9 +160,16 @@
         rank = earlier(places[i], places)
         for half, keys in enumerate((own_ref, other_ref)):
             for low in range(2):
-                source = ((i % 2) * 2 + low) * GROUP * 8 + (i // 2) * NZH * 8
                 target = pl.multiple_of(rank * SPAN + half * 32 + low * 16, 16)
-                sorted_keys[pl.ds(target, 16), :] = keys[source : source + 16, :]
+                y = (i % 2) * 2 + low
+                first = (i // 2) * NZH * 8
+                for j in range(LAT // 128):
+                    sorted_keys[pl.ds(target, 16), j * 128 : (j + 1) * 128] = keys[
+                        y, j * 128 + first : j * 128 + first + 16, :
+                    ]
+                tail = keys[y, LAT + first % 64 : LAT + first % 64 + 16, :]
+                side = lax.broadcasted_iota(jnp.int32, tail.shape, 1) // ROPE
+                sorted_keys[pl.ds(target, 16), LAT:] = jnp.where(side == first // 64, tail, jnp.zeros_like(tail))
 
     asking = [spans_ref[(zl * NX + (x + NX - b // 2) % NX) * 2 + b % 2] for b in range(2 * NX)]
     for b in range(2 * NX):
@@ -195,7 +203,7 @@
                 products = [
                     [
                         lax.dot_general(
-                            sorted_keys[n * CHUNK : (n + 1) * CHUNK, :KEYW],
+                            sorted_keys[n * CHUNK : (n + 1) * CHUNK, :],
                             query[b],
                             dims,
                             preferred_element_type=jnp.float32,
@@ -230,25 +238,28 @@
 
     lax.fori_loop(0, 2 * NX // GROUPED, some_spans, 0)
 
-    for h in range(HEADS):
-        at = slice(h * SPAN, (h + 1) * SPAN)
-        joined = jnp.concatenate([contexts[b, :LAT, at] for b in range(2 * NX)], axis=1)
-        values = jnp.dot(value_ref[h], joined, preferred_element_type=jnp.float32).astype(jnp.bfloat16)
+    left = lax.broadcasted_iota(jnp.int32, (VD, 128), 1) < SPAN
+    for p in range(HEADS // 2):
+        tile = slice(p * 128, (p + 1) * 128)
+        joined = jnp.concatenate([contexts[b, :LAT, tile] for b in range(2 * NX)], axis=1)
+        both = jnp.dot(value_ref[p], joined, preferred_element_type=jnp.float32)
         for k in range(NX):
-            tokens = slice(k * 2 * SPAN, (k + 1) * 2 * SPAN)
-            out_ref[(x + NX - k) % NX, h * VD : (h + 1) * VD, :] = values[:, tokens]
+            early, late = [
+                jnp.where(left, both[:VD, b * 128 : (b + 1) * 128], both[VD:, b * 128 : (b + 1) * 128])
+                for b in (2 * k, 2 * k + 1)
+            ]
+            target = (x + NX - k) % NX
+            for side, values in enumerate(
+                (jnp.where(left, early, pltpu.roll(late, SPAN, axis=1)), jnp.where(left, pltpu.roll(early, SPAN, axis=1), late))
+            ):
+                out_ref[target, (2 * p + side) * VD : (2 * p + side + 1) * VD, :] = values.astype(jnp.bfloat16)
     for k in range(NX):
-        logs = [
-            functools.reduce(
-                jnp.add,
-                [
-                    contexts[b, LAT:, h * SPAN : (h + 1) * SPAN].astype(jnp.float32)
-                    for h in range(HEADS)
-                ],
-            )
-            for b in (2 * k, 2 * k + 1)
-        ]
-        out_ref[(x + NX - k) % NX, HEADS * VD :, :] = jnp.concatenate(logs, axis=1).astype(jnp.bfloat16)
+        logs = []
+        for b in (2 * k, 2 * k + 1):
+            rows = contexts[b, LAT:, :].astype(jnp.float32)
+            rows = rows[:, :128] + rows[:, 128:]
+            logs.append(rows + pltpu.roll(rows, SPAN, axis=1))
+        out_ref[(x + NX - k) % NX, HEADS * VD :, :] = jnp.where(left[:16], *logs).astype(jnp.bfloat16)
 
 
 def attend(spans, query, own, other, turned_value):
@@ -265,6 +276,40 @@
         ],
         compiler_params=pltpu.CompilerParams(vmem_limit_bytes=VMEM_LIMIT),
     )(spans, query, own, other, turned_value)
+
+
+def replicate_kernel(keys_ref, out_ref):
+    rows = keys_ref.shape[0]
+    side = lax.broadcasted_iota(jnp.int32, (rows // 2, 128), 1) < ROPE
+    tail = jnp.where(side, keys_ref[: rows // 2, LAT:], keys_ref[rows // 2 :, LAT:])
+    for k in range(NY):
+        for j in range(LAT // 128):
+            out_ref[k, j * rows : (j + 1) * rows, :] = keys_ref[:, j * 128 : (j + 1) * 128]
+        out_ref[k, LAT // 128 * rows :, :] = tail
+
+
+def replicate(keys):
+    return pl.pallas_call(
+        replicate_kernel,
+        out_shape=jax.ShapeDtypeStruct((NY, keys.shape[0] * KEYW // 128, 128), jnp.bfloat16),
+        in_specs=[WHOLE],
+        out_specs=WHOLE,
+        compiler_params=pltpu.CompilerParams(vmem_limit_bytes=VMEM_LIMIT),
+    )(keys)
+
+
+def add_kernel(first_ref, second_ref, out_ref):
+    out_ref[...] = (first_ref[...].astype(jnp.float32) + second_ref[...].astype(jnp.float32)).astype(jnp.bfloat16)
+
+
+def added(first, second):
+    return pl.pallas_call(
+        add_kernel,
+        out_shape=jax.ShapeDtypeStruct(first.shape, jnp.bfloat16),
+        in_specs=[WHOLE, WHOLE],
+        out_specs=WHOLE,
+        compiler_params=pltpu.CompilerParams(vmem_limit_bytes=VMEM_LIMIT),
+    )(first, second)
 
 
 def project_kernel(parts_ref, weight_ref, send_ref, keep_ref):
@@ -342,13 +387,13 @@
     blocks = [queries, shifted(queries, 1), None, shifted(queries, NX - 1)]
     along_z, blocks[1], blocks[3] = lax.optimization_barrier((along_z, blocks[1], blocks[3]))
     blocks[2] = shifted(blocks[1], 1)
-    own = exchanged(jnp.broadcast_to(along_z[None], (NY, GROUP * 8, ROWW)), "y").reshape(NY * GROUP * 8, ROWW)
+    own = exchanged(replicate(along_z), "y")
     own, blocks[2] = lax.optimization_barrier((own, blocks[2]))
     other = swapped(own, "c")
     query, turned_value = absorb(blocks, key_up, value_up)
     parts = attend(kept_spans, query, own, other, turned_value)
     send, keep = project(exchanged(parts, "x"), output_weight)
-    both = (keep.astype(jnp.float32) + swapped(send, "c").astype(jnp.float32)).astype(jnp.bfloat16)
+    both = added(keep, swapped(send, "c"))
     over_y = exchanged(both, "y").astype(jnp.float32)
     mine = jnp.sum(lax.dynamic_index_in_dim(over_y, zh, 1, keepdims=False), axis=0)
     theirs = jnp.sum(lax.dynamic_index_in_dim(over_y, 1 - zh, 1, keepdims=False), axis=0).astype(jnp.bfloat16)

time: 109 us -> 110 us (level)
  Pallas kernels: 14 us -> 15.8 us
  waiting for transfers between devices: 31.9 us -> 33 us
    pallas_call x0 -> x2, Pallas kernels: none -> 1.79 us  [the longest x1 0.9 us: replicate(): pl.pallas_call(replicate_kernel, out_shape=jax.ShapeDtypeStruct((NY, keys...]
    ppermute x3, waiting for transfers between devices: 9.59 us -> 10.8 us  [swapped(): return lax.ppermute(value, axis, [(0, 1), (1, 0)])]
  transfers between devices with their start and end apart: 9 -> 9, of which waited for: 7 -> 7; matrix products, arithmetic and copies ran while one was open for 0% -> 0% of each run, Pallas kernels for 4% -> 3%
where the time goes in v7:
time: 110 us
  starting transfers between devices  45.5 us (41%)
  waiting for transfers between devices  33 us (30%)
  Pallas kernels  15.8 us (14%)
  blocking collectives  15 us (14%)
    all_to_all x3, starting transfers between devices, exchanged(): return lax.all_to_all(value, axis, split_axis=0, concat_axis=0, tiled=True)  23.6 us
    all_to_all x1, blocking collectives, exchanged(): return lax.all_to_all(value, axis, split_axis=0, concat_axis=0, tiled=True)  15 us
    all_to_all x3, waiting for transfers between devices, exchanged(): return lax.all_to_all(value, axis, split_axis=0, concat_axis=0, tiled=True)  12.6 us
    ppermute x3, starting transfers between devices, swapped(): return lax.ppermute(value, axis, [(0, 1), (1, 0)])  11.5 us
    ppermute x3, waiting for transfers between devices, swapped(): return lax.ppermute(value, axis, [(0, 1), (1, 0)])  10.8 us
    ppermute x3, starting transfers between devices, shifted(): return lax.ppermute(value, 'x', [(i, (i + by) % NX) for i in range(NX)])  10.4 us
    ppermute x3, waiting for transfers between devices, shifted(): return lax.ppermute(value, 'x', [(i, (i + by) % NX) for i in range(NX)])  9.61 us
    pallas_call x1, Pallas kernels, attend(): pl.pallas_call(attend_kernel, out_shape=jax.ShapeDtypeStruct((NX, PARTROW...  7.49 us
  transfers between devices with their start and end apart: 9, of which 7 were waited for; matrix products, arithmetic and copies ran while one was open for 0% of the time, Pallas kernels for 3%

profile of v7, /device:TPU:32, one launch (start us, length us, event | category | flops | bytes accessed | tf_op | source)
XLA Modules:
  0.0 110.2 jit_solution(3883427664345323326)
XLA Ops:
  0.0 1.7 %shard_map.82.after_ref = bf16[16,8,640]{2,1,0:T(8,128)(2,1)} custom-call(s32[64]{0:T(128)} %spans_ref.3, bf16[8,576]{1,0:T(8,128)(2,1)} %keys_ref.1, f32[4,64,128]{2,1,0:T(8,128)} %constant.20.clone.tables_ref), custom_call_target="tpu_custom_call" | custom-call | tf_op jit(solution)/shard_map/pallas_call | solution.py:373
  1.7 15.2 %all-to-all-start = ((bf16[16,8,640]{2,1,0:T(8,128)(2,1)}), bf16[16,8,640]{2,1,0:T(8,128)(2,1)S(1)}, u32[]{:S(2)}, u32[]{:S(2)}) async-start(bf16[16,8,640]{2,1,0:T(8,128)(2,1)} %shard_map.82.after_ref), calls=%async_computation | async-start | bytes 327680 | tf_op jit(solution)/shard_map/all_to_all | solution.py:367
  17.0 1.8 %shard_map.83 = (bf16[128,768]{1,0:T(8,128)(2,1)}, s32[64]{0:T(128)}) custom-call(s32[64]{0:T(128)} %spans_ref.3, bf16[128,512]{1,0:T(8,128)(2,1)} %plain_ref.1, bf16[128,256]{1,0:T(8,128)(2,1)} %rotary_ref.1, f32[4,64,128]{2,1,0:T(8,128)} %constant.20.clone.tables_ref, bf16[16,8,640]{2,1,0:T(8,128)(2,1)} %shard_map.82.after_ref), custom_call_target="tpu_custom_call" | custom-call | tf_op jit(solution)/shard_map/pallas_call | solution.py:380
  18.8 3.4 %collective-permute-start = (bf16[128,768]{1,0:T(8,128)(2,1)}, bf16[128,768]{1,0:T(8,128)(2,1)S(1)}, u32[]{:S(2)}, u32[]{:S(2)}) collective-permute-start(bf16[128,768]{1,0:T(8,128)(2,1)} %get-tuple-element.17.q0_hbm), channel_id=1, source_target_pairs={{0,16},{16,32},{32,48},{48,0},{1,17},{17,33},{33,49},{49,1},{2,18}... | collective-permute-start | bytes 589832 | tf_op jit(solution)/shard_map/ppermute | solution.py:359
  22.2 3.7 %collective-permute-start.1 = (bf16[128,768]{1,0:T(8,128)(2,1)}, bf16[128,768]{1,0:T(8,128)(2,1)S(1)}, u32[]{:S(2)}, u32[]{:S(2)}) collective-permute-start(bf16[128,768]{1,0:T(8,128)(2,1)} %get-tuple-element.17.q0_hbm), channel_id=1, source_target_pairs={{0,48},{16,0},{32,16},{48,32},{1,49},{17,1},{33,17},{49,33},{2,50}... | collective-permute-start | bytes 589832 | tf_op jit(solution)/shard_map/ppermute | solution.py:359
  25.8 2.3 %collective-permute-done.q1 = bf16[128,768]{1,0:T(8,128)(2,1)S(1)} collective-permute-done((bf16[128,768]{1,0:T(8,128)(2,1)}, bf16[128,768]{1,0:T(8,128)(2,1)S(1)}, u32[]{:S(2)}, u32[]{:S(2)}) %collective-permute-start) | collective-permute-done | bytes 196640 | tf_op jit(solution)/shard_map/ppermute | solution.py:359
  28.2 1.9 %collective-permute-done.1.q3 = bf16[128,768]{1,0:T(8,128)(2,1)S(1)} collective-permute-done((bf16[128,768]{1,0:T(8,128)(2,1)}, bf16[128,768]{1,0:T(8,128)(2,1)S(1)}, u32[]{:S(2)}, u32[]{:S(2)}) %collective-permute-start.1) | collective-permute-done | bytes 196640 | tf_op jit(solution)/shard_map/ppermute | solution.py:359
  30.1 3.5 %all-to-all-done = bf16[16,8,640]{2,1,0:T(8,128)(2,1)S(1)} async-done(((bf16[16,8,640]{2,1,0:T(8,128)(2,1)}), bf16[16,8,640]{2,1,0:T(8,128)(2,1)S(1)}, u32[]{:S(2)}, u32[]{:S(2)}) %all-to-all-start) | async-done | bytes 163872 | tf_op jit(solution)/shard_map/all_to_all | solution.py:367
  33.6 0.9 shard_map.84
  34.5 4.5 %all-to-all-start.1 = ((bf16[4,576,128]{2,1,0:T(8,128)(2,1)}), bf16[4,576,128]{2,1,0:T(8,128)(2,1)S(1)}, u32[]{:S(2)}, u32[]{:S(2)}) async-start(bf16[4,576,128]{2,1,0:T(8,128)(2,1)} %shard_map.84), calls=%async_computation.1 | async-start | bytes 1179648 | tf_op jit(solution)/shard_map/all_to_all | solution.py:367
  38.9 3.4 %collective-permute-start.2 = (bf16[128,768]{1,0:T(8,128)(2,1)S(1)}, bf16[128,768]{1,0:T(8,128)(2,1)S(1)}, u32[]{:S(2)}, u32[]{:S(2)}) collective-permute-start(bf16[128,768]{1,0:T(8,128)(2,1)S(1)} %collective-permute-done.q1), channel_id=1, source_target_pairs={{0,16},{16,32},{32,48},{48,0},{1,17},{17,33},{33,49},{49,1},{2,18}... | collective-permute-start | bytes 589832 | tf_op jit(solution)/shard_map/ppermute | solution.py:359
  42.3 5.4 %collective-permute-done.2.q2 = bf16[128,768]{1,0:T(8,128)(2,1)S(1)} collective-permute-done((bf16[128,768]{1,0:T(8,128)(2,1)S(1)}, bf16[128,768]{1,0:T(8,128)(2,1)S(1)}, u32[]{:S(2)}, u32[]{:S(2)}) %collective-permute-start.2) | collective-permute-done | bytes 196640 | tf_op jit(solution)/shard_map/ppermute | solution.py:359
  47.7 2.2 %collective-permute-start.3 = (bf16[4,576,128]{2,1,0:T(8,128)(2,1)S(1)}, bf16[4,576,128]{2,1,0:T(8,128)(2,1)S(1)}, u32[]{:S(2)}, u32[]{:S(2)}) collective-permute-start(bf16[4,576,128]{2,1,0:T(8,128)(2,1)S(1)} %all-to-all-done.1.own_ref), channel_id=1, source_target_pairs={{0,1},{1,0},{2,3},{3,2},{4,5},{5,4},{6,7},{7,6},{8,9},{9,8},{10,11... | collective-permute-start | bytes 1769480 | tf_op jit(solution)/shard_map/ppermute | solution.py:363
  49.9 2.0 %shard_map.85 = (bf16[8,256,640]{2,1,0:T(8,128)(2,1)S(1)}, bf16[2,256,512]{2,1,0:T(8,128)(2,1)S(1)}) custom-call(bf16[128,768]{1,0:T(8,128)(2,1)} %get-tuple-element.17.q0_hbm, bf16[128,768]{1,0:T(8,128)(2,1)S(1)} %collective-permute-done.q1, bf16[128,768]{1,0:T(8,128)(2,1)S(1)} %collective-permute-done.2.q2, ...), custom_call_target="tpu_custom_call" | custom-call | tf_op jit(solution)/shard_map/pallas_call | solution.py:129
  52.0 7.5 %shard_map.86 = bf16[4,528,128]{2,1,0:T(8,128)(2,1)S(1)} custom-call(s32[64]{0:T(128)S(1)} %copy-done.1, bf16[8,256,640]{2,1,0:T(8,128)(2,1)S(1)} %get-tuple-element.22.query, bf16[4,576,128]{2,1,0:T(8,128)(2,1)S(1)} %all-to-all-done.1.own_ref, bf16[4,576,128]{2,1,0:T(8,128)(2,1)S(1)} %collective-permute-done.3.other_ref, ...), custom_call_target="tpu_custom_call" | custom-call | tf_op jit(solution)/shard_map/pallas_call | solution.py:266
  59.5 15.0 %all_to_all.20.parts_ref = bf16[4,528,128]{2,1,0:T(8,128)(2,1)S(1)} all-to-all(bf16[4,528,128]{2,1,0:T(8,128)(2,1)S(1)} %shard_map.86), channel_id=1, replica_groups=mesh['zl'=8,'x'=4,'y'=4,'zh'=2,'c'=2] {'x'}, dimensions={0} | all-to-all | bytes 1081344 | tf_op jit(solution)/shard_map/all_to_all | solution.py:367
  74.5 0.9 shard_map.87
  75.4 1.9 %collective-permute-start.4 = (bf16[4,2,224,128]{3,2,1,0:T(8,128)(2,1)S(1)}, bf16[4,2,224,128]{3,2,1,0:T(8,128)(2,1)S(1)}, u32[]{:S(2)}, u32[]{:S(2)}) collective-permute-start(bf16[4,2,224,128]{3,2,1,0:T(8,128)(2,1)S(1)} %get-tuple-element.26), channel_id=1, source_target_pairs={{0,1},{1,0},{2,3},{3,2},{4,5},{5,4},{6,7},{7,6},{8,9},{9,8},{10,11... | collective-permute-start | bytes 1376264 | tf_op jit(solution)/shard_map/ppermute | solution.py:363
  77.3 1.8 %collective-permute-done.4.second_ref = bf16[4,2,224,128]{3,2,1,0:T(8,128)(2,1)S(1)} collective-permute-done((bf16[4,2,224,128]{3,2,1,0:T(8,128)(2,1)S(1)}, bf16[4,2,224,128]{3,2,1,0:T(8,128)(2,1)S(1)}, u32[]{:S(2)}, u32[]{:S(2)}) %collective-permute-start.4) | collective-permute-done | bytes 458784 | tf_op jit(solution)/shard_map/ppermute | solution.py:363
  79.1 0.9 shard_map.88
  80.0 3.9 %all-to-all-start.3 = ((bf16[4,2,224,128]{3,2,1,0:T(8,128)(2,1)}), bf16[4,2,224,128]{3,2,1,0:T(8,128)(2,1)S(1)}, u32[]{:S(2)}, u32[]{:S(2)}) async-start(bf16[4,2,224,128]{3,2,1,0:T(8,128)(2,1)} %shard_map.88), calls=%async_computation.3 | async-start | bytes 917504 | tf_op jit(solution)/shard_map/all_to_all | solution.py:367
  83.9 9.1 %all-to-all-done.3 = bf16[4,2,224,128]{3,2,1,0:T(8,128)(2,1)S(1)} async-done(((bf16[4,2,224,128]{3,2,1,0:T(8,128)(2,1)}), bf16[4,2,224,128]{3,2,1,0:T(8,128)(2,1)S(1)}, u32[]{:S(2)}, u32[]{:S(2)}) %all-to-all-start.3) | async-done | bytes 458784 | tf_op jit(solution)/shard_map/all_to_all | solution.py:367
  93.1 7.4 %collective-permute-start.5 = (bf16[224,128]{1,0:T(8,128)(2,1)S(1)}, bf16[224,128]{1,0:T(8,128)(2,1)S(1)}, u32[]{:S(2)}, u32[]{:S(2)}) collective-permute-start(bf16[224,128]{1,0:T(8,128)(2,1)S(1)} %get-tuple-element.27), channel_id=1, source_target_pairs={{0,2},{2,0},{1,3},{3,1},{4,6},{6,4},{5,7},{7,5},{8,10},{10,8},{9,1... | collective-permute-start | bytes 172040 | tf_op jit(solution)/shard_map/ppermute | solution.py:363
  100.5 9.0 %collective-permute-done.5 = bf16[224,128]{1,0:T(8,128)(2,1)S(1)} collective-permute-done((bf16[224,128]{1,0:T(8,128)(2,1)S(1)}, bf16[224,128]{1,0:T(8,128)(2,1)S(1)}, u32[]{:S(2)}, u32[]{:S(2)}) %collective-permute-start.5) | collective-permute-done | bytes 57376 | tf_op jit(solution)/shard_map/ppermute | solution.py:363
  (9 shorter events, 0.8 us)
Async XLA Ops:
  1.7 31.8 %all-to-all-start = ((bf16[16,8,640]{2,1,0:T(8,128)(2,1)}), bf16[16,8,640]{2,1,0:T(8,128)(2,1)S(1)}, u32[]{:S(2)}, u32[]{:S(2)}) async-start(bf16[16,8,640]{2,1,0:T(8,128)(2,1)} %shard_map.82.after_ref), calls=%async_computation | async-start | bytes 327680 | tf_op jit(solution)/shard_map/all_to_all | solution.py:367
  18.8 33.2 %copy-start.1 = (s32[64]{0:T(128)S(1)}, s32[64]{0:T(128)}, u32[]{:S(2)}) copy-start(s32[64]{0:T(128)} %get-tuple-element.16.spans_ref) | copy-start | bytes 772
  18.8 9.4 %collective-permute-start = (bf16[128,768]{1,0:T(8,128)(2,1)}, bf16[128,768]{1,0:T(8,128)(2,1)S(1)}, u32[]{:S(2)}, u32[]{:S(2)}) collective-permute-start(bf16[128,768]{1,0:T(8,128)(2,1)} %get-tuple-element.17.q0_hbm), channel_id=1, source_target_pairs={{0,16},{16,32},{32,48},{48,0},{1,17},{17,33},{33,49},{49,1},{2,18}... | collective-permute-start | bytes 589832 | tf_op jit(solution)/shard_map/ppermute | solution.py:359
  22.2 7.9 %collective-permute-start.1 = (bf16[128,768]{1,0:T(8,128)(2,1)}, bf16[128,768]{1,0:T(8,128)(2,1)S(1)}, u32[]{:S(2)}, u32[]{:S(2)}) collective-permute-start(bf16[128,768]{1,0:T(8,128)(2,1)} %get-tuple-element.17.q0_hbm), channel_id=1, source_target_pairs={{0,48},{16,0},{32,16},{48,32},{1,49},{17,1},{33,17},{49,33},{2,50}... | collective-permute-start | bytes 589832 | tf_op jit(solution)/shard_map/ppermute | solution.py:359
  34.5 13.2 %all-to-all-start.1 = ((bf16[4,576,128]{2,1,0:T(8,128)(2,1)}), bf16[4,576,128]{2,1,0:T(8,128)(2,1)S(1)}, u32[]{:S(2)}, u32[]{:S(2)}) async-start(bf16[4,576,128]{2,1,0:T(8,128)(2,1)} %shard_map.84), calls=%async_computation.1 | async-start | bytes 1179648 | tf_op jit(solution)/shard_map/all_to_all | solution.py:367
  38.9 8.8 %collective-permute-start.2 = (bf16[128,768]{1,0:T(8,128)(2,1)S(1)}, bf16[128,768]{1,0:T(8,128)(2,1)S(1)}, u32[]{:S(2)}, u32[]{:S(2)}) collective-permute-start(bf16[128,768]{1,0:T(8,128)(2,1)S(1)} %collective-permute-done.q1), channel_id=1, source_target_pairs={{0,16},{16,32},{32,48},{48,0},{1,17},{17,33},{33,49},{49,1},{2,18}... | collective-permute-start | bytes 589832 | tf_op jit(solution)/shard_map/ppermute | solution.py:359
  47.7 26.7 %copy-start = (bf16[512,3584]{1,0:T(8,128)(2,1)S(1)}, bf16[512,3584]{1,0:T(8,128)(2,1)}, u32[]{:S(2)}) copy-start(bf16[512,3584]{1,0:T(8,128)(2,1)} %weight_ref.1) | copy-start | bytes 11010052
  47.7 4.2 %collective-permute-start.3 = (bf16[4,576,128]{2,1,0:T(8,128)(2,1)S(1)}, bf16[4,576,128]{2,1,0:T(8,128)(2,1)S(1)}, u32[]{:S(2)}, u32[]{:S(2)}) collective-permute-start(bf16[4,576,128]{2,1,0:T(8,128)(2,1)S(1)} %all-to-all-done.1.own_ref), channel_id=1, source_target_pairs={{0,1},{1,0},{2,3},{3,2},{4,5},{5,4},{6,7},{7,6},{8,9},{9,8},{10,11... | collective-permute-start | bytes 1769480 | tf_op jit(solution)/shard_map/ppermute | solution.py:363
  75.4 3.7 %collective-permute-start.4 = (bf16[4,2,224,128]{3,2,1,0:T(8,128)(2,1)S(1)}, bf16[4,2,224,128]{3,2,1,0:T(8,128)(2,1)S(1)}, u32[]{:S(2)}, u32[]{:S(2)}) collective-permute-start(bf16[4,2,224,128]{3,2,1,0:T(8,128)(2,1)S(1)} %get-tuple-element.26), channel_id=1, source_target_pairs={{0,1},{1,0},{2,3},{3,2},{4,5},{5,4},{6,7},{7,6},{8,9},{9,8},{10,11... | collective-permute-start | bytes 1376264 | tf_op jit(solution)/shard_map/ppermute | solution.py:363
  80.0 13.0 %all-to-all-start.3 = ((bf16[4,2,224,128]{3,2,1,0:T(8,128)(2,1)}), bf16[4,2,224,128]{3,2,1,0:T(8,128)(2,1)S(1)}, u32[]{:S(2)}, u32[]{:S(2)}) async-start(bf16[4,2,224,128]{3,2,1,0:T(8,128)(2,1)} %shard_map.88), calls=%async_computation.3 | async-start | bytes 917504 | tf_op jit(solution)/shard_map/all_to_all | solution.py:367
  93.1 16.4 %collective-permute-start.5 = (bf16[224,128]{1,0:T(8,128)(2,1)S(1)}, bf16[224,128]{1,0:T(8,128)(2,1)S(1)}, u32[]{:S(2)}, u32[]{:S(2)}) collective-permute-start(bf16[224,128]{1,0:T(8,128)(2,1)S(1)} %get-tuple-element.27), channel_id=1, source_target_pairs={{0,2},{2,0},{1,3},{3,1},{4,6},{6,4},{5,7},{7,5},{8,10},{10,8},{9,1... | collective-permute-start | bytes 172040 | tf_op jit(solution)/shard_map/ppermute | solution.py:363

commit v8 on v7

--- a/solution.py
+++ b/solution.py
@@ -31,7 +31,7 @@
 BASE = 10000.0
 LOW = -1e30
 SCALE = math.log2(math.e) / math.sqrt(NOPE + ROPE)
-VMEM_LIMIT = 48 * 1024 * 1024
+MIB = 1024 * 1024
 
 
 def rotary_tables():
@@ -98,10 +98,12 @@
 HBM = pl.BlockSpec(memory_space=pltpu.HBM)
 
 
-def absorb_kernel(q0_hbm, q1, q2, q3, up_hbm, value_hbm, query, turned_value, q0, up_ref, value_ref, arrived):
+def absorb_kernel(*refs):
+    sources, (query, turned_value), targets, arrived = refs[:6], refs[6:8], refs[8:14], refs[14]
+    q0, q1, q2, q3, up_ref, value_ref = targets
     fetches = [
         pltpu.make_async_copy(source, target, arrived.at[i])
-        for i, (source, target) in enumerate(((q0_hbm, q0), (up_hbm, up_ref), (value_hbm, value_ref)))
+        for i, (source, target) in enumerate(zip(sources, targets))
     ]
     for fetch in fetches:
         fetch.start()
@@ -132,21 +134,21 @@
             jax.ShapeDtypeStruct((2 * NX, HEADS * SPAN, ROWW), jnp.bfloat16),
             jax.ShapeDtypeStruct((HEADS // 2, 2 * VD, LAT), jnp.bfloat16),
         ),
-        in_specs=[HBM] + [WHOLE] * 3 + [HBM] * 2,
+        in_specs=[HBM] * 6,
         out_specs=(WHOLE, WHOLE),
         scratch_shapes=[
-            pltpu.VMEM(blocks[0].shape, jnp.bfloat16),
-            pltpu.VMEM(key_up.shape, jnp.bfloat16),
-            pltpu.VMEM(value_up.shape, jnp.bfloat16),
-            pltpu.SemaphoreType.DMA((3,)),
+            *[pltpu.VMEM(v.shape, jnp.bfloat16) for v in (*blocks, key_up, value_up)],
+            pltpu.SemaphoreType.DMA((6,)),
         ],
-        compiler_params=pltpu.CompilerParams(vmem_limit_bytes=VMEM_LIMIT),
-    )(in_hbm(blocks[0]), *blocks[1:], in_hbm(key_up), in_hbm(value_up))
+        compiler_params=pltpu.CompilerParams(vmem_limit_bytes=16 * MIB),
+    )(*[in_hbm(v) for v in (*blocks, key_up, value_up)])
 
 
 def attend_kernel(
-    spans_ref, query, own_ref, other_ref, value_ref, out_ref, sorted_keys, latent, contexts, order
+    spans_ref, query, own_ref, other_ref, value_hbm, out_ref, sorted_keys, latent, contexts, order, value_ref, arrived
 ):
+    fetch = pltpu.make_async_copy(value_hbm, value_ref, arrived)
+    fetch.start()
     zl = lax.axis_index("zl")
     x = lax.axis_index("x")
     c = lax.axis_index("c")
@@ -238,6 +240,7 @@
 
     lax.fori_loop(0, 2 * NX // GROUPED, some_spans, 0)
 
+    fetch.wait()
     left = lax.broadcasted_iota(jnp.int32, (VD, 128), 1) < SPAN
     for p in range(HEADS // 2):
         tile = slice(p * 128, (p + 1) * 128)
@@ -266,16 +269,18 @@
     return pl.pallas_call(
         attend_kernel,
         out_shape=jax.ShapeDtypeStruct((NX, PARTROWS, 2 * SPAN), jnp.bfloat16),
-        in_specs=[SMEM] + [WHOLE] * 4,
+        in_specs=[SMEM] + [WHOLE] * 3 + [HBM],
         out_specs=WHOLE,
         scratch_shapes=[
             pltpu.VMEM((NSPAN * SPAN, ROWW), jnp.bfloat16),
             pltpu.VMEM((LAT, NSPAN * SPAN), jnp.bfloat16),
             pltpu.VMEM((2 * NX, LAT + 16, HEADS * SPAN), jnp.bfloat16),
             pltpu.SMEM((2 * NX,), jnp.int32),
+            pltpu.VMEM(turned_value.shape, jnp.bfloat16),
+            pltpu.SemaphoreType.DMA(()),
         ],
-        compiler_params=pltpu.CompilerParams(vmem_limit_bytes=VMEM_LIMIT),
-    )(spans, query, own, other, turned_value)
+        compiler_params=pltpu.CompilerParams(vmem_limit_bytes=28 * MIB),
+    )(spans, query, own, other, in_hbm(turned_value))
 
 
 def replicate_kernel(keys_ref, out_ref):
@@ -294,7 +299,7 @@
         out_shape=jax.ShapeDtypeStruct((NY, keys.shape[0] * KEYW // 128, 128), jnp.bfloat16),
         in_specs=[WHOLE],
         out_specs=WHOLE,
-        compiler_params=pltpu.CompilerParams(vmem_limit_bytes=VMEM_LIMIT),
+        compiler_params=pltpu.CompilerParams(vmem_limit_bytes=6 * MIB),
     )(keys)
 
 
@@ -308,7 +313,7 @@
         out_shape=jax.ShapeDtypeStruct(first.shape, jnp.bfloat16),
         in_specs=[WHOLE, WHOLE],
         out_specs=WHOLE,
-        compiler_params=pltpu.CompilerParams(vmem_limit_bytes=VMEM_LIMIT),
+        compiler_params=pltpu.CompilerParams(vmem_limit_bytes=6 * MIB),
     )(first, second)
 
 
@@ -351,7 +356,7 @@
         out_shape=(piece, piece),
         in_specs=[WHOLE, WHOLE],
         out_specs=(WHOLE, WHOLE),
-        compiler_params=pltpu.CompilerParams(vmem_limit_bytes=VMEM_LIMIT),
+        compiler_params=pltpu.CompilerParams(vmem_limit_bytes=20 * MIB),
     )(parts, weight)
 
 
@@ -385,12 +390,12 @@
     )(span_order, query_plain, query_rotary, tables, sent_keys)
     along_z = exchanged(sent_keys, ("zl", "zh")).reshape(GROUP * 8, ROWW)
     blocks = [queries, shifted(queries, 1), None, shifted(queries, NX - 1)]
-    along_z, blocks[1], blocks[3] = lax.optimization_barrier((along_z, blocks[1], blocks[3]))
     blocks[2] = shifted(blocks[1], 1)
+    along_z, *blocks = lax.optimization_barrier((along_z, *blocks))
+    query, turned_value = absorb(blocks, key_up, value_up)
     own = exchanged(replicate(along_z), "y")
-    own, blocks[2] = lax.optimization_barrier((own, blocks[2]))
+    own, query, turned_value = lax.optimization_barrier((own, query, turned_value))
     other = swapped(own, "c")
-    query, turned_value = absorb(blocks, key_up, value_up)
     parts = attend(kept_spans, query, own, other, turned_value)
     send, keep = project(exchanged(parts, "x"), output_weight)
     both = added(keep, swapped(send, "c"))

time: 110 us -> 111 us (level)
  the two profiles are of different devices: /device:TPU:32 before, /device:TPU:64 now
where the time goes in v8:
time: 111 us; the launch traced here: 110 us
  starting transfers between devices  46.3 us (42%)
  waiting for transfers between devices  32.6 us (29%)
  Pallas kernels  17 us (15%)
  blocking collectives  12.6 us (11%)
    all_to_all x3, starting transfers between devices, exchanged(): return lax.all_to_all(value, axis, split_axis=0, concat_axis=0, tiled=True)  22.7 us
    all_to_all x3, waiting for transfers between devices, exchanged(): return lax.all_to_all(value, axis, split_axis=0, concat_axis=0, tiled=True)  14.6 us
    ppermute x3, starting transfers between devices, swapped(): return lax.ppermute(value, axis, [(0, 1), (1, 0)])  14.4 us
    all_to_all x1, blocking collectives, exchanged(): return lax.all_to_all(value, axis, split_axis=0, concat_axis=0, tiled=True)  12.6 us
    ppermute x3, starting transfers between devices, shifted(): return lax.ppermute(value, 'x', [(i, (i + by) % NX) for i in range(NX)])  9.23 us
    ppermute x3, waiting for transfers between devices, swapped(): return lax.ppermute(value, axis, [(0, 1), (1, 0)])  9.09 us
    ppermute x3, waiting for transfers between devices, shifted(): return lax.ppermute(value, 'x', [(i, (i + by) % NX) for i in range(NX)])  8.89 us
    pallas_call x1, Pallas kernels, attend(): pl.pallas_call(attend_kernel, out_shape=jax.ShapeDtypeStruct((NX, PARTROW...  8.47 us
  transfers between devices with their start and end apart: 9, of which 7 were waited for; matrix products, arithmetic and copies ran while one was open for 0% of the time, Pallas kernels for 4%

profile of v8, /device:TPU:64, one launch (start us, length us, event | category | flops | bytes accessed | tf_op | source)
XLA Modules:
  0.0 110.3 jit_solution(4750093721206031019)
XLA Ops:
  0.0 1.8 %shard_map.82.after_ref = bf16[16,8,640]{2,1,0:T(8,128)(2,1)} custom-call(s32[64]{0:T(128)} %spans_ref.3, bf16[8,576]{1,0:T(8,128)(2,1)} %keys_ref.1, f32[4,64,128]{2,1,0:T(8,128)} %constant.20.clone.tables_ref), custom_call_target="tpu_custom_call" | custom-call | tf_op jit(solution)/shard_map/pallas_call | solution.py:378
  1.8 14.8 %all-to-all-start = ((bf16[16,8,640]{2,1,0:T(8,128)(2,1)}), bf16[16,8,640]{2,1,0:T(8,128)(2,1)S(1)}, u32[]{:S(2)}, u32[]{:S(2)}) async-start(bf16[16,8,640]{2,1,0:T(8,128)(2,1)} %shard_map.82.after_ref), calls=%async_computation | async-start | bytes 327680 | tf_op jit(solution)/shard_map/all_to_all | solution.py:372
  16.5 1.8 %shard_map.83 = (bf16[128,768]{1,0:T(8,128)(2,1)}, s32[64]{0:T(128)}) custom-call(s32[64]{0:T(128)} %spans_ref.3, bf16[128,512]{1,0:T(8,128)(2,1)} %plain_ref.1, bf16[128,256]{1,0:T(8,128)(2,1)} %rotary_ref.1, f32[4,64,128]{2,1,0:T(8,128)} %constant.20.clone.tables_ref, bf16[16,8,640]{2,1,0:T(8,128)(2,1)} %shard_map.82.after_ref), custom_call_target="tpu_custom_call" | custom-call | tf_op jit(solution)/shard_map/pallas_call | solution.py:385
  18.3 3.4 %collective-permute-start = (bf16[128,768]{1,0:T(8,128)(2,1)}, bf16[128,768]{1,0:T(8,128)(2,1)S(1)}, u32[]{:S(2)}, u32[]{:S(2)}) collective-permute-start(bf16[128,768]{1,0:T(8,128)(2,1)} %get-tuple-element.22.refs_0_), channel_id=1, source_target_pairs={{0,16},{16,32},{32,48},{48,0},{1,17},{17,33},{33,49},{49,1},{2,18}... | collective-permute-start | bytes 589832 | tf_op jit(solution)/shard_map/ppermute | solution.py:364
  21.7 3.7 %collective-permute-start.2 = (bf16[128,768]{1,0:T(8,128)(2,1)}, bf16[128,768]{1,0:T(8,128)(2,1)S(1)}, u32[]{:S(2)}, u32[]{:S(2)}) collective-permute-start(bf16[128,768]{1,0:T(8,128)(2,1)} %get-tuple-element.22.refs_0_), channel_id=1, source_target_pairs={{0,48},{16,0},{32,16},{48,32},{1,49},{17,1},{33,17},{49,33},{2,50}... | collective-permute-start | bytes 589832 | tf_op jit(solution)/shard_map/ppermute | solution.py:364
  25.4 2.3 %collective-permute-done.refs_1_ = bf16[128,768]{1,0:T(8,128)(2,1)S(1)} collective-permute-done((bf16[128,768]{1,0:T(8,128)(2,1)}, bf16[128,768]{1,0:T(8,128)(2,1)S(1)}, u32[]{:S(2)}, u32[]{:S(2)}) %collective-permute-start) | collective-permute-done | bytes 196640 | tf_op jit(solution)/shard_map/ppermute | solution.py:364
  27.7 2.2 %collective-permute-start.1 = (bf16[128,768]{1,0:T(8,128)(2,1)S(1)}, bf16[128,768]{1,0:T(8,128)(2,1)S(1)}, u32[]{:S(2)}, u32[]{:S(2)}) collective-permute-start(bf16[128,768]{1,0:T(8,128)(2,1)S(1)} %collective-permute-done.refs_1_), channel_id=1, source_target_pairs={{0,16},{16,32},{32,48},{48,0},{1,17},{17,33},{33,49},{49,1},{2,18}... | collective-permute-start | bytes 589832 | tf_op jit(solution)/shard_map/ppermute | solution.py:364
  29.9 6.6 %collective-permute-done.1.refs_2_ = bf16[128,768]{1,0:T(8,128)(2,1)S(1)} collective-permute-done((bf16[128,768]{1,0:T(8,128)(2,1)S(1)}, bf16[128,768]{1,0:T(8,128)(2,1)S(1)}, u32[]{:S(2)}, u32[]{:S(2)}) %collective-permute-start.1) | collective-permute-done | bytes 196640 | tf_op jit(solution)/shard_map/ppermute | solution.py:364
  36.5 0.9 shard_map.84
  37.4 4.5 %all-to-all-start.1 = ((bf16[4,576,128]{2,1,0:T(8,128)(2,1)}), bf16[4,576,128]{2,1,0:T(8,128)(2,1)S(1)}, u32[]{:S(2)}, u32[]{:S(2)}) async-start(bf16[4,576,128]{2,1,0:T(8,128)(2,1)} %shard_map.84), calls=%async_computation.1 | async-start | bytes 1179648 | tf_op jit(solution)/shard_map/all_to_all | solution.py:372
  41.9 2.3 %shard_map.85 = (bf16[8,256,640]{2,1,0:T(8,128)(2,1)S(1)}, bf16[2,256,512]{2,1,0:T(8,128)(2,1)S(1)}) custom-call(bf16[128,768]{1,0:T(8,128)(2,1)} %get-tuple-element.22.refs_0_, bf16[128,768]{1,0:T(8,128)(2,1)} %copy-done.3, bf16[128,768]{1,0:T(8,128)(2,1)} %copy-done.5, bf16[128,768]{1,0:T(8,128)(2,1)} %copy-done.4, bf16[4,128,512]{2,1,0:T(8,128)(2,1)} %refs_4_.1, ...), custom_call_target="tpu_custom_call" | custom-call | tf_op jit(solution)/shard_map/pallas_call | solution.py:131
  45.0 5.3 %all-to-all-done.1.own_ref = bf16[4,576,128]{2,1,0:T(8,128)(2,1)S(1)} async-done(((bf16[4,576,128]{2,1,0:T(8,128)(2,1)}), bf16[4,576,128]{2,1,0:T(8,128)(2,1)S(1)}, u32[]{:S(2)}, u32[]{:S(2)}) %all-to-all-start.1) | async-done | bytes 589856 | tf_op jit(solution)/shard_map/all_to_all | solution.py:372
  50.3 2.2 %collective-permute-start.3 = (bf16[4,576,128]{2,1,0:T(8,128)(2,1)S(1)}, bf16[4,576,128]{2,1,0:T(8,128)(2,1)S(1)}, u32[]{:S(2)}, u32[]{:S(2)}) collective-permute-start(bf16[4,576,128]{2,1,0:T(8,128)(2,1)S(1)} %all-to-all-done.1.own_ref), channel_id=1, source_target_pairs={{0,1},{1,0},{2,3},{3,2},{4,5},{5,4},{6,7},{7,6},{8,9},{9,8},{10,11... | collective-permute-start | bytes 1769480 | tf_op jit(solution)/shard_map/ppermute | solution.py:368
  52.5 2.0 %collective-permute-done.3.other_ref = bf16[4,576,128]{2,1,0:T(8,128)(2,1)S(1)} collective-permute-done((bf16[4,576,128]{2,1,0:T(8,128)(2,1)S(1)}, bf16[4,576,128]{2,1,0:T(8,128)(2,1)S(1)}, u32[]{:S(2)}, u32[]{:S(2)}) %collective-permute-start.3) | collective-permute-done | bytes 589856 | tf_op jit(solution)/shard_map/ppermute | solution.py:368
  54.5 8.5 %shard_map.86 = bf16[4,528,128]{2,1,0:T(8,128)(2,1)S(1)} custom-call(s32[64]{0:T(128)S(1)} %copy-done.2, bf16[8,256,640]{2,1,0:T(8,128)(2,1)S(1)} %get-tuple-element.28.query, bf16[4,576,128]{2,1,0:T(8,128)(2,1)S(1)} %all-to-all-done.1.own_ref, bf16[4,576,128]{2,1,0:T(8,128)(2,1)S(1)} %collective-permute-done.3.other_ref, bf16[2,256,512]{2,1,0:T(8,128)(2,1)} %copy-done.1), custom_call_target="tpu_custom_call" | custom-call | tf_op jit(solution)/shard_map/pallas_call | solution.py:269
  62.9 12.6 %all_to_all.20.parts_ref = bf16[4,528,128]{2,1,0:T(8,128)(2,1)S(1)} all-to-all(bf16[4,528,128]{2,1,0:T(8,128)(2,1)S(1)} %shard_map.86), channel_id=1, replica_groups=mesh['zl'=8,'x'=4,'y'=4,'zh'=2,'c'=2] {'x'}, dimensions={0} | all-to-all | bytes 1081344 | tf_op jit(solution)/shard_map/all_to_all | solution.py:372
  75.5 0.9 shard_map.87
  76.5 1.9 %collective-permute-start.4 = (bf16[4,2,224,128]{3,2,1,0:T(8,128)(2,1)S(1)}, bf16[4,2,224,128]{3,2,1,0:T(8,128)(2,1)S(1)}, u32[]{:S(2)}, u32[]{:S(2)}) collective-permute-start(bf16[4,2,224,128]{3,2,1,0:T(8,128)(2,1)S(1)} %get-tuple-element.32), channel_id=1, source_target_pairs={{0,1},{1,0},{2,3},{3,2},{4,5},{5,4},{6,7},{7,6},{8,9},{9,8},{10,11... | collective-permute-start | bytes 1376264 | tf_op jit(solution)/shard_map/ppermute | solution.py:368
  78.4 1.8 %collective-permute-done.4.second_ref = bf16[4,2,224,128]{3,2,1,0:T(8,128)(2,1)S(1)} collective-permute-done((bf16[4,2,224,128]{3,2,1,0:T(8,128)(2,1)S(1)}, bf16[4,2,224,128]{3,2,1,0:T(8,128)(2,1)S(1)}, u32[]{:S(2)}, u32[]{:S(2)}) %collective-permute-start.4) | collective-permute-done | bytes 458784 | tf_op jit(solution)/shard_map/ppermute | solution.py:368
  80.2 0.9 shard_map.88
  81.1 3.5 %all-to-all-start.3 = ((bf16[4,2,224,128]{3,2,1,0:T(8,128)(2,1)}), bf16[4,2,224,128]{3,2,1,0:T(8,128)(2,1)S(1)}, u32[]{:S(2)}, u32[]{:S(2)}) async-start(bf16[4,2,224,128]{3,2,1,0:T(8,128)(2,1)} %shard_map.88), calls=%async_computation.3 | async-start | bytes 917504 | tf_op jit(solution)/shard_map/all_to_all | solution.py:372
  84.5 9.3 %all-to-all-done.3 = bf16[4,2,224,128]{3,2,1,0:T(8,128)(2,1)S(1)} async-done(((bf16[4,2,224,128]{3,2,1,0:T(8,128)(2,1)}), bf16[4,2,224,128]{3,2,1,0:T(8,128)(2,1)S(1)}, u32[]{:S(2)}, u32[]{:S(2)}) %all-to-all-start.3) | async-done | bytes 458784 | tf_op jit(solution)/shard_map/all_to_all | solution.py:372
  94.0 10.3 %collective-permute-start.5 = (bf16[224,128]{1,0:T(8,128)(2,1)S(1)}, bf16[224,128]{1,0:T(8,128)(2,1)S(1)}, u32[]{:S(2)}, u32[]{:S(2)}) collective-permute-start(bf16[224,128]{1,0:T(8,128)(2,1)S(1)} %get-tuple-element.33), channel_id=1, source_target_pairs={{0,2},{2,0},{1,3},{3,1},{4,6},{6,4},{5,7},{7,5},{8,10},{10,8},{9,1... | collective-permute-start | bytes 172040 | tf_op jit(solution)/shard_map/ppermute | solution.py:368
  104.3 5.3 %collective-permute-done.5 = bf16[224,128]{1,0:T(8,128)(2,1)S(1)} collective-permute-done((bf16[224,128]{1,0:T(8,128)(2,1)S(1)}, bf16[224,128]{1,0:T(8,128)(2,1)S(1)}, u32[]{:S(2)}, u32[]{:S(2)}) %collective-permute-start.5) | collective-permute-done | bytes 57376 | tf_op jit(solution)/shard_map/ppermute | solution.py:368
  (17 shorter events, 1.6 us)
Async XLA Ops:
  1.8 34.8 %all-to-all-start = ((bf16[16,8,640]{2,1,0:T(8,128)(2,1)}), bf16[16,8,640]{2,1,0:T(8,128)(2,1)S(1)}, u32[]{:S(2)}, u32[]{:S(2)}) async-start(bf16[16,8,640]{2,1,0:T(8,128)(2,1)} %shard_map.82.after_ref), calls=%async_computation | async-start | bytes 327680 | tf_op jit(solution)/shard_map/all_to_all | solution.py:372
  18.3 36.1 %copy-start.2 = (s32[64]{0:T(128)S(1)}, s32[64]{0:T(128)}, u32[]{:S(2)}) copy-start(s32[64]{0:T(128)} %get-tuple-element.19.spans_ref) | copy-start | bytes 772
  18.3 9.4 %collective-permute-start = (bf16[128,768]{1,0:T(8,128)(2,1)}, bf16[128,768]{1,0:T(8,128)(2,1)S(1)}, u32[]{:S(2)}, u32[]{:S(2)}) collective-permute-start(bf16[128,768]{1,0:T(8,128)(2,1)} %get-tuple-element.22.refs_0_), channel_id=1, source_target_pairs={{0,16},{16,32},{32,48},{48,0},{1,17},{17,33},{33,49},{49,1},{2,18}... | collective-permute-start | bytes 589832 | tf_op jit(solution)/shard_map/ppermute | solution.py:364
  21.7 8.2 %collective-permute-start.2 = (bf16[128,768]{1,0:T(8,128)(2,1)}, bf16[128,768]{1,0:T(8,128)(2,1)S(1)}, u32[]{:S(2)}, u32[]{:S(2)}) collective-permute-start(bf16[128,768]{1,0:T(8,128)(2,1)} %get-tuple-element.22.refs_0_), channel_id=1, source_target_pairs={{0,48},{16,0},{32,16},{48,32},{1,49},{17,1},{33,17},{49,33},{2,50}... | collective-permute-start | bytes 589832 | tf_op jit(solution)/shard_map/ppermute | solution.py:364
  27.7 14.1 %copy-start.3 = (bf16[128,768]{1,0:T(8,128)(2,1)}, bf16[128,768]{1,0:T(8,128)(2,1)S(1)}, u32[]{:S(2)}) copy-start(bf16[128,768]{1,0:T(8,128)(2,1)S(1)} %collective-permute-done.refs_1_) | copy-start | bytes 589828
  27.7 8.8 %collective-permute-start.1 = (bf16[128,768]{1,0:T(8,128)(2,1)S(1)}, bf16[128,768]{1,0:T(8,128)(2,1)S(1)}, u32[]{:S(2)}, u32[]{:S(2)}) collective-permute-start(bf16[128,768]{1,0:T(8,128)(2,1)S(1)} %collective-permute-done.refs_1_), channel_id=1, source_target_pairs={{0,16},{16,32},{32,48},{48,0},{1,17},{17,33},{33,49},{49,1},{2,18}... | collective-permute-start | bytes 589832 | tf_op jit(solution)/shard_map/ppermute | solution.py:364
  29.9 7.5 %copy-start.4 = (bf16[128,768]{1,0:T(8,128)(2,1)}, bf16[128,768]{1,0:T(8,128)(2,1)S(1)}, u32[]{:S(2)}) copy-start(bf16[128,768]{1,0:T(8,128)(2,1)S(1)} %collective-permute-done.2.refs_3_) | copy-start | bytes 589828
  36.5 0.9 copy-start.5
  37.4 12.9 %all-to-all-start.1 = ((bf16[4,576,128]{2,1,0:T(8,128)(2,1)}), bf16[4,576,128]{2,1,0:T(8,128)(2,1)S(1)}, u32[]{:S(2)}, u32[]{:S(2)}) async-start(bf16[4,576,128]{2,1,0:T(8,128)(2,1)} %shard_map.84), calls=%async_computation.1 | async-start | bytes 1179648 | tf_op jit(solution)/shard_map/all_to_all | solution.py:372
  44.2 0.8 copy-start.1
  50.3 25.2 %copy-start = (bf16[512,3584]{1,0:T(8,128)(2,1)S(1)}, bf16[512,3584]{1,0:T(8,128)(2,1)}, u32[]{:S(2)}) copy-start(bf16[512,3584]{1,0:T(8,128)(2,1)} %weight_ref.1) | copy-start | bytes 11010052
  50.3 4.1 %collective-permute-start.3 = (bf16[4,576,128]{2,1,0:T(8,128)(2,1)S(1)}, bf16[4,576,128]{2,1,0:T(8,128)(2,1)S(1)}, u32[]{:S(2)}, u32[]{:S(2)}) collective-permute-start(bf16[4,576,128]{2,1,0:T(8,128)(2,1)S(1)} %all-to-all-done.1.own_ref), channel_id=1, source_target_pairs={{0,1},{1,0},{2,3},{3,2},{4,5},{5,4},{6,7},{7,6},{8,9},{9,8},{10,11... | collective-permute-start | bytes 1769480 | tf_op jit(solution)/shard_map/ppermute | solution.py:368
  76.5 3.7 %collective-permute-start.4 = (bf16[4,2,224,128]{3,2,1,0:T(8,128)(2,1)S(1)}, bf16[4,2,224,128]{3,2,1,0:T(8,128)(2,1)S(1)}, u32[]{:S(2)}, u32[]{:S(2)}) collective-permute-start(bf16[4,2,224,128]{3,2,1,0:T(8,128)(2,1)S(1)} %get-tuple-element.32), channel_id=1, source_target_pairs={{0,1},{1,0},{2,3},{3,2},{4,5},{5,4},{6,7},{7,6},{8,9},{9,8},{10,11... | collective-permute-start | bytes 1376264 | tf_op jit(solution)/shard_map/ppermute | solution.py:368
  81.1 12.8 %all-to-all-start.3 = ((bf16[4,2,224,128]{3,2,1,0:T(8,128)(2,1)}), bf16[4,2,224,128]{3,2,1,0:T(8,128)(2,1)S(1)}, u32[]{:S(2)}, u32[]{:S(2)}) async-start(bf16[4,2,224,128]{3,2,1,0:T(8,128)(2,1)} %shard_map.88), calls=%async_computation.3 | async-start | bytes 917504 | tf_op jit(solution)/shard_map/all_to_all | solution.py:372
  94.0 15.6 %collective-permute-start.5 = (bf16[224,128]{1,0:T(8,128)(2,1)S(1)}, bf16[224,128]{1,0:T(8,128)(2,1)S(1)}, u32[]{:S(2)}, u32[]{:S(2)}) collective-permute-start(bf16[224,128]{1,0:T(8,128)(2,1)S(1)} %get-tuple-element.33), channel_id=1, source_target_pairs={{0,2},{2,0},{1,3},{3,1},{4,6},{6,4},{5,7},{7,5},{8,10},{10,8},{9,1... | collective-permute-start | bytes 172040 | tf_op jit(solution)/shard_map/ppermute | solution.py:368

commit v9 on v7

--- a/solution.py
+++ b/solution.py
@@ -278,20 +278,19 @@
     )(spans, query, own, other, turned_value)
 
 
-def replicate_kernel(keys_ref, out_ref):
+def pack_kernel(keys_ref, out_ref):
     rows = keys_ref.shape[0]
     side = lax.broadcasted_iota(jnp.int32, (rows // 2, 128), 1) < ROPE
     tail = jnp.where(side, keys_ref[: rows // 2, LAT:], keys_ref[rows // 2 :, LAT:])
-    for k in range(NY):
-        for j in range(LAT // 128):
-            out_ref[k, j * rows : (j + 1) * rows, :] = keys_ref[:, j * 128 : (j + 1) * 128]
-        out_ref[k, LAT // 128 * rows :, :] = tail
-
-
-def replicate(keys):
+    for j in range(LAT // 128):
+        out_ref[j * rows : (j + 1) * rows, :] = keys_ref[:, j * 128 : (j + 1) * 128]
+    out_ref[LAT // 128 * rows :, :] = tail
+
+
+def pack(keys):
     return pl.pallas_call(
-        replicate_kernel,
-        out_shape=jax.ShapeDtypeStruct((NY, keys.shape[0] * KEYW // 128, 128), jnp.bfloat16),
+        pack_kernel,
+        out_shape=jax.ShapeDtypeStruct((keys.shape[0] * KEYW // 128, 128), jnp.bfloat16),
         in_specs=[WHOLE],
         out_specs=WHOLE,
         compiler_params=pltpu.CompilerParams(vmem_limit_bytes=VMEM_LIMIT),
@@ -387,7 +386,7 @@
     blocks = [queries, shifted(queries, 1), None, shifted(queries, NX - 1)]
     along_z, blocks[1], blocks[3] = lax.optimization_barrier((along_z, blocks[1], blocks[3]))
     blocks[2] = shifted(blocks[1], 1)
-    own = exchanged(replicate(along_z), "y")
+    own = lax.all_gather(pack(along_z), "y", axis=0, tiled=False)
     own, blocks[2] = lax.optimization_barrier((own, blocks[2]))
     other = swapped(own, "c")
     query, turned_value = absorb(blocks, key_up, value_up)

time: 110 us -> 112 us (1.018)
  blocking collectives: 15 us -> 27.6 us
  waiting for transfers between devices: 33 us -> 26 us
  starting transfers between devices: 45.5 us -> 42 us
    all_gather x0 -> x1, blocking collectives: none -> 13.4 us  [on_device(): own = lax.all_gather(pack(along_z), 'y', axis=0, tiled=False)]
    ppermute x3, waiting for transfers between devices: 9.61 us -> 4.25 us  [shifted(): return lax.ppermute(value, 'x', [(i, (i + by) % NX) for i in range(NX)])]
    all_to_all x3 -> x2, starting transfers between devices: 23.6 us -> 19 us  [exchanged(): return lax.all_to_all(value, axis, split_axis=0, concat_axis=0, tiled=True)]
    ppermute x3, waiting for transfers between devices: 10.8 us -> 9.2 us  [swapped(): return lax.ppermute(value, axis, [(0, 1), (1, 0)])]
    all_to_all x3 -> x2, waiting for transfers between devices: 12.6 us -> 12.6 us  [exchanged(): return lax.all_to_all(value, axis, split_axis=0, concat_axis=0, tiled=True)]
  transfers between devices with their start and end apart: 9 -> 8, of which waited for: 7 -> 6; matrix products, arithmetic and copies ran while one was open for 0% -> 0% of each run, Pallas kernels for 3% -> 3%
where the time goes in v9:
time: 112 us
  starting transfers between devices  42 us (38%)
  blocking collectives  27.6 us (25%)
  waiting for transfers between devices  26 us (23%)
  Pallas kernels  14.9 us (13%)
    all_to_all x2, starting transfers between devices, exchanged(): return lax.all_to_all(value, axis, split_axis=0, concat_axis=0, tiled=True)  19 us
    all_to_all x1, blocking collectives, exchanged(): return lax.all_to_all(value, axis, split_axis=0, concat_axis=0, tiled=True)  14.1 us
    all_gather x1, blocking collectives, on_device(): own = lax.all_gather(pack(along_z), 'y', axis=0, tiled=False)  13.4 us
    all_to_all x2, waiting for transfers between devices, exchanged(): return lax.all_to_all(value, axis, split_axis=0, concat_axis=0, tiled=True)  12.6 us
    ppermute x3, starting transfers between devices, swapped(): return lax.ppermute(value, axis, [(0, 1), (1, 0)])  12.5 us
    ppermute x3, starting transfers between devices, shifted(): return lax.ppermute(value, 'x', [(i, (i + by) % NX) for i in range(NX)])  10.4 us
    ppermute x3, waiting for transfers between devices, swapped(): return lax.ppermute(value, axis, [(0, 1), (1, 0)])  9.2 us
    pallas_call x1, Pallas kernels, attend(): pl.pallas_call(attend_kernel, out_shape=jax.ShapeDtypeStruct((NX, PARTROW...  7.49 us
  transfers between devices with their start and end apart: 8, of which 6 were waited for; matrix products, arithmetic and copies ran while one was open for 0% of the time, Pallas kernels for 3%

profile of v9, /device:TPU:32, one launch (start us, length us, event | category | flops | bytes accessed | tf_op | source)
XLA Modules:
  0.0 111.9 jit_solution(5630907974469771739)
XLA Ops:
  0.0 1.7 %shard_map.82.after_ref = bf16[16,8,640]{2,1,0:T(8,128)(2,1)} custom-call(s32[64]{0:T(128)} %spans_ref.3, bf16[8,576]{1,0:T(8,128)(2,1)} %keys_ref.1, f32[4,64,128]{2,1,0:T(8,128)} %constant.20.clone.tables_ref), custom_call_target="tpu_custom_call" | custom-call | tf_op jit(solution)/shard_map/pallas_call | solution.py:372
  1.7 15.2 %all-to-all-start = ((bf16[16,8,640]{2,1,0:T(8,128)(2,1)}), bf16[16,8,640]{2,1,0:T(8,128)(2,1)S(1)}, u32[]{:S(2)}, u32[]{:S(2)}) async-start(bf16[16,8,640]{2,1,0:T(8,128)(2,1)} %shard_map.82.after_ref), calls=%async_computation | async-start | bytes 327680 | tf_op jit(solution)/shard_map/all_to_all | solution.py:366
  16.9 1.8 %shard_map.83 = (bf16[128,768]{1,0:T(8,128)(2,1)}, s32[64]{0:T(128)}) custom-call(s32[64]{0:T(128)} %spans_ref.3, bf16[128,512]{1,0:T(8,128)(2,1)} %plain_ref.1, bf16[128,256]{1,0:T(8,128)(2,1)} %rotary_ref.1, f32[4,64,128]{2,1,0:T(8,128)} %constant.20.clone.tables_ref, bf16[16,8,640]{2,1,0:T(8,128)(2,1)} %shard_map.82.after_ref), custom_call_target="tpu_custom_call" | custom-call | tf_op jit(solution)/shard_map/pallas_call | solution.py:379
  18.8 3.4 %collective-permute-start = (bf16[128,768]{1,0:T(8,128)(2,1)}, bf16[128,768]{1,0:T(8,128)(2,1)S(1)}, u32[]{:S(2)}, u32[]{:S(2)}) collective-permute-start(bf16[128,768]{1,0:T(8,128)(2,1)} %get-tuple-element.17.q0_hbm), channel_id=1, source_target_pairs={{0,16},{16,32},{32,48},{48,0},{1,17},{17,33},{33,49},{49,1},{2,18}... | collective-permute-start | bytes 589832 | tf_op jit(solution)/shard_map/ppermute | solution.py:358
  22.2 3.7 %collective-permute-start.1 = (bf16[128,768]{1,0:T(8,128)(2,1)}, bf16[128,768]{1,0:T(8,128)(2,1)S(1)}, u32[]{:S(2)}, u32[]{:S(2)}) collective-permute-start(bf16[128,768]{1,0:T(8,128)(2,1)} %get-tuple-element.17.q0_hbm), channel_id=1, source_target_pairs={{0,48},{16,0},{32,16},{48,32},{1,49},{17,1},{33,17},{49,33},{2,50}... | collective-permute-start | bytes 589832 | tf_op jit(solution)/shard_map/ppermute | solution.py:358
  25.8 2.3 %collective-permute-done.q1 = bf16[128,768]{1,0:T(8,128)(2,1)S(1)} collective-permute-done((bf16[128,768]{1,0:T(8,128)(2,1)}, bf16[128,768]{1,0:T(8,128)(2,1)S(1)}, u32[]{:S(2)}, u32[]{:S(2)}) %collective-permute-start) | collective-permute-done | bytes 196640 | tf_op jit(solution)/shard_map/ppermute | solution.py:358
  28.2 1.9 %collective-permute-done.1.q3 = bf16[128,768]{1,0:T(8,128)(2,1)S(1)} collective-permute-done((bf16[128,768]{1,0:T(8,128)(2,1)}, bf16[128,768]{1,0:T(8,128)(2,1)S(1)}, u32[]{:S(2)}, u32[]{:S(2)}) %collective-permute-start.1) | collective-permute-done | bytes 196640 | tf_op jit(solution)/shard_map/ppermute | solution.py:358
  30.1 3.5 %all-to-all-done = bf16[16,8,640]{2,1,0:T(8,128)(2,1)S(1)} async-done(((bf16[16,8,640]{2,1,0:T(8,128)(2,1)}), bf16[16,8,640]{2,1,0:T(8,128)(2,1)S(1)}, u32[]{:S(2)}, u32[]{:S(2)}) %all-to-all-start) | async-done | bytes 163872 | tf_op jit(solution)/shard_map/all_to_all | solution.py:366
  33.6 3.4 %collective-permute-start.2 = (bf16[128,768]{1,0:T(8,128)(2,1)S(1)}, bf16[128,768]{1,0:T(8,128)(2,1)S(1)}, u32[]{:S(2)}, u32[]{:S(2)}) collective-permute-start(bf16[128,768]{1,0:T(8,128)(2,1)S(1)} %collective-permute-done.q1), channel_id=1, source_target_pairs={{0,16},{16,32},{32,48},{48,0},{1,17},{17,33},{33,49},{49,1},{2,18}... | collective-permute-start | bytes 589832 | tf_op jit(solution)/shard_map/ppermute | solution.py:358
  37.0 13.4 %all-gather = bf16[2304,128]{1,0:T(8,128)(2,1)S(1)} all-gather(bf16[576,128]{1,0:T(8,128)(2,1)S(1)} %shard_map.84), channel_id=2, replica_groups=mesh['zl'=8,'x'=4,'y'=4,'zh'=2,'c'=2] {'y'}, dimensions={0}, use_global_device_ids=true | all-gather | bytes 737280 | tf_op jit(solution)/shard_map/all_gather | solution.py:389
  50.5 2.2 %collective-permute-start.3 = (bf16[4,576,128]{2,1,0:T(8,128)(2,1)S(1)}, bf16[4,576,128]{2,1,0:T(8,128)(2,1)S(1)}, u32[]{:S(2)}, u32[]{:S(2)}) collective-permute-start(bf16[4,576,128]{2,1,0:T(8,128)(2,1)S(1)} %bitcast.4), channel_id=1, source_target_pairs={{0,1},{1,0},{2,3},{3,2},{4,5},{5,4},{6,7},{7,6},{8,9},{9,8},{10,11... | collective-permute-start | bytes 1769480 | tf_op jit(solution)/shard_map/ppermute | solution.py:362
  52.6 2.0 %shard_map.85 = (bf16[8,256,640]{2,1,0:T(8,128)(2,1)S(1)}, bf16[2,256,512]{2,1,0:T(8,128)(2,1)S(1)}) custom-call(bf16[128,768]{1,0:T(8,128)(2,1)} %get-tuple-element.17.q0_hbm, bf16[128,768]{1,0:T(8,128)(2,1)S(1)} %collective-permute-done.q1, bf16[128,768]{1,0:T(8,128)(2,1)S(1)} %collective-permute-done.2.q2, ...), custom_call_target="tpu_custom_call" | custom-call | tf_op jit(solution)/shard_map/pallas_call | solution.py:129
  54.7 0.6 copy-done.1
  55.3 7.5 %shard_map.86 = bf16[4,528,128]{2,1,0:T(8,128)(2,1)S(1)} custom-call(s32[64]{0:T(128)S(1)} %copy-done.1, bf16[8,256,640]{2,1,0:T(8,128)(2,1)S(1)} %get-tuple-element.22.query, bf16[4,576,128]{2,1,0:T(8,128)(2,1)S(1)} %bitcast.5, bf16[4,576,128]{2,1,0:T(8,128)(2,1)S(1)} %collective-permute-done.3.other_ref, bf16[2,256,512]{2,1,0:T(8,128)(2,1)S(1)} %get-tuple-element.24.value_ref), custom_call_target="tpu_custom_call" | custom-call | tf_op jit(solution)/shard_map/pallas_call | solution.py:266
  62.8 14.1 %all_to_all.15.parts_ref = bf16[4,528,128]{2,1,0:T(8,128)(2,1)S(1)} all-to-all(bf16[4,528,128]{2,1,0:T(8,128)(2,1)S(1)} %shard_map.86), channel_id=1, replica_groups=mesh['zl'=8,'x'=4,'y'=4,'zh'=2,'c'=2] {'x'}, dimensions={0} | all-to-all | bytes 1081344 | tf_op jit(solution)/shard_map/all_to_all | solution.py:366
  77.0 0.9 shard_map.87
  77.9 1.9 %collective-permute-start.4 = (bf16[4,2,224,128]{3,2,1,0:T(8,128)(2,1)S(1)}, bf16[4,2,224,128]{3,2,1,0:T(8,128)(2,1)S(1)}, u32[]{:S(2)}, u32[]{:S(2)}) collective-permute-start(bf16[4,2,224,128]{3,2,1,0:T(8,128)(2,1)S(1)} %get-tuple-element.26), channel_id=1, source_target_pairs={{0,1},{1,0},{2,3},{3,2},{4,5},{5,4},{6,7},{7,6},{8,9},{9,8},{10,11... | collective-permute-start | bytes 1376264 | tf_op jit(solution)/shard_map/ppermute | solution.py:362
  79.8 1.8 %collective-permute-done.4.second_ref = bf16[4,2,224,128]{3,2,1,0:T(8,128)(2,1)S(1)} collective-permute-done((bf16[4,2,224,128]{3,2,1,0:T(8,128)(2,1)S(1)}, bf16[4,2,224,128]{3,2,1,0:T(8,128)(2,1)S(1)}, u32[]{:S(2)}, u32[]{:S(2)}) %collective-permute-start.4) | collective-permute-done | bytes 458784 | tf_op jit(solution)/shard_map/ppermute | solution.py:362
  81.6 0.9 shard_map.88
  82.5 3.8 %all-to-all-start.2 = ((bf16[4,2,224,128]{3,2,1,0:T(8,128)(2,1)}), bf16[4,2,224,128]{3,2,1,0:T(8,128)(2,1)S(1)}, u32[]{:S(2)}, u32[]{:S(2)}) async-start(bf16[4,2,224,128]{3,2,1,0:T(8,128)(2,1)} %shard_map.88), calls=%async_computation.2 | async-start | bytes 917504 | tf_op jit(solution)/shard_map/all_to_all | solution.py:366
  86.2 9.1 %all-to-all-done.2 = bf16[4,2,224,128]{3,2,1,0:T(8,128)(2,1)S(1)} async-done(((bf16[4,2,224,128]{3,2,1,0:T(8,128)(2,1)}), bf16[4,2,224,128]{3,2,1,0:T(8,128)(2,1)S(1)}, u32[]{:S(2)}, u32[]{:S(2)}) %all-to-all-start.2) | async-done | bytes 458784 | tf_op jit(solution)/shard_map/all_to_all | solution.py:366
  95.4 8.5 %collective-permute-start.5 = (bf16[224,128]{1,0:T(8,128)(2,1)S(1)}, bf16[224,128]{1,0:T(8,128)(2,1)S(1)}, u32[]{:S(2)}, u32[]{:S(2)}) collective-permute-start(bf16[224,128]{1,0:T(8,128)(2,1)S(1)} %get-tuple-element.27), channel_id=1, source_target_pairs={{0,2},{2,0},{1,3},{3,1},{4,6},{6,4},{5,7},{7,5},{8,10},{10,8},{9,1... | collective-permute-start | bytes 172040 | tf_op jit(solution)/shard_map/ppermute | solution.py:362
  103.9 7.4 %collective-permute-done.5 = bf16[224,128]{1,0:T(8,128)(2,1)S(1)} collective-permute-done((bf16[224,128]{1,0:T(8,128)(2,1)S(1)}, bf16[224,128]{1,0:T(8,128)(2,1)S(1)}, u32[]{:S(2)}, u32[]{:S(2)}) %collective-permute-start.5) | collective-permute-done | bytes 57376 | tf_op jit(solution)/shard_map/ppermute | solution.py:362
  111.3 0.6 fusion
  (8 shorter events, 0.2 us)
Async XLA Ops:
  1.7 31.8 %all-to-all-start = ((bf16[16,8,640]{2,1,0:T(8,128)(2,1)}), bf16[16,8,640]{2,1,0:T(8,128)(2,1)S(1)}, u32[]{:S(2)}, u32[]{:S(2)}) async-start(bf16[16,8,640]{2,1,0:T(8,128)(2,1)} %shard_map.82.after_ref), calls=%async_computation | async-start | bytes 327680 | tf_op jit(solution)/shard_map/all_to_all | solution.py:366
  18.8 9.4 %collective-permute-start = (bf16[128,768]{1,0:T(8,128)(2,1)}, bf16[128,768]{1,0:T(8,128)(2,1)S(1)}, u32[]{:S(2)}, u32[]{:S(2)}) collective-permute-start(bf16[128,768]{1,0:T(8,128)(2,1)} %get-tuple-element.17.q0_hbm), channel_id=1, source_target_pairs={{0,16},{16,32},{32,48},{48,0},{1,17},{17,33},{33,49},{49,1},{2,18}... | collective-permute-start | bytes 589832 | tf_op jit(solution)/shard_map/ppermute | solution.py:358
  22.2 7.9 %collective-permute-start.1 = (bf16[128,768]{1,0:T(8,128)(2,1)}, bf16[128,768]{1,0:T(8,128)(2,1)S(1)}, u32[]{:S(2)}, u32[]{:S(2)}) collective-permute-start(bf16[128,768]{1,0:T(8,128)(2,1)} %get-tuple-element.17.q0_hbm), channel_id=1, source_target_pairs={{0,48},{16,0},{32,16},{48,32},{1,49},{17,1},{33,17},{49,33},{2,50}... | collective-permute-start | bytes 589832 | tf_op jit(solution)/shard_map/ppermute | solution.py:358
  33.6 16.9 %collective-permute-start.2 = (bf16[128,768]{1,0:T(8,128)(2,1)S(1)}, bf16[128,768]{1,0:T(8,128)(2,1)S(1)}, u32[]{:S(2)}, u32[]{:S(2)}) collective-permute-start(bf16[128,768]{1,0:T(8,128)(2,1)S(1)} %collective-permute-done.q1), channel_id=1, source_target_pairs={{0,16},{16,32},{32,48},{48,0},{1,17},{17,33},{33,49},{49,1},{2,18}... | collective-permute-start | bytes 589832 | tf_op jit(solution)/shard_map/ppermute | solution.py:358
  50.4 26.5 %copy-start = (bf16[512,3584]{1,0:T(8,128)(2,1)S(1)}, bf16[512,3584]{1,0:T(8,128)(2,1)}, u32[]{:S(2)}) copy-start(bf16[512,3584]{1,0:T(8,128)(2,1)} %weight_ref.1) | copy-start | bytes 11010052
  50.5 4.2 %collective-permute-start.3 = (bf16[4,576,128]{2,1,0:T(8,128)(2,1)S(1)}, bf16[4,576,128]{2,1,0:T(8,128)(2,1)S(1)}, u32[]{:S(2)}, u32[]{:S(2)}) collective-permute-start(bf16[4,576,128]{2,1,0:T(8,128)(2,1)S(1)} %bitcast.4), channel_id=1, source_target_pairs={{0,1},{1,0},{2,3},{3,2},{4,5},{5,4},{6,7},{7,6},{8,9},{9,8},{10,11... | collective-permute-start | bytes 1769480 | tf_op jit(solution)/shard_map/ppermute | solution.py:362
  54.7 0.7 copy-start.1
  77.9 3.7 %collective-permute-start.4 = (bf16[4,2,224,128]{3,2,1,0:T(8,128)(2,1)S(1)}, bf16[4,2,224,128]{3,2,1,0:T(8,128)(2,1)S(1)}, u32[]{:S(2)}, u32[]{:S(2)}) collective-permute-start(bf16[4,2,224,128]{3,2,1,0:T(8,128)(2,1)S(1)} %get-tuple-element.26), channel_id=1, source_target_pairs={{0,1},{1,0},{2,3},{3,2},{4,5},{5,4},{6,7},{7,6},{8,9},{9,8},{10,11... | collective-permute-start | bytes 1376264 | tf_op jit(solution)/shard_map/ppermute | solution.py:362
  82.5 12.8 %all-to-all-start.2 = ((bf16[4,2,224,128]{3,2,1,0:T(8,128)(2,1)}), bf16[4,2,224,128]{3,2,1,0:T(8,128)(2,1)S(1)}, u32[]{:S(2)}, u32[]{:S(2)}) async-start(bf16[4,2,224,128]{3,2,1,0:T(8,128)(2,1)} %shard_map.88), calls=%async_computation.2 | async-start | bytes 917504 | tf_op jit(solution)/shard_map/all_to_all | solution.py:366
  95.4 15.9 %collective-permute-start.5 = (bf16[224,128]{1,0:T(8,128)(2,1)S(1)}, bf16[224,128]{1,0:T(8,128)(2,1)S(1)}, u32[]{:S(2)}, u32[]{:S(2)}) collective-permute-start(bf16[224,128]{1,0:T(8,128)(2,1)S(1)} %get-tuple-element.27), channel_id=1, source_target_pairs={{0,2},{2,0},{1,3},{3,1},{4,6},{6,4},{5,7},{7,5},{8,10},{10,8},{9,1... | collective-permute-start | bytes 172040 | tf_op jit(solution)/shard_map/ppermute | solution.py:362
